TPU v7x, 32 devices: a whole 2x2x4 slice. The times are simulated.
32 devices in a mesh: rows: 8 (over z, y), feat: 4 (over x, core).
Axes of the slice: x: 2, y: 2, z: 4, core: 2. Of those that a mesh axis runs over, the one named last changes fastest.
Arguments:
- features: bfloat16 [16384, 1024], P('rows', 'feat'), may hold values from -6 to 6
- tiles: bfloat16 [5120, 128, 128], P('rows'), may hold values from -0.078125 to 0.078125
- tile_row: int32 [5120], P('rows'), may hold values from 0 to 15, as said below
- tile_panel: int32 [5120], P('rows'), may hold values from 0 to 7
- tile_slot: int32 [5120], P('rows'), may hold values from 0 to 7
- counts: int32 [8], P('rows'), may hold values from 1 to 640, as said below
- need_list: int32 [8, 8, 8], replicated, may hold values from 0 to 15, as said below
- weight: bfloat16 [1024, 1024], replicated, may hold values from -0.1875 to 0.1875
Outputs:
- activations: bfloat16 [16384, 1024], P(('rows', 'feat'))
Inputs may be any that keep to these rules, and one draw needn't show every extreme that they name: need_list[g, p] holds 8 distinct tile rows of panel p. Within a row group the slots name distinct (tile_row, tile_panel, tile_slot) triples. `counts`: some row group lists exactly 640 tiles.
All inputs are finite; a program needn't handle non-finite values.
Results may differ from a plain program's by a relative error of at most 0.0049.
Values may be sent and summed in bfloat16 or wider, within the bound.
No kernel may reach another device: no remote copies, remote signals or barrier semaphores. Data moves between devices by JAX's collectives and lax.ppermute only.
A program may use at most 128 MiB of HBM per device.

v0:
```python
import functools

import jax
import jax.numpy as jnp
from jax import lax
from jax.experimental import pallas as pl
from jax.experimental.pallas import tpu as pltpu
from jax.sharding import PartitionSpec as P


TILE = 128
TPP = 16
NEED = 8
PER_PANEL = TPP * NEED
ROWS = TPP * TILE
DEPTH = NEED * TILE
VMEM_LIMIT = 34 * 1024 * 1024
PIECES = 2


def densify_kernel(offsets, groups, table, tiles, out, dense, live, tile_sem, out_sem):
    buffers = dense.shape[0]
    entries = out.shape[0]

    def fetch(entry):
        buf = entry % buffers
        base = group_at(offsets[entry], groups) * PER_PANEL

        def row_step(row, found):
            for k in range(NEED):
                slot = table[base + row * NEED + k]
                rows = pl.ds(pl.multiple_of(row * TILE, TILE), TILE)
                cols = pl.ds(k * TILE, TILE)

                @pl.when(slot > 0)
                def _():
                    pltpu.make_async_copy(tiles.at[slot - 1], dense.at[buf, rows, cols], tile_sem.at[buf]).start()

                @pl.when(slot == 0)
                def _():
                    dense[buf, rows, cols] = jnp.zeros((TILE, TILE), jnp.bfloat16)

                found = found + jnp.where(slot > 0, 1, 0)
            return found

        live[buf] = lax.fori_loop(0, TPP, row_step, 0)

    def store(entry):
        buf = entry % buffers
        return pltpu.make_async_copy(dense.at[buf], out.at[entry], out_sem.at[buf])

    def arrive(entry):
        buf = entry % buffers

        def wait_one(i, c):
            pltpu.make_async_copy(tiles.at[0], dense.at[buf, pl.ds(0, TILE), pl.ds(0, TILE)], tile_sem.at[buf]).wait()
            return c

        lax.fori_loop(0, live[buf], wait_one, 0)
        store(entry).start()

    for entry in range(entries):
        if entry >= buffers:
            store(entry - buffers).wait()
        fetch(entry)
        if entry:
            arrive(entry - 1)
    arrive(entries - 1)
    for entry in range(max(0, entries - buffers), entries):
        store(entry).wait()


def densify(offsets, groups, table, tiles):
    smem = pl.BlockSpec(memory_space=pltpu.SMEM)
    hbm = pl.BlockSpec(memory_space=pl.ANY)
    buffers = 4
    entries = len(offsets)
    return pl.pallas_call(
        functools.partial(densify_kernel, offsets, groups),
        out_shape=jax.ShapeDtypeStruct((entries, ROWS, DEPTH), jnp.bfloat16),
        in_specs=[smem, hbm],
        out_specs=hbm,
        scratch_shapes=[
            pltpu.VMEM((buffers, ROWS, DEPTH), jnp.bfloat16),
            pltpu.SMEM((buffers,), jnp.int32),
            pltpu.SemaphoreType.DMA((buffers,)),
            pltpu.SemaphoreType.DMA((buffers,)),
        ],
        compiler_params=pltpu.CompilerParams(vmem_limit_bytes=44 * 1024 * 1024),
        cost_estimate=pl.CostEstimate(flops=0, bytes_accessed=4 * entries * ROWS * DEPTH, transcendentals=0),
        name="densify",
    )(table, tiles)


def aggregate_kernel(base, plan, offsets, groups, n_sources, first, blocks, need, dense_hbm, *refs):
    sources = refs[:n_sources]
    refs = refs[n_sources:]
    start_total = None if first else refs[0]
    refs = refs if first else refs[1:]
    if blocks:
        outs, total, (dense, feats, sem) = refs[:blocks], refs[blocks], refs[blocks + 1 :]
    else:
        total, dense, feats, sem = refs
    entries = len(plan)
    size = ROWS // PIECES

    def load(e, p):
        rows = pl.ds(p * size, size)
        return pltpu.make_async_copy(dense_hbm.at[base + e, rows, :], dense.at[e, rows, :], sem.at[e, p])

    for e in range(entries):
        for p in range(PIECES):
            load(e, p).start()
    for e, pieces in enumerate(plan):
        for source, column, width, whole in pieces:
            cols = pl.ds(column, width)
            if whole:
                for k in range(NEED):
                    rows = needed_rows(need, groups, 0, offsets[e], k)
                    feats[e, pl.ds(k * TILE, TILE), cols] = sources[source][rows, :]
            else:
                feats[e, :, cols] = sources[source][...]
    for e in range(entries):
        for p in range(PIECES):
            rows = pl.ds(p * size, size)
            load(e, p).wait()
            term = jnp.dot(dense[e, rows, :], feats[e], preferred_element_type=jnp.float32)
            if e:
                total[rows, :] += term
            elif first:
                total[rows, :] = term
            else:
                total[rows, :] = start_total[rows, :] + term
    if blocks:
        own = lax.axis_index("feat")
        size = ROWS // blocks
        for m in range(blocks):
            rows = pl.ds(pl.multiple_of((own ^ m) * size, size), size)
            outs[m][...] = total[rows, :].astype(jnp.bfloat16)


def aggregate(base, plan, offsets, groups, need, dense, sources, start_total, width, blocks=0):
    entries = len(plan)
    first = start_total is None
    smem = pl.BlockSpec(memory_space=pltpu.SMEM)
    vmem = pl.BlockSpec(memory_space=pltpu.VMEM)
    hbm = pl.BlockSpec(memory_space=pl.ANY)
    scratch = [
        pltpu.VMEM((entries, ROWS, DEPTH), jnp.bfloat16),
        pltpu.VMEM((entries, DEPTH, width), jnp.bfloat16),
        pltpu.SemaphoreType.DMA((entries, PIECES)),
    ]
    if blocks:
        out_shape = [jax.ShapeDtypeStruct((ROWS // blocks, width), jnp.bfloat16)] * blocks
        out_specs = [vmem] * blocks
        scratch = [pltpu.VMEM((ROWS, width), jnp.float32)] + scratch
    else:
        out_shape = jax.ShapeDtypeStruct((ROWS, width), jnp.float32)
        out_specs = vmem
    return pl.pallas_call(
        functools.partial(aggregate_kernel, base, plan, offsets, groups, len(sources), first, blocks),
        out_shape=out_shape,
        in_specs=[smem, hbm] + [vmem] * len(sources) + ([] if first else [vmem]),
        out_specs=out_specs,
        scratch_shapes=scratch,
        compiler_params=pltpu.CompilerParams(vmem_limit_bytes=VMEM_LIMIT),
        cost_estimate=pl.CostEstimate(
            flops=2 * entries * ROWS * DEPTH * width,
            bytes_accessed=entries * PER_PANEL * TILE * TILE * 2,
            transcendentals=0,
        ),
        name="aggregate",
    )(need, dense, *sources, *(() if first else (start_total,)))


def product_kernel(blocks, *refs):
    w, out = refs[blocks], refs[blocks + 1]
    width = refs[0].shape[1]
    own = lax.axis_index("feat")
    total = None
    for m in range(blocks):
        rows = pl.ds(pl.multiple_of((own ^ m) * width, width), width)
        term = jnp.dot(refs[m][...], w[rows, :], preferred_element_type=jnp.float32)
        total = term if total is None else total + term
    out[...] = jnp.maximum(total, 0.0).astype(out.dtype)


def product(parts, w):
    blocks = len(parts)
    rows, width = parts[0].shape
    depth, cols = w.shape
    step = 256
    return pl.pallas_call(
        functools.partial(product_kernel, blocks),
        grid=(cols // step,),
        out_shape=jax.ShapeDtypeStruct((rows, cols), jnp.bfloat16),
        in_specs=[pl.BlockSpec((rows, width), lambda j: (0, 0))] * blocks
        + [pl.BlockSpec((depth, step), lambda j: (0, j))],
        out_specs=pl.BlockSpec((rows, step), lambda j: (0, j)),
        compiler_params=pltpu.CompilerParams(vmem_limit_bytes=32 * 1024 * 1024),
        name="product",
    )(*parts, w)


def slot_table(groups, tile_row, tile_panel, tile_slot, counts):
    slots = lax.iota(jnp.int32, tile_row.shape[0])
    key = (tile_panel * TPP + tile_row) * NEED + tile_slot
    key = jnp.where(slots < counts[0], key, -1)
    places = lax.iota(jnp.int32, groups * PER_PANEL)
    return jnp.max(jnp.where(key[None, :] == places[:, None], slots[None, :] + 1, 0), axis=1)


def group_at(offset, groups):
    own = lax.axis_index("rows")
    place = jnp.where(lax.rem(own, 2) == 0, lax.div(own, 2), groups - 1 - lax.div(own, 2))
    place = lax.rem(place + offset + groups, groups)
    return jnp.where(place < groups // 2, 2 * place, 2 * (groups - 1 - place) + 1)


def needed_rows(need, groups, reader, offset, k):
    tile = need[(group_at(reader, groups) * groups + group_at(offset, groups)) * NEED + k]
    return pl.ds(pl.multiple_of(tile * TILE, TILE), TILE)


def pick_kernel(reader, offset, groups, need, source, out):
    for k in range(NEED):
        out[pl.ds(k * TILE, TILE), :] = source[needed_rows(need, groups, reader, offset, k), :]


def pick(need, source, reader, offset, groups):
    vmem = pl.BlockSpec(memory_space=pltpu.VMEM)
    return pl.pallas_call(
        functools.partial(pick_kernel, reader, offset, groups),
        out_shape=jax.ShapeDtypeStruct((DEPTH, source.shape[1]), source.dtype),
        in_specs=[pl.BlockSpec(memory_space=pltpu.SMEM), vmem],
        out_specs=vmem,
        compiler_params=pltpu.CompilerParams(vmem_limit_bytes=4 * 1024 * 1024),
        name="pick",
    )(need, source)


def ring_pairs(groups, way):
    order = [2 * p if p < groups // 2 else 2 * (groups - 1 - p) + 1 for p in range(groups)]
    return [(order[p], order[(p + way) % groups]) for p in range(groups)]


def per_device(features, tiles, tile_row, tile_panel, tile_slot, counts, need_list, weight):
    width = features.shape[1]
    groups = lax.axis_size("rows")
    blocks = lax.axis_size("feat")
    far = groups // 2

    def send(array, way):
        return lax.ppermute(array, "rows", ring_pairs(groups, way))

    table = slot_table(groups, tile_row, tile_panel, tile_slot, counts)
    need = need_list.reshape(-1)

    stages = [[0]] + [[-d, d] for d in range(1, far)] + [[far]]
    dense = densify([o for stage in stages for o in stage], groups, table, tiles)

    def add(total, d, pieces, final=0):
        plan, sources = [], []
        for entry in pieces:
            column, steps = 0, []
            for array, whole in entry:
                steps.append((len(sources), column, array.shape[1], whole))
                sources.append(array)
                column += array.shape[1]
            plan.append(tuple(steps))
        base = sum(len(stage) for stage in stages[:d])
        return aggregate(base, tuple(plan), stages[d], groups, need, dense, sources, total, width, final)

    cuts = 2 if width % (2 * TILE) == 0 else 1
    part = width // cuts
    long_way = [1, -1][:cuts]
    held = {way: [(features[:, c * part : (c + 1) * part], True) for c in range(cuts)] for way in (1, -1)}
    total = add(None, 0, [[(features, True)]])
    for d in range(1, far + 1):
        fresh = {}
        for c in range(cuts):
            for way in (1, -1):
                last = far if way == long_way[c] else far - 1
                if d > last:
                    continue
                array = held[way][c][0]
                if d == last:
                    array = pick(need, array, way, way - way * d, groups)
                fresh[way, c] = (send(array, way), d < last)
        if d == far:
            break
        for way in (1, -1):
            held[way] = [fresh[way, c] for c in range(cuts)]
        if d > 1:
            total = add(total, d - 1, [before[1], before[-1]])
        before = dict(held)
    total = add(total, far - 1, [before[1], before[-1]])
    parts = add(total, far, [[fresh[long_way[c], c] for c in range(cuts)]], blocks)
    arrived = [parts[0]]
    for m in range(1, blocks):
        arrived.append(lax.ppermute(parts[m], "feat", [(f, f ^ m) for f in range(blocks)]))
    return product(arrived, weight)


def solution(mesh):
    return jax.shard_map(
        per_device,
        mesh=mesh,
        in_specs=(
            P("rows", "feat"),
            P("rows", None, None),
            P("rows"),
            P("rows"),
            P("rows"),
            P("rows"),
            P(),
            P(),
        ),
        out_specs=P(("rows", "feat"), None),
        check_vma=False,
    )
```

profile of v0, /device:TPU:21, one launch (start us, length us, event | category | flops | bytes accessed | tf_op | source)
XLA Modules:
  0.0 119.9 jit_solution(16406694959411445197)
XLA Ops:
  0.0 1.3 %fusion = (bf16[2048,128]{1,0:T(8,128)(2,1)S(1)}, bf16[2048,128]{1,0:T(8,128)(2,1)S(1)}) fusion(bf16[2048,256]{1,0:T(8,128)(2,1)} %refs_0_.1), kind=kLoop, calls=%fused_computation.5 | loop fusion | bytes 2097152 | tf_op jit(solution)/shard_map/slice | solution.py:277
  1.3 0.2 collective-permute-start
  1.5 1.3 %collective-permute-start.4 = (bf16[2048,128]{1,0:T(8,128)(2,1)S(1)}, bf16[2048,128]{1,0:T(8,128)(2,1)S(1)}, u32[]{:S(2)}, u32[]{:S(2)}) collective-permute-start(bf16[2048,128]{1,0:T(8,128)(2,1)S(1)} %get-tuple-element.13), channel_id=1, source_target_pairs={{0,4},{8,0},{16,8},{24,16},{28,24},{20,28},{12,20},{4,12},{1,5},{9... | collective-permute-start | bytes 1572872 | tf_op jit(solution)/shard_map/ppermute | solution.py:254
  3.0 1.3 %collective-permute-start.11 = (bf16[2048,128]{1,0:T(8,128)(2,1)S(1)}, bf16[2048,128]{1,0:T(8,128)(2,1)}, u32[]{:S(2)}, u32[]{:S(2)}) collective-permute-start(bf16[2048,128]{1,0:T(8,128)(2,1)S(1)} %get-tuple-element.14), channel_id=1, source_target_pairs={{0,4},{8,0},{16,8},{24,16},{28,24},{20,28},{12,20},{4,12},{1,5},{9... | collective-permute-start | bytes 1572872 | tf_op jit(solution)/shard_map/ppermute | solution.py:254
  4.3 9.9 %collective-permute-done.refs_0_ = bf16[2048,128]{1,0:T(8,128)(2,1)S(1)} collective-permute-done((bf16[2048,128]{1,0:T(8,128)(2,1)S(1)}, bf16[2048,128]{1,0:T(8,128)(2,1)S(1)}, u32[]{:S(2)}, u32[]{:S(2)}) %collective-permute-start) | collective-permute-done | bytes 524320 | tf_op jit(solution)/shard_map/ppermute | solution.py:254
  14.3 1.3 %collective-permute-start.5 = (bf16[2048,128]{1,0:T(8,128)(2,1)S(1)}, bf16[2048,128]{1,0:T(8,128)(2,1)}, u32[]{:S(2)}, u32[]{:S(2)}) collective-permute-start(bf16[2048,128]{1,0:T(8,128)(2,1)S(1)} %collective-permute-done.4.refs_3_), channel_id=1, source_target_pairs={{0,4},{8,0},{16,8},{24,16},{28,24},{20,28},{12,20},{4,12},{1,5},{9... | collective-permute-start | bytes 1572872 | tf_op jit(solution)/shard_map/ppermute | solution.py:254
  15.6 0.8 copy-done.2
  16.4 9.1 %collective-permute-done.8.refs_1_ = bf16[2048,128]{1,0:T(8,128)(2,1)} collective-permute-done((bf16[2048,128]{1,0:T(8,128)(2,1)S(1)}, bf16[2048,128]{1,0:T(8,128)(2,1)}, u32[]{:S(2)}, u32[]{:S(2)}) %collective-permute-start.8) | collective-permute-done | bytes 524320 | tf_op jit(solution)/shard_map/ppermute | solution.py:254
  25.6 1.3 %collective-permute-start.12 = (bf16[2048,128]{1,0:T(8,128)(2,1)}, bf16[2048,128]{1,0:T(8,128)(2,1)S(1)}, u32[]{:S(2)}, u32[]{:S(2)}) collective-permute-start(bf16[2048,128]{1,0:T(8,128)(2,1)} %collective-permute-done.11.refs_2_), channel_id=1, source_target_pairs={{0,4},{8,0},{16,8},{24,16},{28,24},{20,28},{12,20},{4,12},{1,5},{9... | collective-permute-start | bytes 1572872 | tf_op jit(solution)/shard_map/ppermute | solution.py:254
  27.6 9.1 %collective-permute-done.1.refs_0_ = bf16[2048,128]{1,0:T(8,128)(2,1)S(1)} collective-permute-done((bf16[2048,128]{1,0:T(8,128)(2,1)S(1)}, bf16[2048,128]{1,0:T(8,128)(2,1)S(1)}, u32[]{:S(2)}, u32[]{:S(2)}) %collective-permute-start.1) | collective-permute-done | bytes 524320 | tf_op jit(solution)/shard_map/ppermute | solution.py:254
  36.9 1.3 %collective-permute-start.6 = (bf16[2048,128]{1,0:T(8,128)(2,1)}, bf16[2048,128]{1,0:T(8,128)(2,1)S(1)}, u32[]{:S(2)}, u32[]{:S(2)}) collective-permute-start(bf16[2048,128]{1,0:T(8,128)(2,1)} %collective-permute-done.5.refs_3_), channel_id=1, source_target_pairs={{0,4},{8,0},{16,8},{24,16},{28,24},{20,28},{12,20},{4,12},{1,5},{9... | collective-permute-start | bytes 1572872 | tf_op jit(solution)/shard_map/ppermute | solution.py:254
  38.2 0.7 iota_add_fusion
  38.9 0.8 reshape.9.need
  39.8 0.4 select_reduce_fusion.table
  40.2 21.1 %densify.1.dense_hbm = bf16[8,2048,1024]{2,1,0:T(8,128)(2,1)} custom-call(s32[1024]{0:T(1024)S(1)} %select_reduce_fusion.table, bf16[640,128,128]{2,1,0:T(8,128)(2,1)} %tiles.1), custom_call_target="tpu_custom_call" | custom-call | bytes 67108864 | tf_op jit(solution)/shard_map/densify/pallas_call | solution.py:78
  61.3 4.6 %aggregate.5.refs_4_ = f32[2048,256]{1,0:T(8,128)S(1)} custom-call(s32[512]{0:T(512)S(1)} %reshape.9.need, bf16[8,2048,1024]{2,1,0:T(8,128)(2,1)} %densify.1.dense_hbm, bf16[2048,256]{1,0:T(8,128)(2,1)S(1)} %copy-done), custom_call_target="tpu_custom_call" | custom-call | flops 1073741824 | bytes 4194304 | tf_op jit(solution)/shard_map/aggregate/pallas_call | solution.py:160
  65.9 0.6 pick.6
  66.6 0.6 pick.7
  67.3 1.5 %collective-permute-start.13 = (bf16[1024,128]{1,0:T(8,128)(2,1)S(1)}, bf16[1024,128]{1,0:T(8,128)(2,1)S(1)}, u32[]{:S(2)}, u32[]{:S(2)}) collective-permute-start(bf16[1024,128]{1,0:T(8,128)(2,1)S(1)} %pick.7), channel_id=1, source_target_pairs={{0,4},{8,0},{16,8},{24,16},{28,24},{20,28},{12,20},{4,12},{1,5},{9... | collective-permute-start | bytes 786440 | tf_op jit(solution)/shard_map/ppermute | solution.py:254
  68.8 7.7 %aggregate.6.refs_4_ = f32[2048,256]{1,0:T(8,128)S(1)} custom-call(s32[512]{0:T(512)S(1)} %reshape.9.need, bf16[8,2048,1024]{2,1,0:T(8,128)(2,1)} %densify.1.dense_hbm, bf16[2048,128]{1,0:T(8,128)(2,1)S(1)} %collective-permute-done.refs_0_, bf16[2048,128]{1,0:T(8,128)(2,1)} %collective-permute-done.8.refs_1_, ...), custom_call_target="tpu_custom_call" | custom-call | flops 2147483648 | bytes 8388608 | tf_op jit(solution)/shard_map/aggregate/pallas_call | solution.py:160
  76.4 0.6 pick.4
  77.1 0.6 pick.5
  77.7 1.7 %collective-permute-start.7 = (bf16[1024,128]{1,0:T(8,128)(2,1)S(1)}, bf16[1024,128]{1,0:T(8,128)(2,1)S(1)}, u32[]{:S(2)}, u32[]{:S(2)}) collective-permute-start(bf16[1024,128]{1,0:T(8,128)(2,1)S(1)} %pick.5), channel_id=1, source_target_pairs={{0,4},{8,0},{16,8},{24,16},{28,24},{20,28},{12,20},{4,12},{1,5},{9... | collective-permute-start | bytes 786440 | tf_op jit(solution)/shard_map/ppermute | solution.py:254
  79.4 7.5 %aggregate.7.refs_4_ = f32[2048,256]{1,0:T(8,128)S(1)} custom-call(s32[512]{0:T(512)S(1)} %reshape.9.need, bf16[8,2048,1024]{2,1,0:T(8,128)(2,1)} %densify.1.dense_hbm, bf16[2048,128]{1,0:T(8,128)(2,1)S(1)} %collective-permute-done.1.refs_0_, bf16[2048,128]{1,0:T(8,128)(2,1)S(1)} %collective-permute-done.9.source.refs_1_, ...), custom_call_target="tpu_custom_call" | custom-call | flops 2147483648 | bytes 8388608 | tf_op jit(solution)/shard_map/aggregate/pallas_call | solution.py:160
  86.9 7.0 %aggregate.8.refs_2_ = f32[2048,256]{1,0:T(8,128)S(1)} custom-call(s32[512]{0:T(512)S(1)} %reshape.9.need, bf16[8,2048,1024]{2,1,0:T(8,128)(2,1)} %densify.1.dense_hbm, bf16[2048,128]{1,0:T(8,128)(2,1)S(1)} %collective-permute-done.2.source.refs_0_, bf16[1024,128]{1,0:T(8,128)(2,1)S(1)} %collective-permute-done.10.refs_1_, ...), custom_call_target="tpu_custom_call" | custom-call | flops 2147483648 | bytes 8388608 | tf_op jit(solution)/shard_map/aggregate/pallas_call | solution.py:160
  94.0 4.8 %aggregate.9 = (bf16[512,256]{1,0:T(8,128)(2,1)S(1)}, bf16[512,256]{1,0:T(8,128)(2,1)S(1)}, bf16[512,256]{1,0:T(8,128)(2,1)S(1)}, bf16[512,256]{1,0:T(8,128)(2,1)S(1)}) custom-call(s32[512]{0:T(512)S(1)} %reshape.9.need, bf16[8,2048,1024]{2,1,0:T(8,128)(2,1)} %densify.1.dense_hbm, bf16[1024,128]{1,0:T(8,128)(2,1)S(1)} %collective-permute-done.3.refs_0_, ...), custom_call_target="tpu_custom_call" | custom-call | flops 1073741824 | bytes 4194304 | tf_op jit(solution)/shard_map/aggregate/pallas_call | solution.py:160
  98.8 4.4 %collective-permute-start.14 = (bf16[512,256]{1,0:T(8,128)(2,1)S(1)}, bf16[512,256]{1,0:T(8,128)(2,1)S(1)}, u32[]{:S(2)}, u32[]{:S(2)}) collective-permute-start(bf16[512,256]{1,0:T(8,128)(2,1)S(1)} %get-tuple-element.10), channel_id=1, source_target_pairs={{0,1},{1,0},{2,3},{3,2},{4,5},{5,4},{6,7},{7,6},{8,9},{9,8},{10,11... | collective-permute-start | bytes 786440 | tf_op jit(solution)/shard_map/ppermute | solution.py:301
  103.2 1.2 %collective-permute-start.15 = (bf16[512,256]{1,0:T(8,128)(2,1)S(1)}, bf16[512,256]{1,0:T(8,128)(2,1)S(1)}, u32[]{:S(2)}, u32[]{:S(2)}) collective-permute-start(bf16[512,256]{1,0:T(8,128)(2,1)S(1)} %get-tuple-element.11), channel_id=1, source_target_pairs={{0,2},{1,3},{2,0},{3,1},{4,6},{5,7},{6,4},{7,5},{8,10},{9,11},{10,... | collective-permute-start | bytes 786440 | tf_op jit(solution)/shard_map/ppermute | solution.py:301
  104.5 0.5 collective-permute-start.16
  105.0 6.1 %collective-permute-done.15.refs_2_ = bf16[512,256]{1,0:T(8,128)(2,1)S(1)} collective-permute-done((bf16[512,256]{1,0:T(8,128)(2,1)S(1)}, bf16[512,256]{1,0:T(8,128)(2,1)S(1)}, u32[]{:S(2)}, u32[]{:S(2)}) %collective-permute-start.15) | collective-permute-done | bytes 262176 | tf_op jit(solution)/shard_map/ppermute | solution.py:301
  111.0 5.9 %collective-permute-done.16.refs_3_ = bf16[512,256]{1,0:T(8,128)(2,1)S(1)} collective-permute-done((bf16[512,256]{1,0:T(8,128)(2,1)S(1)}, bf16[512,256]{1,0:T(8,128)(2,1)S(1)}, u32[]{:S(2)}, u32[]{:S(2)}) %collective-permute-start.16) | collective-permute-done | bytes 262176 | tf_op jit(solution)/shard_map/ppermute | solution.py:301
  116.9 3.0 %product.1 = bf16[512,1024]{1,0:T(8,128)(2,1)} custom-call(bf16[512,256]{1,0:T(8,128)(2,1)S(1)} %get-tuple-element.9.refs_0_, bf16[512,256]{1,0:T(8,128)(2,1)S(1)} %collective-permute-done.14.refs_1_, bf16[512,256]{1,0:T(8,128)(2,1)S(1)} %collective-permute-done.15.refs_2_, bf16[512,256]{1,0:T(8,128)(2,1)S(1)} %collective-permute-done.16.refs_3_, ...), custom_call_target="tpu_custom_call" | custom-call | tf_op jit(solution)/shard_map/product/pallas_call | solution.py:193
  (25 shorter events, 0.9 us)
Async XLA Ops:
  1.3 12.9 %collective-permute-start = (bf16[2048,128]{1,0:T(8,128)(2,1)S(1)}, bf16[2048,128]{1,0:T(8,128)(2,1)S(1)}, u32[]{:S(2)}, u32[]{:S(2)}) collective-permute-start(bf16[2048,128]{1,0:T(8,128)(2,1)S(1)} %get-tuple-element.14), channel_id=1, source_target_pairs={{0,8},{8,16},{16,24},{24,28},{28,20},{20,12},{12,4},{4,0},{1,9},{9... | collective-permute-start | bytes 1572872 | tf_op jit(solution)/shard_map/ppermute | solution.py:254
  1.5 12.8 %collective-permute-start.4 = (bf16[2048,128]{1,0:T(8,128)(2,1)S(1)}, bf16[2048,128]{1,0:T(8,128)(2,1)S(1)}, u32[]{:S(2)}, u32[]{:S(2)}) collective-permute-start(bf16[2048,128]{1,0:T(8,128)(2,1)S(1)} %get-tuple-element.13), channel_id=1, source_target_pairs={{0,4},{8,0},{16,8},{24,16},{28,24},{20,28},{12,20},{4,12},{1,5},{9... | collective-permute-start | bytes 1572872 | tf_op jit(solution)/shard_map/ppermute | solution.py:254
  2.8 22.7 %collective-permute-start.8 = (bf16[2048,128]{1,0:T(8,128)(2,1)S(1)}, bf16[2048,128]{1,0:T(8,128)(2,1)}, u32[]{:S(2)}, u32[]{:S(2)}) collective-permute-start(bf16[2048,128]{1,0:T(8,128)(2,1)S(1)} %get-tuple-element.13), channel_id=1, source_target_pairs={{0,8},{8,16},{16,24},{24,28},{28,20},{20,12},{12,4},{4,0},{1,9},{9... | collective-permute-start | bytes 1572872 | tf_op jit(solution)/shard_map/ppermute | solution.py:254
  3.0 22.7 %collective-permute-start.11 = (bf16[2048,128]{1,0:T(8,128)(2,1)S(1)}, bf16[2048,128]{1,0:T(8,128)(2,1)}, u32[]{:S(2)}, u32[]{:S(2)}) collective-permute-start(bf16[2048,128]{1,0:T(8,128)(2,1)S(1)} %get-tuple-element.14), channel_id=1, source_target_pairs={{0,4},{8,0},{16,8},{24,16},{28,24},{20,28},{12,20},{4,12},{1,5},{9... | collective-permute-start | bytes 1572872 | tf_op jit(solution)/shard_map/ppermute | solution.py:254
  14.1 22.6 %collective-permute-start.1 = (bf16[2048,128]{1,0:T(8,128)(2,1)S(1)}, bf16[2048,128]{1,0:T(8,128)(2,1)S(1)}, u32[]{:S(2)}, u32[]{:S(2)}) collective-permute-start(bf16[2048,128]{1,0:T(8,128)(2,1)S(1)} %collective-permute-done.refs_0_), channel_id=1, source_target_pairs={{0,8},{8,16},{16,24},{24,28},{28,20},{20,12},{12,4},{4,0},{1,9},{9... | collective-permute-start | bytes 1572872 | tf_op jit(solution)/shard_map/ppermute | solution.py:254
  14.3 22.6 %collective-permute-start.5 = (bf16[2048,128]{1,0:T(8,128)(2,1)S(1)}, bf16[2048,128]{1,0:T(8,128)(2,1)}, u32[]{:S(2)}, u32[]{:S(2)}) collective-permute-start(bf16[2048,128]{1,0:T(8,128)(2,1)S(1)} %collective-permute-done.4.refs_3_), channel_id=1, source_target_pairs={{0,4},{8,0},{16,8},{24,16},{28,24},{20,28},{12,20},{4,12},{1,5},{9... | collective-permute-start | bytes 1572872 | tf_op jit(solution)/shard_map/ppermute | solution.py:254
  15.6 0.8 copy-start.2
  25.5 40.5 %collective-permute-start.9 = (bf16[2048,128]{1,0:T(8,128)(2,1)}, bf16[2048,128]{1,0:T(8,128)(2,1)S(1)}, u32[]{:S(2)}, u32[]{:S(2)}) collective-permute-start(bf16[2048,128]{1,0:T(8,128)(2,1)} %collective-permute-done.8.refs_1_), channel_id=1, source_target_pairs={{0,8},{8,16},{16,24},{24,28},{28,20},{20,12},{12,4},{4,0},{1,9},{9... | collective-permute-start | bytes 1572872 | tf_op jit(solution)/shard_map/ppermute | solution.py:254
  25.6 41.0 %collective-permute-start.12 = (bf16[2048,128]{1,0:T(8,128)(2,1)}, bf16[2048,128]{1,0:T(8,128)(2,1)S(1)}, u32[]{:S(2)}, u32[]{:S(2)}) collective-permute-start(bf16[2048,128]{1,0:T(8,128)(2,1)} %collective-permute-done.11.refs_2_), channel_id=1, source_target_pairs={{0,4},{8,0},{16,8},{24,16},{28,24},{20,28},{12,20},{4,12},{1,5},{9... | collective-permute-start | bytes 1572872 | tf_op jit(solution)/shard_map/ppermute | solution.py:254
  36.7 39.7 %collective-permute-start.2 = (bf16[2048,128]{1,0:T(8,128)(2,1)S(1)}, bf16[2048,128]{1,0:T(8,128)(2,1)S(1)}, u32[]{:S(2)}, u32[]{:S(2)}) collective-permute-start(bf16[2048,128]{1,0:T(8,128)(2,1)S(1)} %collective-permute-done.1.refs_0_), channel_id=1, source_target_pairs={{0,8},{8,16},{16,24},{24,28},{28,20},{20,12},{12,4},{4,0},{1,9},{9... | collective-permute-start | bytes 1572872 | tf_op jit(solution)/shard_map/ppermute | solution.py:254
  36.9 40.2 %collective-permute-start.6 = (bf16[2048,128]{1,0:T(8,128)(2,1)}, bf16[2048,128]{1,0:T(8,128)(2,1)S(1)}, u32[]{:S(2)}, u32[]{:S(2)}) collective-permute-start(bf16[2048,128]{1,0:T(8,128)(2,1)} %collective-permute-done.5.refs_3_), channel_id=1, source_target_pairs={{0,4},{8,0},{16,8},{24,16},{28,24},{20,28},{12,20},{4,12},{1,5},{9... | collective-permute-start | bytes 1572872 | tf_op jit(solution)/shard_map/ppermute | solution.py:254
  40.2 21.1 %copy-start = (bf16[2048,256]{1,0:T(8,128)(2,1)S(1)}, bf16[2048,256]{1,0:T(8,128)(2,1)}, u32[]{:S(2)}) copy-start(bf16[2048,256]{1,0:T(8,128)(2,1)} %refs_0_.1) | copy-start | bytes 3145732
  61.3 7.5 %copy-start.3 = (bf16[2048,128]{1,0:T(8,128)(2,1)S(1)}, bf16[2048,128]{1,0:T(8,128)(2,1)}, u32[]{:S(2)}) copy-start(bf16[2048,128]{1,0:T(8,128)(2,1)} %copy-done.2) | copy-start | bytes 1572868
  66.6 20.4 %collective-permute-start.10 = (bf16[1024,128]{1,0:T(8,128)(2,1)S(1)}, bf16[1024,128]{1,0:T(8,128)(2,1)S(1)}, u32[]{:S(2)}, u32[]{:S(2)}) collective-permute-start(bf16[1024,128]{1,0:T(8,128)(2,1)S(1)} %pick.6), channel_id=1, source_target_pairs={{0,8},{8,16},{16,24},{24,28},{28,20},{20,12},{12,4},{4,0},{1,9},{9... | collective-permute-start | bytes 786440 | tf_op jit(solution)/shard_map/ppermute | solution.py:254
  67.3 19.7 %collective-permute-start.13 = (bf16[1024,128]{1,0:T(8,128)(2,1)S(1)}, bf16[1024,128]{1,0:T(8,128)(2,1)S(1)}, u32[]{:S(2)}, u32[]{:S(2)}) collective-permute-start(bf16[1024,128]{1,0:T(8,128)(2,1)S(1)} %pick.7), channel_id=1, source_target_pairs={{0,4},{8,0},{16,8},{24,16},{28,24},{20,28},{12,20},{4,12},{1,5},{9... | collective-permute-start | bytes 786440 | tf_op jit(solution)/shard_map/ppermute | solution.py:254
  77.0 16.9 %collective-permute-start.3 = (bf16[1024,128]{1,0:T(8,128)(2,1)S(1)}, bf16[1024,128]{1,0:T(8,128)(2,1)S(1)}, u32[]{:S(2)}, u32[]{:S(2)}) collective-permute-start(bf16[1024,128]{1,0:T(8,128)(2,1)S(1)} %pick.4), channel_id=1, source_target_pairs={{0,8},{8,16},{16,24},{24,28},{28,20},{20,12},{12,4},{4,0},{1,9},{9... | collective-permute-start | bytes 786440 | tf_op jit(solution)/shard_map/ppermute | solution.py:254
  77.7 16.2 %collective-permute-start.7 = (bf16[1024,128]{1,0:T(8,128)(2,1)S(1)}, bf16[1024,128]{1,0:T(8,128)(2,1)S(1)}, u32[]{:S(2)}, u32[]{:S(2)}) collective-permute-start(bf16[1024,128]{1,0:T(8,128)(2,1)S(1)} %pick.5), channel_id=1, source_target_pairs={{0,4},{8,0},{16,8},{24,16},{28,24},{20,28},{12,20},{4,12},{1,5},{9... | collective-permute-start | bytes 786440 | tf_op jit(solution)/shard_map/ppermute | solution.py:254
  94.0 22.9 %copy-start.1 = (bf16[1024,1024]{1,0:T(8,128)(2,1)S(1)}, bf16[1024,1024]{1,0:T(8,128)(2,1)}, u32[]{:S(2)}) copy-start(bf16[1024,1024]{1,0:T(8,128)(2,1)} %refs_4_.1) | copy-start | bytes 6291460
  98.8 6.1 %collective-permute-start.14 = (bf16[512,256]{1,0:T(8,128)(2,1)S(1)}, bf16[512,256]{1,0:T(8,128)(2,1)S(1)}, u32[]{:S(2)}, u32[]{:S(2)}) collective-permute-start(bf16[512,256]{1,0:T(8,128)(2,1)S(1)} %get-tuple-element.10), channel_id=1, source_target_pairs={{0,1},{1,0},{2,3},{3,2},{4,5},{5,4},{6,7},{7,6},{8,9},{9,8},{10,11... | collective-permute-start | bytes 786440 | tf_op jit(solution)/shard_map/ppermute | solution.py:301
  103.2 7.8 %collective-permute-start.15 = (bf16[512,256]{1,0:T(8,128)(2,1)S(1)}, bf16[512,256]{1,0:T(8,128)(2,1)S(1)}, u32[]{:S(2)}, u32[]{:S(2)}) collective-permute-start(bf16[512,256]{1,0:T(8,128)(2,1)S(1)} %get-tuple-element.11), channel_id=1, source_target_pairs={{0,2},{1,3},{2,0},{3,1},{4,6},{5,7},{6,4},{7,5},{8,10},{9,11},{10,... | collective-permute-start | bytes 786440 | tf_op jit(solution)/shard_map/ppermute | solution.py:301
  104.5 12.4 %collective-permute-start.16 = (bf16[512,256]{1,0:T(8,128)(2,1)S(1)}, bf16[512,256]{1,0:T(8,128)(2,1)S(1)}, u32[]{:S(2)}, u32[]{:S(2)}) collective-permute-start(bf16[512,256]{1,0:T(8,128)(2,1)S(1)} %get-tuple-element.12), channel_id=1, source_target_pairs={{0,3},{1,2},{2,1},{3,0},{4,7},{5,6},{6,5},{7,4},{8,11},{9,10},{10,... | collective-permute-start | bytes 786440 | tf_op jit(solution)/shard_map/ppermute | solution.py:301
where the time goes:
time: 121 us; the launch traced here: 120 us
  Pallas kernels  58.1 us (48%)
  waiting for transfers between devices  40 us (33%)
  starting transfers between devices  16.8 us (14%)
  local copies, waits for them, and re-layouts  2.92 us (2%)
    pallas_call x5, Pallas kernels, aggregate(): pl.pallas_call(functools.partial(aggregate_kernel, base, plan, offsets, g...  31.6 us
    ppermute x14, waiting for transfers between devices, send(): return lax.ppermute(array, 'rows', ring_pairs(groups, way))  28.1 us
    pallas_call x1, Pallas kernels, densify(): pl.pallas_call(functools.partial(densify_kernel, offsets, groups), out_sh...  21.1 us
    ppermute x3, waiting for transfers between devices, per_device(): lax.ppermute(parts[m], 'feat', [(f, f ^ m) for f in range(blocks)])  11.9 us
    ppermute x14, starting transfers between devices, send(): return lax.ppermute(array, 'rows', ring_pairs(groups, way))  10.7 us
    ppermute x3, starting transfers between devices, per_device(): lax.ppermute(parts[m], 'feat', [(f, f ^ m) for f in range(blocks)])  6.11 us
    pallas_call x1, Pallas kernels, product(): pl.pallas_call(functools.partial(product_kernel, blocks), grid=(cols // s...  2.99 us
    pallas_call x4, Pallas kernels, pick(): pl.pallas_call(functools.partial(pick_kernel, reader, offset, groups), ou...  2.45 us
  transfers between devices with their start and end apart: 17, of which 5 were waited for; matrix products, arithmetic and copies ran while one was open for 2% of the time, Pallas kernels for 42%

commit v1 on v0

--- a/solution.py
+++ b/solution.py
@@ -14,103 +14,112 @@
 PER_PANEL = TPP * NEED
 ROWS = TPP * TILE
 DEPTH = NEED * TILE
-VMEM_LIMIT = 34 * 1024 * 1024
+MIB = 1024 * 1024
+RESIDENT_PANELS = 8
+RESIDENT_LIMIT = 9 * MIB
+STREAM_LIMIT = 14 * MIB
+DENSIFY_LIMIT = 38 * MIB
 PIECES = 2
 
 
-def densify_kernel(offsets, groups, table, tiles, out, dense, live, tile_sem, out_sem):
+def place_tiles(panel, table, tiles, dense, sem):
+    base = panel * PER_PANEL
+
+    def row_step(row, found):
+        for k in range(NEED):
+            slot = table[base + row * NEED + k]
+            rows = pl.ds(pl.multiple_of(row * TILE, TILE), TILE)
+            cols = pl.ds(k * TILE, TILE)
+
+            @pl.when(slot > 0)
+            def _():
+                pltpu.make_async_copy(tiles.at[slot - 1], dense.at[rows, cols], sem).start()
+
+            @pl.when(slot == 0)
+            def _():
+                dense[rows, cols] = jnp.zeros((TILE, TILE), jnp.bfloat16)
+
+            found = found + jnp.where(slot > 0, 1, 0)
+        return found
+
+    return lax.fori_loop(0, TPP, row_step, 0)
+
+
+def await_tiles(found, tiles, dense, sem):
+    def wait_one(i, c):
+        pltpu.make_async_copy(tiles.at[0], dense.at[pl.ds(0, TILE), pl.ds(0, TILE)], sem).wait()
+        return c
+
+    lax.fori_loop(0, found, wait_one, 0)
+
+
+def densify_kernel(stages, resident, groups, table, tiles, *refs):
+    outs, (dense, tile_sem, out_sem) = refs[: len(stages)], refs[len(stages) :]
+    entries = [(out, e, o) for out, stage in zip(outs, stages) for e, o in enumerate(stage)]
+    if resident:
+        found = [
+            place_tiles(group_at(o, groups), table, tiles, out.at[e], tile_sem.at[0]) for out, e, o in entries
+        ]
+        out, e, o = entries[0]
+        await_tiles(sum(found), tiles, out.at[e], tile_sem.at[0])
+        return
     buffers = dense.shape[0]
-    entries = out.shape[0]
-
-    def fetch(entry):
-        buf = entry % buffers
-        base = group_at(offsets[entry], groups) * PER_PANEL
-
-        def row_step(row, found):
-            for k in range(NEED):
-                slot = table[base + row * NEED + k]
-                rows = pl.ds(pl.multiple_of(row * TILE, TILE), TILE)
-                cols = pl.ds(k * TILE, TILE)
-
-                @pl.when(slot > 0)
-                def _():
-                    pltpu.make_async_copy(tiles.at[slot - 1], dense.at[buf, rows, cols], tile_sem.at[buf]).start()
-
-                @pl.when(slot == 0)
-                def _():
-                    dense[buf, rows, cols] = jnp.zeros((TILE, TILE), jnp.bfloat16)
-
-                found = found + jnp.where(slot > 0, 1, 0)
-            return found
-
-        live[buf] = lax.fori_loop(0, TPP, row_step, 0)
-
-    def store(entry):
-        buf = entry % buffers
-        return pltpu.make_async_copy(dense.at[buf], out.at[entry], out_sem.at[buf])
-
-    def arrive(entry):
-        buf = entry % buffers
-
-        def wait_one(i, c):
-            pltpu.make_async_copy(tiles.at[0], dense.at[buf, pl.ds(0, TILE), pl.ds(0, TILE)], tile_sem.at[buf]).wait()
-            return c
-
-        lax.fori_loop(0, live[buf], wait_one, 0)
-        store(entry).start()
-
-    for entry in range(entries):
-        if entry >= buffers:
-            store(entry - buffers).wait()
-        fetch(entry)
-        if entry:
-            arrive(entry - 1)
-    arrive(entries - 1)
-    for entry in range(max(0, entries - buffers), entries):
-        store(entry).wait()
-
-
-def densify(offsets, groups, table, tiles):
-    smem = pl.BlockSpec(memory_space=pltpu.SMEM)
-    hbm = pl.BlockSpec(memory_space=pl.ANY)
-    buffers = 4
-    entries = len(offsets)
+
+    def store(i):
+        out, e, _ = entries[i]
+        return pltpu.make_async_copy(dense.at[i % buffers], out.at[e], out_sem.at[i % buffers])
+
+    for i, (out, e, o) in enumerate(entries):
+        buf = i % buffers
+        if i >= buffers:
+            store(i - buffers).wait()
+        found = place_tiles(group_at(o, groups), table, tiles, dense.at[buf], tile_sem.at[buf])
+        await_tiles(found, tiles, dense.at[buf], tile_sem.at[buf])
+        store(i).start()
+    for i in range(max(0, len(entries) - buffers), len(entries)):
+        store(i).wait()
+
+
+def densify(stages, resident, groups, table, tiles):
+    buffers = 1 if resident else 2
+    out_space = pltpu.VMEM if resident else pl.ANY
+    entries = sum(len(stage) for stage in stages)
     return pl.pallas_call(
-        functools.partial(densify_kernel, offsets, groups),
-        out_shape=jax.ShapeDtypeStruct((entries, ROWS, DEPTH), jnp.bfloat16),
-        in_specs=[smem, hbm],
-        out_specs=hbm,
+        functools.partial(densify_kernel, stages, resident, groups),
+        out_shape=[jax.ShapeDtypeStruct((len(stage), ROWS, DEPTH), jnp.bfloat16) for stage in stages],
+        in_specs=[pl.BlockSpec(memory_space=pltpu.SMEM), pl.BlockSpec(memory_space=pl.ANY)],
+        out_specs=[pl.BlockSpec(memory_space=out_space)] * len(stages),
         scratch_shapes=[
-            pltpu.VMEM((buffers, ROWS, DEPTH), jnp.bfloat16),
-            pltpu.SMEM((buffers,), jnp.int32),
+            pltpu.VMEM((8, TILE) if resident else (buffers, ROWS, DEPTH), jnp.bfloat16),
             pltpu.SemaphoreType.DMA((buffers,)),
             pltpu.SemaphoreType.DMA((buffers,)),
         ],
-        compiler_params=pltpu.CompilerParams(vmem_limit_bytes=44 * 1024 * 1024),
-        cost_estimate=pl.CostEstimate(flops=0, bytes_accessed=4 * entries * ROWS * DEPTH, transcendentals=0),
+        compiler_params=pltpu.CompilerParams(vmem_limit_bytes=max(10 * MIB, DENSIFY_LIMIT - 2 * entries * ROWS * DEPTH)),
+        cost_estimate=pl.CostEstimate(flops=0, bytes_accessed=2 * entries * ROWS * DEPTH, transcendentals=0),
         name="densify",
     )(table, tiles)
 
 
-def aggregate_kernel(base, plan, offsets, groups, n_sources, first, blocks, need, dense_hbm, *refs):
+def aggregate_kernel(plan, offsets, groups, n_sources, first, resident, blocks, need, dense, *refs):
     sources = refs[:n_sources]
     refs = refs[n_sources:]
     start_total = None if first else refs[0]
     refs = refs if first else refs[1:]
     if blocks:
-        outs, total, (dense, feats, sem) = refs[:blocks], refs[blocks], refs[blocks + 1 :]
+        outs, total, (streamed, feats, sem) = refs[:blocks], refs[blocks], refs[blocks + 1 :]
     else:
-        total, dense, feats, sem = refs
+        total, streamed, feats, sem = refs
     entries = len(plan)
     size = ROWS // PIECES
 
     def load(e, p):
-        rows = pl.ds(p * size, size)
-        return pltpu.make_async_copy(dense_hbm.at[base + e, rows, :], dense.at[e, rows, :], sem.at[e, p])
-
-    for e in range(entries):
-        for p in range(PIECES):
-            load(e, p).start()
+        rows = pl.ds(pl.multiple_of(p * size, size), size)
+        return pltpu.make_async_copy(dense.at[e, rows, :], streamed.at[e, rows, :], sem.at[e, p])
+
+    if not resident:
+        for e in range(entries):
+            for p in range(PIECES):
+                load(e, p).start()
     for e, pieces in enumerate(plan):
         for source, column, width, whole in pieces:
             cols = pl.ds(column, width)
@@ -120,17 +129,24 @@
                     feats[e, pl.ds(k * TILE, TILE), cols] = sources[source][rows, :]
             else:
                 feats[e, :, cols] = sources[source][...]
-    for e in range(entries):
-        for p in range(PIECES):
-            rows = pl.ds(p * size, size)
-            load(e, p).wait()
-            term = jnp.dot(dense[e, rows, :], feats[e], preferred_element_type=jnp.float32)
+    if resident:
+        for e in range(entries):
+            term = jnp.dot(dense[e], feats[e], preferred_element_type=jnp.float32)
             if e:
-                total[rows, :] += term
-            elif first:
-                total[rows, :] = term
+                total[...] += term
             else:
-                total[rows, :] = start_total[rows, :] + term
+                total[...] = term if first else start_total[...] + term
+    else:
+        total[...] = jnp.zeros_like(total) if first else start_total[...]
+        for e in range(entries):
+
+            def part(p, c):
+                rows = pl.ds(pl.multiple_of(p * size, size), size)
+                load(e, p).wait()
+                total[rows, :] += jnp.dot(streamed[e, rows, :], feats[e], preferred_element_type=jnp.float32)
+                return c
+
+            lax.fori_loop(0, PIECES, part, 0)
     if blocks:
         own = lax.axis_index("feat")
         size = ROWS // blocks
@@ -139,14 +155,14 @@
             outs[m][...] = total[rows, :].astype(jnp.bfloat16)
 
 
-def aggregate(base, plan, offsets, groups, need, dense, sources, start_total, width, blocks=0):
+def aggregate(plan, offsets, groups, need, dense, resident, sources, start_total, width, blocks=0):
     entries = len(plan)
     first = start_total is None
     smem = pl.BlockSpec(memory_space=pltpu.SMEM)
     vmem = pl.BlockSpec(memory_space=pltpu.VMEM)
     hbm = pl.BlockSpec(memory_space=pl.ANY)
     scratch = [
-        pltpu.VMEM((entries, ROWS, DEPTH), jnp.bfloat16),
+        pltpu.VMEM((8, TILE) if resident else (entries, ROWS, DEPTH), jnp.bfloat16),
         pltpu.VMEM((entries, DEPTH, width), jnp.bfloat16),
         pltpu.SemaphoreType.DMA((entries, PIECES)),
     ]
@@ -158,15 +174,15 @@
         out_shape = jax.ShapeDtypeStruct((ROWS, width), jnp.float32)
         out_specs = vmem
     return pl.pallas_call(
-        functools.partial(aggregate_kernel, base, plan, offsets, groups, len(sources), first, blocks),
+        functools.partial(aggregate_kernel, plan, offsets, groups, len(sources), first, resident, blocks),
         out_shape=out_shape,
-        in_specs=[smem, hbm] + [vmem] * len(sources) + ([] if first else [vmem]),
+        in_specs=[smem, vmem if resident else hbm] + [vmem] * len(sources) + ([] if first else [vmem]),
         out_specs=out_specs,
         scratch_shapes=scratch,
-        compiler_params=pltpu.CompilerParams(vmem_limit_bytes=VMEM_LIMIT),
+        compiler_params=pltpu.CompilerParams(vmem_limit_bytes=RESIDENT_LIMIT if resident else STREAM_LIMIT),
         cost_estimate=pl.CostEstimate(
             flops=2 * entries * ROWS * DEPTH * width,
-            bytes_accessed=entries * PER_PANEL * TILE * TILE * 2,
+            bytes_accessed=entries * ROWS * DEPTH * 2,
             transcendentals=0,
         ),
         name="aggregate",
@@ -197,7 +213,7 @@
         in_specs=[pl.BlockSpec((rows, width), lambda j: (0, 0))] * blocks
         + [pl.BlockSpec((depth, step), lambda j: (0, j))],
         out_specs=pl.BlockSpec((rows, step), lambda j: (0, j)),
-        compiler_params=pltpu.CompilerParams(vmem_limit_bytes=32 * 1024 * 1024),
+        compiler_params=pltpu.CompilerParams(vmem_limit_bytes=16 * MIB),
         name="product",
     )(*parts, w)
 
@@ -234,7 +250,7 @@
         out_shape=jax.ShapeDtypeStruct((DEPTH, source.shape[1]), source.dtype),
         in_specs=[pl.BlockSpec(memory_space=pltpu.SMEM), vmem],
         out_specs=vmem,
-        compiler_params=pltpu.CompilerParams(vmem_limit_bytes=4 * 1024 * 1024),
+        compiler_params=pltpu.CompilerParams(vmem_limit_bytes=4 * MIB),
         name="pick",
     )(need, source)
 
@@ -257,7 +273,15 @@
     need = need_list.reshape(-1)
 
     stages = [[0]] + [[-d, d] for d in range(1, far)] + [[far]]
-    dense = densify([o for stage in stages for o in stage], groups, table, tiles)
+
+    def is_resident(d):
+        return sum(len(stage) for stage in stages[d:]) <= RESIDENT_PANELS
+
+    dense = []
+    for d in range(far + 1):
+        if d in (0, 2) or is_resident(d) != is_resident(d - 1):
+            upto = next((e for e in range(d + 1, far + 1) if e == 2 or is_resident(e) != is_resident(d)), far + 1)
+            dense += densify(stages[d:upto], is_resident(d), groups, table, tiles)
 
     def add(total, d, pieces, final=0):
         plan, sources = [], []
@@ -268,8 +292,7 @@
                 sources.append(array)
                 column += array.shape[1]
             plan.append(tuple(steps))
-        base = sum(len(stage) for stage in stages[:d])
-        return aggregate(base, tuple(plan), stages[d], groups, need, dense, sources, total, width, final)
+        return aggregate(tuple(plan), stages[d], groups, need, dense[d], is_resident(d), sources, total, width, final)
 
     cuts = 2 if width % (2 * TILE) == 0 else 1
     part = width // cuts

time: 121 us -> 116 us (0.959)
  the two profiles are of different devices: /device:TPU:21 before, /device:TPU:0 now
where the time goes in v1:
time: 116 us; the launch traced here: 115 us
  waiting for transfers between devices  38.9 us (34%)
  Pallas kernels  35.6 us (31%)
  local copies, waits for them, and re-layouts  20.2 us (17%)
  starting transfers between devices  17.8 us (15%)
    ppermute x14, waiting for transfers between devices, send(): return lax.ppermute(array, 'rows', ring_pairs(groups, way))  26.9 us
    unnamed x38, local copies, waits for them, and re-layouts  18.8 us
    ppermute x14, starting transfers between devices, send(): return lax.ppermute(array, 'rows', ring_pairs(groups, way))  15.8 us
    pallas_call x5, Pallas kernels, aggregate(): pl.pallas_call(functools.partial(aggregate_kernel, plan, offsets, groups,...  15.7 us
    pallas_call x2, Pallas kernels, densify(): pl.pallas_call(functools.partial(densify_kernel, stages, resident, groups...  14.5 us
    ppermute x3, waiting for transfers between devices, per_device(): lax.ppermute(parts[m], 'feat', [(f, f ^ m) for f in range(blocks)])  12 us
    pallas_call x1, Pallas kernels, product(): pl.pallas_call(functools.partial(product_kernel, blocks), grid=(cols // s...  2.99 us
    pallas_call x4, Pallas kernels, pick(): pl.pallas_call(functools.partial(pick_kernel, reader, offset, groups), ou...  2.45 us
  transfers between devices with their start and end apart: 17, of which 5 were waited for; matrix products, arithmetic and copies ran while one was open for 1% of the time, Pallas kernels for 27%

profile of v1, /device:TPU:0, one launch (start us, length us, event | category | flops | bytes accessed | tf_op | source)
XLA Modules:
  0.0 114.6 jit_solution(4662117348740178824)
XLA Ops:
  0.0 1.3 %fusion = (bf16[2048,128]{1,0:T(8,128)(2,1)S(1)}, bf16[2048,128]{1,0:T(8,128)(2,1)S(1)}) fusion(bf16[2048,256]{1,0:T(8,128)(2,1)} %refs_0_.1), kind=kLoop, calls=%fused_computation.5 | loop fusion | bytes 2097152 | tf_op jit(solution)/shard_map/slice | solution.py:300
  1.3 3.1 %collective-permute-start = (bf16[2048,128]{1,0:T(8,128)(2,1)S(1)}, bf16[2048,128]{1,0:T(8,128)(2,1)S(1)}, u32[]{:S(2)}, u32[]{:S(2)}) collective-permute-start(bf16[2048,128]{1,0:T(8,128)(2,1)S(1)} %get-tuple-element.24), channel_id=1, source_target_pairs={{0,8},{8,16},{16,24},{24,28},{28,20},{20,12},{12,4},{4,0},{1,9},{9... | collective-permute-start | bytes 1572872 | tf_op jit(solution)/shard_map/ppermute | solution.py:270
  4.4 2.0 %collective-permute-start.8 = (bf16[2048,128]{1,0:T(8,128)(2,1)S(1)}, bf16[2048,128]{1,0:T(8,128)(2,1)}, u32[]{:S(2)}, u32[]{:S(2)}) collective-permute-start(bf16[2048,128]{1,0:T(8,128)(2,1)S(1)} %get-tuple-element.23), channel_id=1, source_target_pairs={{0,8},{8,16},{16,24},{24,28},{28,20},{20,12},{12,4},{4,0},{1,9},{9... | collective-permute-start | bytes 1572872 | tf_op jit(solution)/shard_map/ppermute | solution.py:270
  6.4 10.7 %collective-permute-done.refs_0_ = bf16[2048,128]{1,0:T(8,128)(2,1)S(1)} collective-permute-done((bf16[2048,128]{1,0:T(8,128)(2,1)S(1)}, bf16[2048,128]{1,0:T(8,128)(2,1)S(1)}, u32[]{:S(2)}, u32[]{:S(2)}) %collective-permute-start) | collective-permute-done | bytes 524320 | tf_op jit(solution)/shard_map/ppermute | solution.py:270
  17.1 2.1 %collective-permute-start.1 = (bf16[2048,128]{1,0:T(8,128)(2,1)S(1)}, bf16[2048,128]{1,0:T(8,128)(2,1)}, u32[]{:S(2)}, u32[]{:S(2)}) collective-permute-start(bf16[2048,128]{1,0:T(8,128)(2,1)S(1)} %collective-permute-done.refs_0_), channel_id=1, source_target_pairs={{0,8},{8,16},{16,24},{24,28},{28,20},{20,12},{12,4},{4,0},{1,9},{9... | collective-permute-start | bytes 1572872 | tf_op jit(solution)/shard_map/ppermute | solution.py:270
  19.2 0.8 copy-done.10
  20.0 0.8 copy-done.12
  20.8 7.7 %collective-permute-done.8.refs_1_ = bf16[2048,128]{1,0:T(8,128)(2,1)} collective-permute-done((bf16[2048,128]{1,0:T(8,128)(2,1)S(1)}, bf16[2048,128]{1,0:T(8,128)(2,1)}, u32[]{:S(2)}, u32[]{:S(2)}) %collective-permute-start.8) | collective-permute-done | bytes 524320 | tf_op jit(solution)/shard_map/ppermute | solution.py:270
  28.4 2.1 %collective-permute-start.9 = (bf16[2048,128]{1,0:T(8,128)(2,1)}, bf16[2048,128]{1,0:T(8,128)(2,1)S(1)}, u32[]{:S(2)}, u32[]{:S(2)}) collective-permute-start(bf16[2048,128]{1,0:T(8,128)(2,1)} %collective-permute-done.8.refs_1_), channel_id=1, source_target_pairs={{0,8},{8,16},{16,24},{24,28},{28,20},{20,12},{12,4},{4,0},{1,9},{9... | collective-permute-start | bytes 1572872 | tf_op jit(solution)/shard_map/ppermute | solution.py:270
  31.2 8.5 %collective-permute-done.1.refs_0_ = bf16[2048,128]{1,0:T(8,128)(2,1)} collective-permute-done((bf16[2048,128]{1,0:T(8,128)(2,1)S(1)}, bf16[2048,128]{1,0:T(8,128)(2,1)}, u32[]{:S(2)}, u32[]{:S(2)}) %collective-permute-start.1) | collective-permute-done | bytes 524320 | tf_op jit(solution)/shard_map/ppermute | solution.py:270
  39.7 2.1 %collective-permute-start.2 = (bf16[2048,128]{1,0:T(8,128)(2,1)}, bf16[2048,128]{1,0:T(8,128)(2,1)S(1)}, u32[]{:S(2)}, u32[]{:S(2)}) collective-permute-start(bf16[2048,128]{1,0:T(8,128)(2,1)} %collective-permute-done.1.refs_0_), channel_id=1, source_target_pairs={{0,8},{8,16},{16,24},{24,28},{28,20},{20,12},{12,4},{4,0},{1,9},{9... | collective-permute-start | bytes 1572872 | tf_op jit(solution)/shard_map/ppermute | solution.py:270
  41.8 0.7 iota_add_fusion
  42.9 5.7 %densify.3 = (bf16[1,2048,1024]{2,1,0:T(8,128)(2,1)S(1)}, bf16[2,2048,1024]{2,1,0:T(8,128)(2,1)S(1)}) custom-call(s32[1024]{0:T(1024)S(1)} %select_reduce_fusion.table, bf16[640,128,128]{2,1,0:T(8,128)(2,1)} %tiles.3), custom_call_target="tpu_custom_call" | custom-call | bytes 12582912 | tf_op jit(solution)/shard_map/densify/pallas_call | solution.py:87
  48.6 3.3 %copy-done.2 = bf16[2,2048,1024]{2,1,0:T(8,128)(2,1)} copy-done((bf16[2,2048,1024]{2,1,0:T(8,128)(2,1)}, bf16[2,2048,1024]{2,1,0:T(8,128)(2,1)S(1)}, u32[]{:S(2)}) %copy-start.2) | copy-done | bytes 8388632
  51.9 2.0 %copy-done.6 = bf16[1,2048,1024]{2,1,0:T(8,128)(2,1)} copy-done((bf16[1,2048,1024]{2,1,0:T(8,128)(2,1)}, bf16[1,2048,1024]{2,1,0:T(8,128)(2,1)S(1)}, u32[]{:S(2)}) %copy-start.6) | copy-done | bytes 4194328
  53.9 8.8 %densify.2 = (bf16[2,2048,1024]{2,1,0:T(8,128)(2,1)S(1)}, bf16[2,2048,1024]{2,1,0:T(8,128)(2,1)S(1)}, bf16[1,2048,1024]{2,1,0:T(8,128)(2,1)S(1)}) custom-call(s32[1024]{0:T(1024)S(1)} %select_reduce_fusion.table, bf16[640,128,128]{2,1,0:T(8,128)(2,1)} %tiles.3), custom_call_target="tpu_custom_call" | custom-call | bytes 20971520 | tf_op jit(solution)/shard_map/densify/pallas_call | solution.py:87
  62.7 3.3 %copy-done = bf16[2,2048,1024]{2,1,0:T(8,128)(2,1)} copy-done((bf16[2,2048,1024]{2,1,0:T(8,128)(2,1)}, bf16[2,2048,1024]{2,1,0:T(8,128)(2,1)S(1)}, u32[]{:S(2)}) %copy-start) | copy-done | bytes 8388632
  66.0 3.2 %copy-done.1 = bf16[2,2048,1024]{2,1,0:T(8,128)(2,1)} copy-done((bf16[2,2048,1024]{2,1,0:T(8,128)(2,1)}, bf16[2,2048,1024]{2,1,0:T(8,128)(2,1)S(1)}, u32[]{:S(2)}) %copy-start.1) | copy-done | bytes 8388632
  69.2 2.0 %copy-done.4 = bf16[1,2048,1024]{2,1,0:T(8,128)(2,1)} copy-done((bf16[1,2048,1024]{2,1,0:T(8,128)(2,1)}, bf16[1,2048,1024]{2,1,0:T(8,128)(2,1)S(1)}, u32[]{:S(2)}) %copy-start.4) | copy-done | bytes 4194328
  71.3 2.2 %copy-done.7 = bf16[1,2048,1024]{2,1,0:T(8,128)(2,1)S(1)} copy-done((bf16[1,2048,1024]{2,1,0:T(8,128)(2,1)S(1)}, bf16[1,2048,1024]{2,1,0:T(8,128)(2,1)}, u32[]{:S(2)}) %copy-start.7) | copy-done | bytes 4194328
  73.5 1.9 %aggregate.5.refs_4_ = f32[2048,256]{1,0:T(8,128)S(1)} custom-call(s32[512]{0:T(512)S(1)} %reshape.9.need, bf16[1,2048,1024]{2,1,0:T(8,128)(2,1)S(1)} %copy-done.7, bf16[2048,256]{1,0:T(8,128)(2,1)S(1)} %copy-done.8), custom_call_target="tpu_custom_call" | custom-call | flops 1073741824 | bytes 4194304 | tf_op jit(solution)/shard_map/aggregate/pallas_call | solution.py:176
  76.1 1.9 %collective-permute-start.10 = (bf16[1024,128]{1,0:T(8,128)(2,1)S(1)}, bf16[1024,128]{1,0:T(8,128)(2,1)S(1)}, u32[]{:S(2)}, u32[]{:S(2)}) collective-permute-start(bf16[1024,128]{1,0:T(8,128)(2,1)S(1)} %pick.6), channel_id=1, source_target_pairs={{0,8},{8,16},{16,24},{24,28},{28,20},{20,12},{12,4},{4,0},{1,9},{9... | collective-permute-start | bytes 786440 | tf_op jit(solution)/shard_map/ppermute | solution.py:270
  78.9 1.2 %copy-done.13 = bf16[2048,128]{1,0:T(8,128)(2,1)S(1)} copy-done((bf16[2048,128]{1,0:T(8,128)(2,1)S(1)}, bf16[2048,128]{1,0:T(8,128)(2,1)}, u32[]{:S(2)}) %copy-start.13) | copy-done | bytes 524312
  80.0 4.2 %aggregate.6.refs_4_ = f32[2048,256]{1,0:T(8,128)S(1)} custom-call(s32[512]{0:T(512)S(1)} %reshape.9.need, bf16[2,2048,1024]{2,1,0:T(8,128)(2,1)S(1)} %copy-done.3, bf16[2048,128]{1,0:T(8,128)(2,1)S(1)} %copy-done.11, bf16[2048,128]{1,0:T(8,128)(2,1)} %collective-permute-done.8.refs_1_, bf16[2048,128]{1,0:T(8,128)(2,1)} %collective-permute-done.11.refs_2_, ...), custom_call_target="tpu_custom_call" | custom-call | flops 2147483648 | bytes 8388608 | tf_op jit(solution)/shard_map/aggregate/pallas_call | solution.py:176
  84.8 1.9 %collective-permute-start.3 = (bf16[1024,128]{1,0:T(8,128)(2,1)S(1)}, bf16[1024,128]{1,0:T(8,128)(2,1)S(1)}, u32[]{:S(2)}, u32[]{:S(2)}) collective-permute-start(bf16[1024,128]{1,0:T(8,128)(2,1)S(1)} %pick.4), channel_id=1, source_target_pairs={{0,8},{8,16},{16,24},{24,28},{28,20},{20,12},{12,4},{4,0},{1,9},{9... | collective-permute-start | bytes 786440 | tf_op jit(solution)/shard_map/ppermute | solution.py:270
  87.8 4.2 %aggregate.7.refs_4_ = f32[2048,256]{1,0:T(8,128)S(1)} custom-call(s32[512]{0:T(512)S(1)} %reshape.9.need, bf16[2,2048,1024]{2,1,0:T(8,128)(2,1)S(1)} %bitcast.5, bf16[2048,128]{1,0:T(8,128)(2,1)} %collective-permute-done.1.refs_0_, bf16[2048,128]{1,0:T(8,128)(2,1)S(1)} %collective-permute-done.9.source.refs_1_, ...), custom_call_target="tpu_custom_call" | custom-call | flops 2147483648 | bytes 8388608 | tf_op jit(solution)/shard_map/aggregate/pallas_call | solution.py:176
  92.1 3.3 %aggregate.8.refs_2_ = f32[2048,256]{1,0:T(8,128)S(1)} custom-call(s32[512]{0:T(512)S(1)} %reshape.9.need, bf16[2,2048,1024]{2,1,0:T(8,128)(2,1)S(1)} %bitcast.3, bf16[2048,128]{1,0:T(8,128)(2,1)S(1)} %collective-permute-done.2.source.refs_0_, bf16[1024,128]{1,0:T(8,128)(2,1)S(1)} %collective-permute-done.10.refs_1_, ...), custom_call_target="tpu_custom_call" | custom-call | flops 2147483648 | bytes 8388608 | tf_op jit(solution)/shard_map/aggregate/pallas_call | solution.py:176
  95.4 2.1 %aggregate.9 = (bf16[512,256]{1,0:T(8,128)(2,1)S(1)}, bf16[512,256]{1,0:T(8,128)(2,1)S(1)}, bf16[512,256]{1,0:T(8,128)(2,1)S(1)}, bf16[512,256]{1,0:T(8,128)(2,1)S(1)}) custom-call(s32[512]{0:T(512)S(1)} %reshape.9.need, bf16[1,2048,1024]{2,1,0:T(8,128)(2,1)S(1)} %copy-done.5, bf16[1024,128]{1,0:T(8,128)(2,1)S(1)} %collective-permute-done.3.refs_0_, ...), custom_call_target="tpu_custom_call" | custom-call | flops 1073741824 | bytes 4194304 | tf_op jit(solution)/shard_map/aggregate/pallas_call | solution.py:176
  97.6 1.9 %collective-permute-start.15 = (bf16[512,256]{1,0:T(8,128)(2,1)S(1)}, bf16[512,256]{1,0:T(8,128)(2,1)S(1)}, u32[]{:S(2)}, u32[]{:S(2)}) collective-permute-start(bf16[512,256]{1,0:T(8,128)(2,1)S(1)} %get-tuple-element.21), channel_id=1, source_target_pairs={{0,2},{1,3},{2,0},{3,1},{4,6},{5,7},{6,4},{7,5},{8,10},{9,11},{10,... | collective-permute-start | bytes 786440 | tf_op jit(solution)/shard_map/ppermute | solution.py:324
  99.6 7.3 %collective-permute-done.15.refs_2_ = bf16[512,256]{1,0:T(8,128)(2,1)S(1)} collective-permute-done((bf16[512,256]{1,0:T(8,128)(2,1)S(1)}, bf16[512,256]{1,0:T(8,128)(2,1)S(1)}, u32[]{:S(2)}, u32[]{:S(2)}) %collective-permute-start.15) | collective-permute-done | bytes 262176 | tf_op jit(solution)/shard_map/ppermute | solution.py:324
  106.9 4.7 %collective-permute-done.16.refs_3_ = bf16[512,256]{1,0:T(8,128)(2,1)S(1)} collective-permute-done((bf16[512,256]{1,0:T(8,128)(2,1)S(1)}, bf16[512,256]{1,0:T(8,128)(2,1)S(1)}, u32[]{:S(2)}, u32[]{:S(2)}) %collective-permute-start.16) | collective-permute-done | bytes 262176 | tf_op jit(solution)/shard_map/ppermute | solution.py:324
  111.6 3.0 %product.1 = bf16[512,1024]{1,0:T(8,128)(2,1)} custom-call(bf16[512,256]{1,0:T(8,128)(2,1)S(1)} %get-tuple-element.19.refs_0_, bf16[512,256]{1,0:T(8,128)(2,1)S(1)} %collective-permute-done.14.refs_1_, bf16[512,256]{1,0:T(8,128)(2,1)S(1)} %collective-permute-done.15.refs_2_, bf16[512,256]{1,0:T(8,128)(2,1)S(1)} %collective-permute-done.16.refs_3_, ...), custom_call_target="tpu_custom_call" | custom-call | tf_op jit(solution)/shard_map/product/pallas_call | solution.py:209
  (58 shorter events, 3.8 us)
Async XLA Ops:
  1.3 15.8 %collective-permute-start = (bf16[2048,128]{1,0:T(8,128)(2,1)S(1)}, bf16[2048,128]{1,0:T(8,128)(2,1)S(1)}, u32[]{:S(2)}, u32[]{:S(2)}) collective-permute-start(bf16[2048,128]{1,0:T(8,128)(2,1)S(1)} %get-tuple-element.24), channel_id=1, source_target_pairs={{0,8},{8,16},{16,24},{24,28},{28,20},{20,12},{12,4},{4,0},{1,9},{9... | collective-permute-start | bytes 1572872 | tf_op jit(solution)/shard_map/ppermute | solution.py:270
  4.4 15.6 %collective-permute-start.4 = (bf16[2048,128]{1,0:T(8,128)(2,1)S(1)}, bf16[2048,128]{1,0:T(8,128)(2,1)S(1)}, u32[]{:S(2)}, u32[]{:S(2)}) collective-permute-start(bf16[2048,128]{1,0:T(8,128)(2,1)S(1)} %get-tuple-element.23), channel_id=1, source_target_pairs={{0,4},{8,0},{16,8},{24,16},{28,24},{20,28},{12,20},{4,12},{1,5},{9... | collective-permute-start | bytes 1572872 | tf_op jit(solution)/shard_map/ppermute | solution.py:270
  4.4 24.0 %collective-permute-start.8 = (bf16[2048,128]{1,0:T(8,128)(2,1)S(1)}, bf16[2048,128]{1,0:T(8,128)(2,1)}, u32[]{:S(2)}, u32[]{:S(2)}) collective-permute-start(bf16[2048,128]{1,0:T(8,128)(2,1)S(1)} %get-tuple-element.23), channel_id=1, source_target_pairs={{0,8},{8,16},{16,24},{24,28},{28,20},{20,12},{12,4},{4,0},{1,9},{9... | collective-permute-start | bytes 1572872 | tf_op jit(solution)/shard_map/ppermute | solution.py:270
  6.4 24.1 %collective-permute-start.11 = (bf16[2048,128]{1,0:T(8,128)(2,1)S(1)}, bf16[2048,128]{1,0:T(8,128)(2,1)}, u32[]{:S(2)}, u32[]{:S(2)}) collective-permute-start(bf16[2048,128]{1,0:T(8,128)(2,1)S(1)} %get-tuple-element.24), channel_id=1, source_target_pairs={{0,4},{8,0},{16,8},{24,16},{28,24},{20,28},{12,20},{4,12},{1,5},{9... | collective-permute-start | bytes 1572872 | tf_op jit(solution)/shard_map/ppermute | solution.py:270
  17.1 22.6 %collective-permute-start.1 = (bf16[2048,128]{1,0:T(8,128)(2,1)S(1)}, bf16[2048,128]{1,0:T(8,128)(2,1)}, u32[]{:S(2)}, u32[]{:S(2)}) collective-permute-start(bf16[2048,128]{1,0:T(8,128)(2,1)S(1)} %collective-permute-done.refs_0_), channel_id=1, source_target_pairs={{0,8},{8,16},{16,24},{24,28},{28,20},{20,12},{12,4},{4,0},{1,9},{9... | collective-permute-start | bytes 1572872 | tf_op jit(solution)/shard_map/ppermute | solution.py:270
  20.0 21.8 %collective-permute-start.5 = (bf16[2048,128]{1,0:T(8,128)(2,1)S(1)}, bf16[2048,128]{1,0:T(8,128)(2,1)}, u32[]{:S(2)}, u32[]{:S(2)}) collective-permute-start(bf16[2048,128]{1,0:T(8,128)(2,1)S(1)} %collective-permute-done.4.refs_3_), channel_id=1, source_target_pairs={{0,4},{8,0},{16,8},{24,16},{28,24},{20,28},{12,20},{4,12},{1,5},{9... | collective-permute-start | bytes 1572872 | tf_op jit(solution)/shard_map/ppermute | solution.py:270
  28.4 47.0 %collective-permute-start.9 = (bf16[2048,128]{1,0:T(8,128)(2,1)}, bf16[2048,128]{1,0:T(8,128)(2,1)S(1)}, u32[]{:S(2)}, u32[]{:S(2)}) collective-permute-start(bf16[2048,128]{1,0:T(8,128)(2,1)} %collective-permute-done.8.refs_1_), channel_id=1, source_target_pairs={{0,8},{8,16},{16,24},{24,28},{28,20},{20,12},{12,4},{4,0},{1,9},{9... | collective-permute-start | bytes 1572872 | tf_op jit(solution)/shard_map/ppermute | solution.py:270
  30.5 47.5 %collective-permute-start.12 = (bf16[2048,128]{1,0:T(8,128)(2,1)}, bf16[2048,128]{1,0:T(8,128)(2,1)S(1)}, u32[]{:S(2)}, u32[]{:S(2)}) collective-permute-start(bf16[2048,128]{1,0:T(8,128)(2,1)} %collective-permute-done.11.refs_2_), channel_id=1, source_target_pairs={{0,4},{8,0},{16,8},{24,16},{28,24},{20,28},{12,20},{4,12},{1,5},{9... | collective-permute-start | bytes 1572872 | tf_op jit(solution)/shard_map/ppermute | solution.py:270
  39.7 44.5 %collective-permute-start.2 = (bf16[2048,128]{1,0:T(8,128)(2,1)}, bf16[2048,128]{1,0:T(8,128)(2,1)S(1)}, u32[]{:S(2)}, u32[]{:S(2)}) collective-permute-start(bf16[2048,128]{1,0:T(8,128)(2,1)} %collective-permute-done.1.refs_0_), channel_id=1, source_target_pairs={{0,8},{8,16},{16,24},{24,28},{28,20},{20,12},{12,4},{4,0},{1,9},{9... | collective-permute-start | bytes 1572872 | tf_op jit(solution)/shard_map/ppermute | solution.py:270
  41.7 45.0 %collective-permute-start.6 = (bf16[2048,128]{1,0:T(8,128)(2,1)}, bf16[2048,128]{1,0:T(8,128)(2,1)S(1)}, u32[]{:S(2)}, u32[]{:S(2)}) collective-permute-start(bf16[2048,128]{1,0:T(8,128)(2,1)} %collective-permute-done.5.refs_3_), channel_id=1, source_target_pairs={{0,4},{8,0},{16,8},{24,16},{28,24},{20,28},{12,20},{4,12},{1,5},{9... | collective-permute-start | bytes 1572872 | tf_op jit(solution)/shard_map/ppermute | solution.py:270
  48.6 3.3 %copy-start.2 = (bf16[2,2048,1024]{2,1,0:T(8,128)(2,1)}, bf16[2,2048,1024]{2,1,0:T(8,128)(2,1)S(1)}, u32[]{:S(2)}) copy-start(bf16[2,2048,1024]{2,1,0:T(8,128)(2,1)S(1)} %get-tuple-element.17.dense) | copy-start | bytes 25165828
  53.9 17.3 %copy-start.14 = (s32[8,8,8]{2,1,0:T(8,128)S(1)}, s32[8,8,8]{2,1,0:T(8,128)}, u32[]{:S(2)}) copy-start(s32[8,8,8]{2,1,0:T(8,128)} %param.14) | copy-start | bytes 6148
  53.9 17.4 %copy-start.8 = (bf16[2048,256]{1,0:T(8,128)(2,1)S(1)}, bf16[2048,256]{1,0:T(8,128)(2,1)}, u32[]{:S(2)}) copy-start(bf16[2048,256]{1,0:T(8,128)(2,1)} %refs_0_.1) | copy-start | bytes 3145732
  62.7 3.3 %copy-start = (bf16[2,2048,1024]{2,1,0:T(8,128)(2,1)}, bf16[2,2048,1024]{2,1,0:T(8,128)(2,1)S(1)}, u32[]{:S(2)}) copy-start(bf16[2,2048,1024]{2,1,0:T(8,128)(2,1)S(1)} %get-tuple-element.15.dense) | copy-start | bytes 25165828
  66.0 3.2 %copy-start.1 = (bf16[2,2048,1024]{2,1,0:T(8,128)(2,1)}, bf16[2,2048,1024]{2,1,0:T(8,128)(2,1)S(1)}, u32[]{:S(2)}) copy-start(bf16[2,2048,1024]{2,1,0:T(8,128)(2,1)S(1)} %get-tuple-element.16.dense) | copy-start | bytes 25165828
  69.2 2.0 %copy-start.4 = (bf16[1,2048,1024]{2,1,0:T(8,128)(2,1)}, bf16[1,2048,1024]{2,1,0:T(8,128)(2,1)S(1)}, u32[]{:S(2)}) copy-start(bf16[1,2048,1024]{2,1,0:T(8,128)(2,1)S(1)} %get-tuple-element.14.dense) | copy-start | bytes 12582916
  71.3 2.2 %copy-start.7 = (bf16[1,2048,1024]{2,1,0:T(8,128)(2,1)S(1)}, bf16[1,2048,1024]{2,1,0:T(8,128)(2,1)}, u32[]{:S(2)}) copy-start(bf16[1,2048,1024]{2,1,0:T(8,128)(2,1)} %copy-done.6) | copy-start | bytes 12582916
  73.5 5.3 %copy-start.3 = (bf16[2,2048,1024]{2,1,0:T(8,128)(2,1)S(1)}, bf16[2,2048,1024]{2,1,0:T(8,128)(2,1)}, u32[]{:S(2)}) copy-start(bf16[2,2048,1024]{2,1,0:T(8,128)(2,1)} %copy-done.2) | copy-start | bytes 25165828
  73.5 5.3 %copy-start.11 = (bf16[2048,128]{1,0:T(8,128)(2,1)S(1)}, bf16[2048,128]{1,0:T(8,128)(2,1)}, u32[]{:S(2)}) copy-start(bf16[2048,128]{1,0:T(8,128)(2,1)} %copy-done.10) | copy-start | bytes 1572868
  76.1 15.9 %collective-permute-start.10 = (bf16[1024,128]{1,0:T(8,128)(2,1)S(1)}, bf16[1024,128]{1,0:T(8,128)(2,1)S(1)}, u32[]{:S(2)}, u32[]{:S(2)}) collective-permute-start(bf16[1024,128]{1,0:T(8,128)(2,1)S(1)} %pick.6), channel_id=1, source_target_pairs={{0,8},{8,16},{16,24},{24,28},{28,20},{20,12},{12,4},{4,0},{1,9},{9... | collective-permute-start | bytes 786440 | tf_op jit(solution)/shard_map/ppermute | solution.py:270
  78.6 13.4 %collective-permute-start.13 = (bf16[1024,128]{1,0:T(8,128)(2,1)S(1)}, bf16[1024,128]{1,0:T(8,128)(2,1)S(1)}, u32[]{:S(2)}, u32[]{:S(2)}) collective-permute-start(bf16[1024,128]{1,0:T(8,128)(2,1)S(1)} %pick.7), channel_id=1, source_target_pairs={{0,4},{8,0},{16,8},{24,16},{28,24},{20,28},{12,20},{4,12},{1,5},{9... | collective-permute-start | bytes 786440 | tf_op jit(solution)/shard_map/ppermute | solution.py:270
  78.8 8.9 %slice-start.2 = ((s8[8388608]{0:T(1024)(128)(4,1)}), s8[4194304]{0:T(1024)(128)(4,1)S(1)}, s32[]{:S(2)}) async-start(s8[8388608]{0:T(1024)(128)(4,1)} %bitcast.4), calls=%async_computation.2 | async-start | bytes 8388608
  80.0 7.7 %slice-start.3 = ((s8[8388608]{0:T(1024)(128)(4,1)}), s8[4194304]{0:T(1024)(128)(4,1)S(1)}, s32[]{:S(2)}) async-start(s8[8388608]{0:T(1024)(128)(4,1)} %bitcast.4), calls=%async_computation.3 | async-start | bytes 8388608
  84.8 10.6 %collective-permute-start.3 = (bf16[1024,128]{1,0:T(8,128)(2,1)S(1)}, bf16[1024,128]{1,0:T(8,128)(2,1)S(1)}, u32[]{:S(2)}, u32[]{:S(2)}) collective-permute-start(bf16[1024,128]{1,0:T(8,128)(2,1)S(1)} %pick.4), channel_id=1, source_target_pairs={{0,8},{8,16},{16,24},{24,28},{28,20},{20,12},{12,4},{4,0},{1,9},{9... | collective-permute-start | bytes 786440 | tf_op jit(solution)/shard_map/ppermute | solution.py:270
  86.8 5.3 %slice-start = ((s8[8388608]{0:T(1024)(128)(4,1)}), s8[4194304]{0:T(1024)(128)(4,1)S(1)}, s32[]{:S(2)}) async-start(s8[8388608]{0:T(1024)(128)(4,1)} %bitcast.2), calls=%async_computation | async-start | bytes 8388608
  87.4 8.0 %collective-permute-start.7 = (bf16[1024,128]{1,0:T(8,128)(2,1)S(1)}, bf16[1024,128]{1,0:T(8,128)(2,1)S(1)}, u32[]{:S(2)}, u32[]{:S(2)}) collective-permute-start(bf16[1024,128]{1,0:T(8,128)(2,1)S(1)} %pick.5), channel_id=1, source_target_pairs={{0,4},{8,0},{16,8},{24,16},{28,24},{20,28},{12,20},{4,12},{1,5},{9... | collective-permute-start | bytes 786440 | tf_op jit(solution)/shard_map/ppermute | solution.py:270
  87.8 4.3 %slice-start.1 = ((s8[8388608]{0:T(1024)(128)(4,1)}), s8[4194304]{0:T(1024)(128)(4,1)S(1)}, s32[]{:S(2)}) async-start(s8[8388608]{0:T(1024)(128)(4,1)} %bitcast.2), calls=%async_computation.1 | async-start | bytes 8388608
  92.1 3.4 %copy-start.5 = (bf16[1,2048,1024]{2,1,0:T(8,128)(2,1)S(1)}, bf16[1,2048,1024]{2,1,0:T(8,128)(2,1)}, u32[]{:S(2)}) copy-start(bf16[1,2048,1024]{2,1,0:T(8,128)(2,1)} %copy-done.4) | copy-start | bytes 12582916
  95.4 16.2 %copy-start.9 = (bf16[1024,1024]{1,0:T(8,128)(2,1)S(1)}, bf16[1024,1024]{1,0:T(8,128)(2,1)}, u32[]{:S(2)}) copy-start(bf16[1024,1024]{1,0:T(8,128)(2,1)} %refs_4_.1) | copy-start | bytes 6291460
  97.5 2.0 %collective-permute-start.14 = (bf16[512,256]{1,0:T(8,128)(2,1)S(1)}, bf16[512,256]{1,0:T(8,128)(2,1)S(1)}, u32[]{:S(2)}, u32[]{:S(2)}) collective-permute-start(bf16[512,256]{1,0:T(8,128)(2,1)S(1)} %get-tuple-element.20), channel_id=1, source_target_pairs={{0,1},{1,0},{2,3},{3,2},{4,5},{5,4},{6,7},{7,6},{8,9},{9,8},{10,11... | collective-permute-start | bytes 786440 | tf_op jit(solution)/shard_map/ppermute | solution.py:324
  97.6 9.2 %collective-permute-start.15 = (bf16[512,256]{1,0:T(8,128)(2,1)S(1)}, bf16[512,256]{1,0:T(8,128)(2,1)S(1)}, u32[]{:S(2)}, u32[]{:S(2)}) collective-permute-start(bf16[512,256]{1,0:T(8,128)(2,1)S(1)} %get-tuple-element.21), channel_id=1, source_target_pairs={{0,2},{1,3},{2,0},{3,1},{4,6},{5,7},{6,4},{7,5},{8,10},{9,11},{10,... | collective-permute-start | bytes 786440 | tf_op jit(solution)/shard_map/ppermute | solution.py:324
  99.5 12.1 %collective-permute-start.16 = (bf16[512,256]{1,0:T(8,128)(2,1)S(1)}, bf16[512,256]{1,0:T(8,128)(2,1)S(1)}, u32[]{:S(2)}, u32[]{:S(2)}) collective-permute-start(bf16[512,256]{1,0:T(8,128)(2,1)S(1)} %get-tuple-element.22), channel_id=1, source_target_pairs={{0,3},{1,2},{2,1},{3,0},{4,7},{5,6},{6,5},{7,4},{8,11},{9,10},{10,... | collective-permute-start | bytes 786440 | tf_op jit(solution)/shard_map/ppermute | solution.py:324
  (4 other events, 4.7 us)

commit v2 on v1

v2 whole, which is shorter than its diff:
```python
import functools

import jax
import jax.numpy as jnp
from jax import lax
from jax.experimental import pallas as pl
from jax.experimental.pallas import tpu as pltpu
from jax.sharding import PartitionSpec as P


TILE = 128
TPP = 16
NEED = 8
PER_PANEL = TPP * NEED
ROWS = TPP * TILE
DEPTH = NEED * TILE
MIB = 1024 * 1024
RESIDENT_PANELS = 8
RESIDENT_LIMIT = 9 * MIB
STREAM_LIMIT = 14 * MIB
DENSIFY_LIMIT = 38 * MIB


def place_tiles(panel, table, tiles, dense, sem):
    base = panel * PER_PANEL

    def row_step(row, found):
        for k in range(NEED):
            slot = table[base + row * NEED + k]
            rows = pl.ds(pl.multiple_of(row * TILE, TILE), TILE)
            cols = pl.ds(k * TILE, TILE)

            @pl.when(slot > 0)
            def _():
                pltpu.make_async_copy(tiles.at[slot - 1], dense.at[rows, cols], sem).start()

            @pl.when(slot == 0)
            def _():
                dense[rows, cols] = jnp.zeros((TILE, TILE), jnp.bfloat16)

            found = found + jnp.where(slot > 0, 1, 0)
        return found

    return lax.fori_loop(0, TPP, row_step, 0)


def await_tiles(found, tiles, dense, sem):
    def wait_one(i, c):
        pltpu.make_async_copy(tiles.at[0], dense.at[pl.ds(0, TILE), pl.ds(0, TILE)], sem).wait()
        return c

    lax.fori_loop(0, found, wait_one, 0)


def densify_kernel(stages, resident, groups, table, tiles, *refs):
    outs, (dense, tile_sem, out_sem) = refs[: len(stages)], refs[len(stages) :]
    entries = [(out, e, o) for out, stage in zip(outs, stages) for e, o in enumerate(stage)]
    if resident:
        found = [
            place_tiles(group_at(o, groups), table, tiles, out.at[e], tile_sem.at[0]) for out, e, o in entries
        ]
        out, e, o = entries[0]
        await_tiles(sum(found), tiles, out.at[e], tile_sem.at[0])
        return
    buffers = dense.shape[0]

    def store(i):
        out, e, _ = entries[i]
        return pltpu.make_async_copy(dense.at[i % buffers], out.at[e], out_sem.at[i % buffers])

    for i, (out, e, o) in enumerate(entries):
        buf = i % buffers
        if i >= buffers:
            store(i - buffers).wait()
        found = place_tiles(group_at(o, groups), table, tiles, dense.at[buf], tile_sem.at[buf])
        await_tiles(found, tiles, dense.at[buf], tile_sem.at[buf])
        store(i).start()
    for i in range(max(0, len(entries) - buffers), len(entries)):
        store(i).wait()


def densify(stages, resident, groups, table, tiles):
    buffers = 1 if resident else 2
    out_space = pltpu.VMEM if resident else pl.ANY
    entries = sum(len(stage) for stage in stages)
    return pl.pallas_call(
        functools.partial(densify_kernel, stages, resident, groups),
        out_shape=[jax.ShapeDtypeStruct((len(stage), ROWS, DEPTH), jnp.bfloat16) for stage in stages],
        in_specs=[pl.BlockSpec(memory_space=pltpu.SMEM), pl.BlockSpec(memory_space=pl.ANY)],
        out_specs=[pl.BlockSpec(memory_space=out_space)] * len(stages),
        scratch_shapes=[
            pltpu.VMEM((8, TILE) if resident else (buffers, ROWS, DEPTH), jnp.bfloat16),
            pltpu.SemaphoreType.DMA((buffers,)),
            pltpu.SemaphoreType.DMA((buffers,)),
        ],
        compiler_params=pltpu.CompilerParams(vmem_limit_bytes=max(10 * MIB, DENSIFY_LIMIT - 2 * entries * ROWS * DEPTH)),
        cost_estimate=pl.CostEstimate(flops=0, bytes_accessed=2 * entries * ROWS * DEPTH, transcendentals=0),
        name="densify",
    )(table, tiles)


def group_at(offset, groups):
    own = lax.axis_index("rows")
    place = jnp.where(lax.rem(own, 2) == 0, lax.div(own, 2), groups - 1 - lax.div(own, 2))
    place = lax.rem(place + offset + groups, groups)
    return jnp.where(place < groups // 2, 2 * place, 2 * (groups - 1 - place) + 1)


def needed_tile(need, groups, reader, offset, k):
    return need[(group_at(reader, groups) * groups + group_at(offset, groups)) * NEED + k]


def gather_feats(need, groups, reader, offset, chunks, whole, put):
    for k in range(NEED):
        if not whole:
            put(k, chunks[0][pl.ds(k * TILE, TILE), :])
            continue
        tile = needed_tile(need, groups, reader, offset, k)
        per_chunk = TPP // len(chunks)
        if len(chunks) == 1:
            put(k, chunks[0][pl.ds(pl.multiple_of(tile * TILE, TILE), TILE), :])
            continue
        for i, chunk in enumerate(chunks):

            @pl.when(lax.div(tile, per_chunk) == i)
            def _():
                row = pl.multiple_of(lax.rem(tile, per_chunk) * TILE, TILE)
                put(k, chunk[pl.ds(row, TILE), :])


def aggregate_kernel(plan, groups, n_sources, n_dense, n_totals, widths, first, blocks, need, *refs):
    sources, refs = refs[:n_sources], refs[n_sources:]
    denses, refs = refs[:n_dense], refs[n_dense:]
    if not first:
        start_totals, refs = refs[:n_totals], refs[n_totals:]
    n_outs = n_totals * max(1, blocks)
    outs, (streamed, feats, *work, sem) = refs[:n_outs], refs[n_outs:]
    totals = work if blocks else outs
    starts = [sum(widths[:t]) for t in range(n_totals)]
    fresh = [first] * n_totals

    for operand, index, resident, offset, pieces in plan:
        if not resident:
            copy = pltpu.make_async_copy(denses[operand].at[index], streamed, sem)
            copy.start()
        for part, chunks, whole in pieces:
            cols = pl.ds(starts[part], widths[part])

            def put(k, value):
                feats[pl.ds(k * TILE, TILE), cols] = value

            gather_feats(need, groups, 0, offset, [sources[i] for i in chunks], whole, put)
        if not resident:
            copy.wait()
        lhs = denses[operand][index] if resident else streamed[...]
        parts = [part for part, chunks, whole in pieces]
        low, high = starts[parts[0]], starts[parts[-1]] + widths[parts[-1]]
        term = jnp.dot(lhs, feats[:, low:high], preferred_element_type=jnp.float32)
        for part in parts:
            piece = term[:, starts[part] - low : starts[part] - low + widths[part]]
            if fresh[part]:
                totals[part][...] = piece
            elif plan_first(plan, part) == (operand, index):
                totals[part][...] = start_totals[part][...] + piece
            else:
                totals[part][...] += piece
            fresh[part] = False
    for part in range(n_totals):
        if not first and plan_first(plan, part) is None:
            totals[part][...] = start_totals[part][...]
    if blocks:
        own = lax.axis_index("feat")
        size = ROWS // blocks
        for part in range(n_totals):
            for m in range(blocks):
                rows = pl.ds(pl.multiple_of((own ^ m) * size, size), size)
                outs[part * blocks + m][...] = totals[part][rows, :].astype(jnp.bfloat16)


def plan_first(plan, part):
    for operand, index, resident, offset, pieces in plan:
        if any(piece[0] == part for piece in pieces):
            return (operand, index)
    return None


def aggregate(plan, groups, need, sources, denses, totals, widths, blocks=0):
    first = totals is None
    n_totals = len(widths)
    smem = pl.BlockSpec(memory_space=pltpu.SMEM)
    vmem = pl.BlockSpec(memory_space=pltpu.VMEM)
    spaces = [None] * len(denses)
    for operand, index, resident, offset, pieces in plan:
        spaces[operand] = vmem if resident else pl.BlockSpec(memory_space=pl.ANY)
    streams = any(not entry[2] for entry in plan)
    scratch = [
        pltpu.VMEM((ROWS, DEPTH) if streams else (8, TILE), jnp.bfloat16),
        pltpu.VMEM((DEPTH, sum(widths)), jnp.bfloat16),
    ]
    if blocks:
        out_shape = [jax.ShapeDtypeStruct((ROWS // blocks, w), jnp.bfloat16) for w in widths for _ in range(blocks)]
        scratch += [pltpu.VMEM((ROWS, w), jnp.float32) for w in widths]
    else:
        out_shape = [jax.ShapeDtypeStruct((ROWS, w), jnp.float32) for w in widths]
    flops = sum(2 * ROWS * DEPTH * sum(widths[p[0]] for p in entry[4]) for entry in plan)
    return pl.pallas_call(
        functools.partial(
            aggregate_kernel, plan, groups, len(sources), len(denses), n_totals, widths, first, blocks
        ),
        out_shape=out_shape,
        in_specs=[smem] + [vmem] * len(sources) + spaces + ([] if first else [vmem] * n_totals),
        out_specs=[vmem] * len(out_shape),
        scratch_shapes=scratch + [pltpu.SemaphoreType.DMA],
        compiler_params=pltpu.CompilerParams(vmem_limit_bytes=STREAM_LIMIT if streams else RESIDENT_LIMIT),
        cost_estimate=pl.CostEstimate(
            flops=flops, bytes_accessed=len(plan) * ROWS * DEPTH * 2, transcendentals=0
        ),
        name="aggregate",
    )(need, *sources, *denses, *([] if first else totals))


def pick_kernel(reader, offset, groups, need, *refs):
    chunks, out = refs[:-1], refs[-1]

    def put(k, value):
        out[pl.ds(k * TILE, TILE), :] = value

    gather_feats(need, groups, reader, offset, chunks, True, put)


def pick(need, chunks, reader, offset, groups):
    vmem = pl.BlockSpec(memory_space=pltpu.VMEM)
    return pl.pallas_call(
        functools.partial(pick_kernel, reader, offset, groups),
        out_shape=jax.ShapeDtypeStruct((DEPTH, chunks[0].shape[1]), chunks[0].dtype),
        in_specs=[pl.BlockSpec(memory_space=pltpu.SMEM)] + [vmem] * len(chunks),
        out_specs=vmem,
        compiler_params=pltpu.CompilerParams(vmem_limit_bytes=4 * MIB),
        name="pick",
    )(need, *chunks)


def product_kernel(terms, starts, shard, last, w, *refs):
    parts, refs = refs[:terms], refs[terms:]
    own = lax.axis_index("feat")
    total = None if last is None else refs[0][...]
    out = refs[-1]
    for i in range(0, terms, 2):
        pair = range(i, min(i + 2, terms))
        x = jnp.concatenate([parts[j][...] for j in pair], axis=1)
        rows = []
        for j in pair:
            m, column = starts[j]
            row = pl.multiple_of((own ^ m) * shard + column, TILE)
            rows.append(w[pl.ds(row, parts[j].shape[1]), :])
        term = jnp.dot(x, jnp.concatenate(rows, axis=0), preferred_element_type=jnp.float32)
        total = term if total is None else total + term
    out[...] = total if out.dtype == jnp.float32 else jnp.maximum(total, 0.0).astype(out.dtype)


def product(operands, starts, shard, w, start_total, dtype):
    rows = operands[0].shape[0]
    depth, cols = w.shape
    step = 256
    vmem = pl.BlockSpec(memory_space=pltpu.VMEM)
    band = pl.BlockSpec((rows, step), lambda j: (0, j))
    first = start_total is None
    return pl.pallas_call(
        functools.partial(product_kernel, len(operands), starts, shard, None if first else 0),
        grid=(cols // step,),
        out_shape=jax.ShapeDtypeStruct((rows, cols), dtype),
        in_specs=[pl.BlockSpec((depth, step), lambda j: (0, j))]
        + [pl.BlockSpec(x.shape, lambda j: (0, 0)) for x in operands]
        + ([] if first else [band]),
        out_specs=band,
        compiler_params=pltpu.CompilerParams(vmem_limit_bytes=16 * MIB),
        cost_estimate=pl.CostEstimate(
            flops=2 * rows * cols * sum(x.shape[1] for x in operands), bytes_accessed=8 * rows * cols, transcendentals=0
        ),
        name="product",
    )(w, *operands, *([] if first else [start_total]))


def slot_table(groups, tile_row, tile_panel, tile_slot, counts):
    slots = lax.iota(jnp.int32, tile_row.shape[0])
    key = (tile_panel * TPP + tile_row) * NEED + tile_slot
    key = jnp.where(slots < counts[0], key, -1)
    places = lax.iota(jnp.int32, groups * PER_PANEL)
    return jnp.max(jnp.where(key[None, :] == places[:, None], slots[None, :] + 1, 0), axis=1)


def ring_pairs(groups, way):
    order = [2 * p if p < groups // 2 else 2 * (groups - 1 - p) + 1 for p in range(groups)]
    return [(order[p], order[(p + way) % groups]) for p in range(groups)]


def per_device(features, tiles, tile_row, tile_panel, tile_slot, counts, need_list, weight):
    width = features.shape[1]
    groups = lax.axis_size("rows")
    blocks = lax.axis_size("feat")
    far = groups // 2
    cuts = part_count(width)
    part = width // cuts
    widths = (part,) * cuts
    last = cuts - 1
    need = need_list.reshape(-1)

    def send(array, way):
        return lax.ppermute(array, "rows", ring_pairs(groups, way))

    held = {}
    for c in range(cuts):
        column = features[:, c * part : (c + 1) * part]
        for way in (1, -1):
            n = chunk_count(way, c)
            held[way, 0, c] = ([column[i * ROWS // n : (i + 1) * ROWS // n] for i in range(n)], True)
    for d in range(1, far + 1):
        for c in range(cuts):
            for way in (1, -1):
                end = hop_end(way, c, far)
                chunks = held.get((way, d - 1, c), (None,))[0]
                if d < end:
                    held[way, d, c] = ([send(x, way) for x in chunks], True)
                elif d == end:
                    chosen = pick(need, chunks, way, way - way * d, groups)
                    held[way, d, c] = ([send(chosen, way)], False)

    table = slot_table(groups, tile_row, tile_panel, tile_slot, counts)
    stages = [[0]] + [[-d, d] for d in range(1, far)] + [[far]]

    def is_resident(d):
        return sum(len(stage) for stage in stages[d:]) <= RESIDENT_PANELS

    dense = []
    for d in range(far + 1):
        if d in (0, 2) or is_resident(d) != is_resident(d - 1):
            upto = next((e for e in range(d + 1, far + 1) if e == 2 or is_resident(e) != is_resident(d)), far + 1)
            dense += densify(stages[d:upto], is_resident(d), groups, table, tiles)

    def add(totals, entries, columns, final=0):
        sources, operands, plan = [], [], []
        for way, d, parts in entries:
            if d not in operands:
                operands.append(d)
            offset = -way * d
            pieces = []
            for c in parts:
                chunks, whole = held[-1 if d == 0 else way, d, c]
                pieces.append((columns.index(c), tuple(range(len(sources), len(sources) + len(chunks))), whole))
                sources += chunks
            index = stages[d].index(offset) if d < far else 0
            plan.append((operands.index(d), index, is_resident(d), offset, tuple(pieces)))
        sizes = tuple(widths[c] for c in columns)
        return aggregate(tuple(plan), groups, need, sources, [dense[d] for d in operands], totals, sizes, final)

    every = list(range(cuts))
    totals = add(None, [(1, 0, every)], every)
    for d in range(1, far - 2):
        totals = add(totals, [(1, d, every), (-1, d, every)], every)
    d = far - 2
    if cuts > 1:
        early = [(-1, d, every), (1, d, [0]), (1, d + 1, [0])]
        totals = add(totals, early, every)
        rest = add([totals[1]], [(1, d, [1]), (-1, d + 1, [1])], [1])
        ends = [
            add([totals[0]], [(-1, d + 1, [0]), (1, far, [0])], [0], blocks),
            add(rest, [(1, d + 1, [1]), (-1, far, [1])], [1], blocks),
        ]
    else:
        totals = add(totals, [(1, d, every), (-1, d, every)], every)
        totals = add(totals, [(1, d + 1, every), (-1, d + 1, every)], every)
        ends = [add(totals, [(1, far, every)], every, blocks)]

    def exchange(c, m):
        if m == 0:
            return ends[c][0]
        return lax.ppermute(ends[c][m], "feat", [(f, f ^ m) for f in range(blocks)])

    order = [(c, m) for c in range(cuts) for m in reversed(range(blocks))]
    arrived = {key: exchange(*key) for key in order}
    late = [(last, m) for m in range(2, blocks)]
    soon = [(c, m) for m in range(blocks) for c in range(cuts) if (c, m) not in late]

    def multiply(keys, start_total, dtype):
        starts = tuple((m, c * part) for c, m in keys)
        return product([arrived[key] for key in keys], starts, width, weight, start_total, dtype)

    if not late:
        return multiply(soon, None, jnp.bfloat16)
    return multiply(late, multiply(soon, None, jnp.float32), jnp.bfloat16)


def part_count(width):
    return 2 if width % (2 * TILE) == 0 else 1


def chunk_count(way, c):
    return 2 if way > 0 and c == 1 else 1


def hop_end(way, c, far):
    return far if (way > 0) == (c == 0) else far - 1


def solution(mesh):
    return jax.shard_map(
        per_device,
        mesh=mesh,
        in_specs=(
            P("rows", "feat"),
            P("rows", None, None),
            P("rows"),
            P("rows"),
            P("rows"),
            P("rows"),
            P(),
            P(),
        ),
        out_specs=P(("rows", "feat"), None),
        check_vma=False,
    )
```

time: 116 us -> 124 us (1.069)
  waiting for transfers between devices: 38.9 us -> 31.3 us
  Pallas kernels: 35.6 us -> 42.1 us
  starting transfers between devices: 17.8 us -> 23.9 us
  local copies, waits for them, and re-layouts: 20.2 us -> 24.2 us
    ppermute x3 -> x6, waiting for transfers between devices: 12 us -> 4.86 us  [exchange(): return lax.ppermute(ends[c][m], 'feat', [(f, f ^ m) for f in range(blocks)])]
    pallas_call x6 -> x8, Pallas kernels: 18.7 us -> 25.1 us  [the longest x6 20.6 us: aggregate(): pl.pallas_call(functools.partial(aggregate_kernel, plan, groups, len(sour...]
    ppermute x14 -> x16, starting transfers between devices: 15.8 us -> 20 us  [send(): return lax.ppermute(array, 'rows', ring_pairs(groups, way))]
    unnamed x38 -> x40, local copies, waits for them, and re-layouts: 18.8 us -> 21.6 us
    ppermute x3 -> x6, starting transfers between devices: 2.01 us -> 3.89 us  [exchange(): return lax.ppermute(ends[c][m], 'feat', [(f, f ^ m) for f in range(blocks)])]
    slice x1 -> x2, local copies, waits for them, and re-layouts: 1.27 us -> 2.56 us  [the longest x1 1.31 us: per_device(): column = features[:, c * part:(c + 1) * part]]
    ppermute x14 -> x16, waiting for transfers between devices: 26.9 us -> 26.4 us  [send(): return lax.ppermute(array, 'rows', ring_pairs(groups, way))]
  transfers between devices with their start and end apart: 17 -> 22, of which waited for: 5 -> 8; matrix products, arithmetic and copies ran while one was open for 1% -> 1% of each run, Pallas kernels for 27% -> 32%
where the time goes in v2:
time: 124 us; the launch traced here: 123 us
  Pallas kernels  42.1 us (34%)
  waiting for transfers between devices  31.3 us (25%)
  local copies, waits for them, and re-layouts  24.2 us (20%)
  starting transfers between devices  23.9 us (19%)
    ppermute x16, waiting for transfers between devices, send(): return lax.ppermute(array, 'rows', ring_pairs(groups, way))  26.4 us
    unnamed x40, local copies, waits for them, and re-layouts  21.6 us
    pallas_call x6, Pallas kernels, aggregate(): pl.pallas_call(functools.partial(aggregate_kernel, plan, groups, len(sour...  20.6 us
    ppermute x16, starting transfers between devices, send(): return lax.ppermute(array, 'rows', ring_pairs(groups, way))  20 us
    pallas_call x2, Pallas kernels, densify(): pl.pallas_call(functools.partial(densify_kernel, stages, resident, groups...  14.5 us
    ppermute x6, waiting for transfers between devices, exchange(): return lax.ppermute(ends[c][m], 'feat', [(f, f ^ m) for f in range(blocks)])  4.86 us
    pallas_call x2, Pallas kernels, product(): pl.pallas_call(functools.partial(product_kernel, len(operands), starts, s...  4.45 us
    ppermute x6, starting transfers between devices, exchange(): return lax.ppermute(ends[c][m], 'feat', [(f, f ^ m) for f in range(blocks)])  3.89 us
  transfers between devices with their start and end apart: 22, of which 8 were waited for; matrix products, arithmetic and copies ran while one was open for 1% of the time, Pallas kernels for 32%

profile of v2, /device:TPU:0, one launch (start us, length us, event | category | flops | bytes accessed | tf_op | source)
XLA Modules:
  0.0 122.9 jit_solution(3669344553438542254)
XLA Ops:
  1.3 3.1 %collective-permute-start.11 = (bf16[2048,128]{1,0:T(8,128)(2,1)S(1)}, bf16[2048,128]{1,0:T(8,128)(2,1)S(1)}, u32[]{:S(2)}, u32[]{:S(2)}) collective-permute-start(bf16[2048,128]{1,0:T(8,128)(2,1)S(1)} %get-tuple-element.43.refs_0_), channel_id=1, source_target_pairs={{0,8},{8,16},{16,24},{24,28},{28,20},{20,12},{12,4},{4,0},{1,9},{9... | collective-permute-start | bytes 1572872 | tf_op jit(solution)/shard_map/ppermute | solution.py:309
  4.4 2.0 %collective-permute-start.9 = (bf16[2048,128]{1,0:T(8,128)(2,1)S(1)}, bf16[2048,128]{1,0:T(8,128)(2,1)}, u32[]{:S(2)}, u32[]{:S(2)}) collective-permute-start(bf16[2048,128]{1,0:T(8,128)(2,1)S(1)} %get-tuple-element.43.refs_0_), channel_id=1, source_target_pairs={{0,4},{8,0},{16,8},{24,16},{28,24},{20,28},{12,20},{4,12},{1,5},{9... | collective-permute-start | bytes 1572872 | tf_op jit(solution)/shard_map/ppermute | solution.py:309
  6.4 9.9 %collective-permute-done.11.refs_0_ = bf16[2048,128]{1,0:T(8,128)(2,1)S(1)} collective-permute-done((bf16[2048,128]{1,0:T(8,128)(2,1)S(1)}, bf16[2048,128]{1,0:T(8,128)(2,1)S(1)}, u32[]{:S(2)}, u32[]{:S(2)}) %collective-permute-start.11) | collective-permute-done | bytes 524320 | tf_op jit(solution)/shard_map/ppermute | solution.py:309
  16.3 1.8 %collective-permute-start.12 = (bf16[2048,128]{1,0:T(8,128)(2,1)S(1)}, bf16[2048,128]{1,0:T(8,128)(2,1)}, u32[]{:S(2)}, u32[]{:S(2)}) collective-permute-start(bf16[2048,128]{1,0:T(8,128)(2,1)S(1)} %collective-permute-done.11.refs_0_), channel_id=1, source_target_pairs={{0,8},{8,16},{16,24},{24,28},{28,20},{20,12},{12,4},{4,0},{1,9},{9... | collective-permute-start | bytes 1572872 | tf_op jit(solution)/shard_map/ppermute | solution.py:309
  20.5 1.9 %collective-permute-start = (bf16[1024,128]{1,0:T(8,128)(2,1)S(1)}, bf16[1024,128]{1,0:T(8,128)(2,1)S(1)}, u32[]{:S(2)}, u32[]{:S(2)}) collective-permute-start(bf16[1024,128]{1,0:T(8,128)(2,1)S(1)} %get-tuple-element.46), channel_id=1, source_target_pairs={{0,8},{8,16},{16,24},{24,28},{28,20},{20,12},{12,4},{4,0},{1,9},{9... | collective-permute-start | bytes 786440 | tf_op jit(solution)/shard_map/ppermute | solution.py:309
  22.4 1.6 %collective-permute-start.2 = (bf16[1024,128]{1,0:T(8,128)(2,1)S(1)}, bf16[1024,128]{1,0:T(8,128)(2,1)}, u32[]{:S(2)}, u32[]{:S(2)}) collective-permute-start(bf16[1024,128]{1,0:T(8,128)(2,1)S(1)} %get-tuple-element.45), channel_id=1, source_target_pairs={{0,8},{8,16},{16,24},{24,28},{28,20},{20,12},{12,4},{4,0},{1,9},{9... | collective-permute-start | bytes 786440 | tf_op jit(solution)/shard_map/ppermute | solution.py:309
  24.6 6.0 %collective-permute-done.9.refs_3_ = bf16[2048,128]{1,0:T(8,128)(2,1)} collective-permute-done((bf16[2048,128]{1,0:T(8,128)(2,1)S(1)}, bf16[2048,128]{1,0:T(8,128)(2,1)}, u32[]{:S(2)}, u32[]{:S(2)}) %collective-permute-start.9) | collective-permute-done | bytes 524320 | tf_op jit(solution)/shard_map/ppermute | solution.py:309
  31.2 1.8 %collective-permute-start.13 = (bf16[2048,128]{1,0:T(8,128)(2,1)}, bf16[2048,128]{1,0:T(8,128)(2,1)S(1)}, u32[]{:S(2)}, u32[]{:S(2)}) collective-permute-start(bf16[2048,128]{1,0:T(8,128)(2,1)} %collective-permute-done.12.refs_2_), channel_id=1, source_target_pairs={{0,8},{8,16},{16,24},{24,28},{28,20},{20,12},{12,4},{4,0},{1,9},{9... | collective-permute-start | bytes 1572872 | tf_op jit(solution)/shard_map/ppermute | solution.py:309
  33.0 8.8 %collective-permute-done.6.refs_1_ = bf16[2048,128]{1,0:T(8,128)(2,1)} collective-permute-done((bf16[2048,128]{1,0:T(8,128)(2,1)S(1)}, bf16[2048,128]{1,0:T(8,128)(2,1)}, u32[]{:S(2)}, u32[]{:S(2)}) %collective-permute-start.6) | collective-permute-done | bytes 524320 | tf_op jit(solution)/shard_map/ppermute | solution.py:309
  41.8 2.1 %collective-permute-start.1 = (bf16[1024,128]{1,0:T(8,128)(2,1)S(1)}, bf16[1024,128]{1,0:T(8,128)(2,1)S(1)}, u32[]{:S(2)}, u32[]{:S(2)}) collective-permute-start(bf16[1024,128]{1,0:T(8,128)(2,1)S(1)} %collective-permute-done.refs_1_), channel_id=1, source_target_pairs={{0,8},{8,16},{16,24},{24,28},{28,20},{20,12},{12,4},{4,0},{1,9},{9... | collective-permute-start | bytes 786440 | tf_op jit(solution)/shard_map/ppermute | solution.py:309
  43.9 1.6 %collective-permute-start.3 = (bf16[1024,128]{1,0:T(8,128)(2,1)}, bf16[1024,128]{1,0:T(8,128)(2,1)S(1)}, u32[]{:S(2)}, u32[]{:S(2)}) collective-permute-start(bf16[1024,128]{1,0:T(8,128)(2,1)} %collective-permute-done.2.refs_2_), channel_id=1, source_target_pairs={{0,8},{8,16},{16,24},{24,28},{28,20},{20,12},{12,4},{4,0},{1,9},{9... | collective-permute-start | bytes 786440 | tf_op jit(solution)/shard_map/ppermute | solution.py:309
  45.9 5.7 %densify.3 = (bf16[1,2048,1024]{2,1,0:T(8,128)(2,1)S(1)}, bf16[2,2048,1024]{2,1,0:T(8,128)(2,1)S(1)}) custom-call(s32[1024]{0:T(1024)S(1)} %select_reduce_fusion.table, bf16[640,128,128]{2,1,0:T(8,128)(2,1)} %tiles.3), custom_call_target="tpu_custom_call" | custom-call | bytes 12582912 | tf_op jit(solution)/shard_map/densify/pallas_call | solution.py:86
  51.6 3.3 %copy-done.5 = bf16[2,2048,1024]{2,1,0:T(8,128)(2,1)} copy-done((bf16[2,2048,1024]{2,1,0:T(8,128)(2,1)}, bf16[2,2048,1024]{2,1,0:T(8,128)(2,1)S(1)}, u32[]{:S(2)}) %copy-start.5) | copy-done | bytes 8388632
  54.9 2.0 %copy-done.8 = bf16[1,2048,1024]{2,1,0:T(8,128)(2,1)} copy-done((bf16[1,2048,1024]{2,1,0:T(8,128)(2,1)}, bf16[1,2048,1024]{2,1,0:T(8,128)(2,1)S(1)}, u32[]{:S(2)}) %copy-start.8) | copy-done | bytes 4194328
  56.9 8.8 %densify.2 = (bf16[2,2048,1024]{2,1,0:T(8,128)(2,1)S(1)}, bf16[2,2048,1024]{2,1,0:T(8,128)(2,1)S(1)}, bf16[1,2048,1024]{2,1,0:T(8,128)(2,1)S(1)}) custom-call(s32[1024]{0:T(1024)S(1)} %select_reduce_fusion.table, bf16[640,128,128]{2,1,0:T(8,128)(2,1)} %tiles.3), custom_call_target="tpu_custom_call" | custom-call | bytes 20971520 | tf_op jit(solution)/shard_map/densify/pallas_call | solution.py:86
  65.7 3.3 %copy-done = bf16[2,2048,1024]{2,1,0:T(8,128)(2,1)} copy-done((bf16[2,2048,1024]{2,1,0:T(8,128)(2,1)}, bf16[2,2048,1024]{2,1,0:T(8,128)(2,1)S(1)}, u32[]{:S(2)}) %copy-start) | copy-done | bytes 8388632
  69.0 3.3 %copy-done.1 = bf16[2,2048,1024]{2,1,0:T(8,128)(2,1)} copy-done((bf16[2,2048,1024]{2,1,0:T(8,128)(2,1)}, bf16[2,2048,1024]{2,1,0:T(8,128)(2,1)S(1)}, u32[]{:S(2)}) %copy-start.1) | copy-done | bytes 8388632
  72.2 2.1 %copy-done.3 = bf16[1,2048,1024]{2,1,0:T(8,128)(2,1)} copy-done((bf16[1,2048,1024]{2,1,0:T(8,128)(2,1)}, bf16[1,2048,1024]{2,1,0:T(8,128)(2,1)S(1)}, u32[]{:S(2)}) %copy-start.3) | copy-done | bytes 4194328
  74.4 2.2 %copy-done.9 = bf16[1,2048,1024]{2,1,0:T(8,128)(2,1)S(1)} copy-done((bf16[1,2048,1024]{2,1,0:T(8,128)(2,1)S(1)}, bf16[1,2048,1024]{2,1,0:T(8,128)(2,1)}, u32[]{:S(2)}) %copy-start.9) | copy-done | bytes 4194328
  76.6 2.0 %aggregate.6 = (f32[2048,128]{1,0:T(8,128)S(1)}, f32[2048,128]{1,0:T(8,128)S(1)}) custom-call(s32[512]{0:T(512)S(1)} %reshape.9.need, bf16[2048,128]{1,0:T(8,128)(2,1)S(1)} %get-tuple-element.43.refs_0_, bf16[2048,128]{1,0:T(8,128)(2,1)S(1)} %get-tuple-element.44.refs_1_, bf16[1,2048,1024]{2,1,0:T(8,128)(2,1)S(1)} %copy-done.9), custom_call_target="tpu_custom_call" | custom-call | flops 1073741824 | bytes 4194304 | tf_op jit(solution)/shard_map/aggregate/pallas_call | solution.py:206
  80.8 3.4 %copy-done.6 = bf16[2,2048,1024]{2,1,0:T(8,128)(2,1)S(1)} copy-done((bf16[2,2048,1024]{2,1,0:T(8,128)(2,1)S(1)}, bf16[2,2048,1024]{2,1,0:T(8,128)(2,1)}, u32[]{:S(2)}) %copy-start.6) | copy-done | bytes 8388632
  86.3 4.1 %aggregate.7 = (f32[2048,128]{1,0:T(8,128)S(1)}, f32[2048,128]{1,0:T(8,128)S(1)}) custom-call(s32[512]{0:T(512)S(1)} %reshape.9.need, bf16[2048,128]{1,0:T(8,128)(2,1)S(1)} %copy-done.11, bf16[1024,128]{1,0:T(8,128)(2,1)S(1)} %collective-permute-done.refs_1_, bf16[1024,128]{1,0:T(8,128)(2,1)} %collective-permute-done.2.refs_2_, ...), custom_call_target="tpu_custom_call" | custom-call | flops 2147483648 | bytes 8388608 | tf_op jit(solution)/shard_map/aggregate/pallas_call | solution.py:206
  95.1 5.0 %aggregate.8 = (f32[2048,128]{1,0:T(8,128)S(1)}, f32[2048,128]{1,0:T(8,128)S(1)}) custom-call(s32[512]{0:T(512)S(1)} %reshape.9.need, bf16[2048,128]{1,0:T(8,128)(2,1)S(1)} %collective-permute-done.10.refs_0_, bf16[2048,128]{1,0:T(8,128)(2,1)} %collective-permute-done.6.refs_1_, bf16[2048,128]{1,0:T(8,128)(2,1)} %collective-permute-done.12.refs_2_, ...), custom_call_target="tpu_custom_call" | custom-call | flops 2147483648 | bytes 12582912 | tf_op jit(solution)/shard_map/aggregate/pallas_call | solution.py:206
  100.1 3.4 %aggregate.9.refs_4_ = f32[2048,128]{1,0:T(8,128)S(1)} custom-call(s32[512]{0:T(512)S(1)} %reshape.9.need, bf16[1024,128]{1,0:T(8,128)(2,1)S(1)} %collective-permute-done.1.refs_0_, bf16[1024,128]{1,0:T(8,128)(2,1)S(1)} %collective-permute-done.3.refs_1_, bf16[2048,128]{1,0:T(8,128)(2,1)S(1)} %collective-permute-done.7.refs_0_.refs_2_, ...), custom_call_target="tpu_custom_call" | custom-call | flops 1073741824 | bytes 8388608 | tf_op jit(solution)/shard_map/aggregate/pallas_call | solution.py:206
  103.5 3.1 %aggregate.11 = (bf16[512,128]{1,0:T(8,128)(2,1)S(1)}, bf16[512,128]{1,0:T(8,128)(2,1)S(1)}, bf16[512,128]{1,0:T(8,128)(2,1)S(1)}, bf16[512,128]{1,0:T(8,128)(2,1)S(1)}) custom-call(s32[512]{0:T(512)S(1)} %reshape.9.need, bf16[1024,128]{1,0:T(8,128)(2,1)S(1)} %collective-permute-done.16.refs_0_, bf16[1024,128]{1,0:T(8,128)(2,1)S(1)} %collective-permute-done.17.refs_1_, ...), custom_call_target="tpu_custom_call" | custom-call | flops 1073741824 | bytes 8388608 | tf_op jit(solution)/shard_map/aggregate/pallas_call | solution.py:206
  106.6 1.6 %collective-permute-start.20 = (bf16[512,128]{1,0:T(8,128)(2,1)S(1)}, bf16[512,128]{1,0:T(8,128)(2,1)S(1)}, u32[]{:S(2)}, u32[]{:S(2)}) collective-permute-start(bf16[512,128]{1,0:T(8,128)(2,1)S(1)} %get-tuple-element.41), channel_id=1, source_target_pairs={{0,2},{1,3},{2,0},{3,1},{4,6},{5,7},{6,4},{7,5},{8,10},{9,11},{10,... | collective-permute-start | bytes 393224 | tf_op jit(solution)/shard_map/ppermute | solution.py:377
  108.5 3.1 %aggregate.10 = (bf16[512,128]{1,0:T(8,128)(2,1)S(1)}, bf16[512,128]{1,0:T(8,128)(2,1)S(1)}, bf16[512,128]{1,0:T(8,128)(2,1)S(1)}, bf16[512,128]{1,0:T(8,128)(2,1)S(1)}) custom-call(s32[512]{0:T(512)S(1)} %reshape.9.need, bf16[1024,128]{1,0:T(8,128)(2,1)S(1)} %collective-permute-done.4.refs_0_, bf16[1024,128]{1,0:T(8,128)(2,1)S(1)} %collective-permute-done.8.refs_1_, ...), custom_call_target="tpu_custom_call" | custom-call | flops 1073741824 | bytes 8388608 | tf_op jit(solution)/shard_map/aggregate/pallas_call | solution.py:206
  112.0 1.6 %collective-permute-start.14 = (bf16[512,128]{1,0:T(8,128)(2,1)S(1)}, bf16[512,128]{1,0:T(8,128)(2,1)S(1)}, u32[]{:S(2)}, u32[]{:S(2)}) collective-permute-start(bf16[512,128]{1,0:T(8,128)(2,1)S(1)} %get-tuple-element.34), channel_id=1, source_target_pairs={{0,2},{1,3},{2,0},{3,1},{4,6},{5,7},{6,4},{7,5},{8,10},{9,11},{10,... | collective-permute-start | bytes 393224 | tf_op jit(solution)/shard_map/ppermute | solution.py:377
  114.9 2.0 %product.2.refs_2_ = f32[512,1024]{1,0:T(8,128)S(1)} custom-call(bf16[1024,1024]{1,0:T(8,128)(2,1)S(1)} %copy-done.7, bf16[512,128]{1,0:T(8,128)(2,1)S(1)} %get-tuple-element.37.refs_0_, bf16[512,128]{1,0:T(8,128)(2,1)S(1)} %get-tuple-element.38.refs_1_, bf16[512,128]{1,0:T(8,128)(2,1)S(1)} %collective-permute-done.18.refs_2_, ...), custom_call_target="tpu_custom_call" | custom-call | flops 805306368 | bytes 4194304 | tf_op jit(solution)/shard_map/product/pallas_call | solution.py:268
  116.9 1.8 %collective-permute-done.14.refs_0_ = bf16[512,128]{1,0:T(8,128)(2,1)S(1)} collective-permute-done((bf16[512,128]{1,0:T(8,128)(2,1)S(1)}, bf16[512,128]{1,0:T(8,128)(2,1)S(1)}, u32[]{:S(2)}, u32[]{:S(2)}) %collective-permute-start.14) | collective-permute-done | bytes 131104 | tf_op jit(solution)/shard_map/ppermute | solution.py:377
  118.7 1.7 %collective-permute-done.15.refs_1_ = bf16[512,128]{1,0:T(8,128)(2,1)S(1)} collective-permute-done((bf16[512,128]{1,0:T(8,128)(2,1)S(1)}, bf16[512,128]{1,0:T(8,128)(2,1)S(1)}, u32[]{:S(2)}, u32[]{:S(2)}) %collective-permute-start.15) | collective-permute-done | bytes 131104 | tf_op jit(solution)/shard_map/ppermute | solution.py:377
  120.4 2.5 %product.3 = bf16[512,1024]{1,0:T(8,128)(2,1)} custom-call(bf16[1024,1024]{1,0:T(8,128)(2,1)S(1)} %copy-done.7, bf16[512,128]{1,0:T(8,128)(2,1)S(1)} %collective-permute-done.14.refs_0_, bf16[512,128]{1,0:T(8,128)(2,1)S(1)} %collective-permute-done.15.refs_1_, f32[512,1024]{1,0:T(8,128)S(1)} %product.2.refs_2_), custom_call_target="tpu_custom_call" | custom-call | flops 268435456 | bytes 4194304 | tf_op jit(solution)/shard_map/product/pallas_call | solution.py:268
  (72 shorter events, 16.0 us)
Async XLA Ops:
  0.0 41.8 %copy-start.16 = (s32[640]{0:T(1024)S(1)}, s32[640]{0:T(1024)}, u32[]{:S(2)}) copy-start(s32[640]{0:T(1024)} %param.10) | copy-start | bytes 7684
  0.0 41.8 %copy-start.17 = (s32[640]{0:T(1024)S(1)}, s32[640]{0:T(1024)}, u32[]{:S(2)}) copy-start(s32[640]{0:T(1024)} %param.11) | copy-start | bytes 7684
  0.0 41.8 %copy-start.15 = (s32[640]{0:T(1024)S(1)}, s32[640]{0:T(1024)}, u32[]{:S(2)}) copy-start(s32[640]{0:T(1024)} %param.12) | copy-start | bytes 7684
  1.3 15.0 %collective-permute-start.11 = (bf16[2048,128]{1,0:T(8,128)(2,1)S(1)}, bf16[2048,128]{1,0:T(8,128)(2,1)S(1)}, u32[]{:S(2)}, u32[]{:S(2)}) collective-permute-start(bf16[2048,128]{1,0:T(8,128)(2,1)S(1)} %get-tuple-element.43.refs_0_), channel_id=1, source_target_pairs={{0,8},{8,16},{16,24},{24,28},{28,20},{20,12},{12,4},{4,0},{1,9},{9... | collective-permute-start | bytes 1572872 | tf_op jit(solution)/shard_map/ppermute | solution.py:309
  4.4 14.8 %collective-permute-start.5 = (bf16[2048,128]{1,0:T(8,128)(2,1)S(1)}, bf16[2048,128]{1,0:T(8,128)(2,1)S(1)}, u32[]{:S(2)}, u32[]{:S(2)}) collective-permute-start(bf16[2048,128]{1,0:T(8,128)(2,1)S(1)} %get-tuple-element.44.refs_1_), channel_id=1, source_target_pairs={{0,4},{8,0},{16,8},{24,16},{28,24},{20,28},{12,20},{4,12},{1,5},{9... | collective-permute-start | bytes 1572872 | tf_op jit(solution)/shard_map/ppermute | solution.py:309
  4.4 26.1 %collective-permute-start.9 = (bf16[2048,128]{1,0:T(8,128)(2,1)S(1)}, bf16[2048,128]{1,0:T(8,128)(2,1)}, u32[]{:S(2)}, u32[]{:S(2)}) collective-permute-start(bf16[2048,128]{1,0:T(8,128)(2,1)S(1)} %get-tuple-element.43.refs_0_), channel_id=1, source_target_pairs={{0,4},{8,0},{16,8},{24,16},{28,24},{20,28},{12,20},{4,12},{1,5},{9... | collective-permute-start | bytes 1572872 | tf_op jit(solution)/shard_map/ppermute | solution.py:309
  16.3 14.3 %copy-start.10 = (bf16[2048,128]{1,0:T(8,128)(2,1)}, bf16[2048,128]{1,0:T(8,128)(2,1)S(1)}, u32[]{:S(2)}) copy-start(bf16[2048,128]{1,0:T(8,128)(2,1)S(1)} %collective-permute-done.11.refs_0_) | copy-start | bytes 1572868
  16.3 14.9 %collective-permute-start.12 = (bf16[2048,128]{1,0:T(8,128)(2,1)S(1)}, bf16[2048,128]{1,0:T(8,128)(2,1)}, u32[]{:S(2)}, u32[]{:S(2)}) collective-permute-start(bf16[2048,128]{1,0:T(8,128)(2,1)S(1)} %collective-permute-done.11.refs_0_), channel_id=1, source_target_pairs={{0,8},{8,16},{16,24},{24,28},{28,20},{20,12},{12,4},{4,0},{1,9},{9... | collective-permute-start | bytes 1572872 | tf_op jit(solution)/shard_map/ppermute | solution.py:309
  19.2 13.8 %copy-start.12 = (bf16[2048,128]{1,0:T(8,128)(2,1)}, bf16[2048,128]{1,0:T(8,128)(2,1)S(1)}, u32[]{:S(2)}) copy-start(bf16[2048,128]{1,0:T(8,128)(2,1)S(1)} %collective-permute-done.5.refs_4_) | copy-start | bytes 1572868
  19.2 22.6 %collective-permute-start.6 = (bf16[2048,128]{1,0:T(8,128)(2,1)S(1)}, bf16[2048,128]{1,0:T(8,128)(2,1)}, u32[]{:S(2)}, u32[]{:S(2)}) collective-permute-start(bf16[2048,128]{1,0:T(8,128)(2,1)S(1)} %collective-permute-done.5.refs_4_), channel_id=1, source_target_pairs={{0,4},{8,0},{16,8},{24,16},{28,24},{20,28},{12,20},{4,12},{1,5},{9... | collective-permute-start | bytes 1572872 | tf_op jit(solution)/shard_map/ppermute | solution.py:309
  20.5 21.3 %collective-permute-start = (bf16[1024,128]{1,0:T(8,128)(2,1)S(1)}, bf16[1024,128]{1,0:T(8,128)(2,1)S(1)}, u32[]{:S(2)}, u32[]{:S(2)}) collective-permute-start(bf16[1024,128]{1,0:T(8,128)(2,1)S(1)} %get-tuple-element.46), channel_id=1, source_target_pairs={{0,8},{8,16},{16,24},{24,28},{28,20},{20,12},{12,4},{4,0},{1,9},{9... | collective-permute-start | bytes 786440 | tf_op jit(solution)/shard_map/ppermute | solution.py:309
  22.4 21.5 %collective-permute-start.2 = (bf16[1024,128]{1,0:T(8,128)(2,1)S(1)}, bf16[1024,128]{1,0:T(8,128)(2,1)}, u32[]{:S(2)}, u32[]{:S(2)}) collective-permute-start(bf16[1024,128]{1,0:T(8,128)(2,1)S(1)} %get-tuple-element.45), channel_id=1, source_target_pairs={{0,8},{8,16},{16,24},{24,28},{28,20},{20,12},{12,4},{4,0},{1,9},{9... | collective-permute-start | bytes 786440 | tf_op jit(solution)/shard_map/ppermute | solution.py:309
  30.6 59.8 %collective-permute-start.10 = (bf16[2048,128]{1,0:T(8,128)(2,1)}, bf16[2048,128]{1,0:T(8,128)(2,1)S(1)}, u32[]{:S(2)}, u32[]{:S(2)}) collective-permute-start(bf16[2048,128]{1,0:T(8,128)(2,1)} %collective-permute-done.9.refs_3_), channel_id=1, source_target_pairs={{0,4},{8,0},{16,8},{24,16},{28,24},{20,28},{12,20},{4,12},{1,5},{9... | collective-permute-start | bytes 1572872 | tf_op jit(solution)/shard_map/ppermute | solution.py:309
  31.2 60.5 %collective-permute-start.13 = (bf16[2048,128]{1,0:T(8,128)(2,1)}, bf16[2048,128]{1,0:T(8,128)(2,1)S(1)}, u32[]{:S(2)}, u32[]{:S(2)}) collective-permute-start(bf16[2048,128]{1,0:T(8,128)(2,1)} %collective-permute-done.12.refs_2_), channel_id=1, source_target_pairs={{0,8},{8,16},{16,24},{24,28},{28,20},{20,12},{12,4},{4,0},{1,9},{9... | collective-permute-start | bytes 1572872 | tf_op jit(solution)/shard_map/ppermute | solution.py:309
  41.8 52.0 %collective-permute-start.7 = (bf16[2048,128]{1,0:T(8,128)(2,1)}, bf16[2048,128]{1,0:T(8,128)(2,1)S(1)}, u32[]{:S(2)}, u32[]{:S(2)}) collective-permute-start(bf16[2048,128]{1,0:T(8,128)(2,1)} %collective-permute-done.6.refs_1_), channel_id=1, source_target_pairs={{0,4},{8,0},{16,8},{24,16},{28,24},{20,28},{12,20},{4,12},{1,5},{9... | collective-permute-start | bytes 1572872 | tf_op jit(solution)/shard_map/ppermute | solution.py:309
  41.8 36.7 %collective-permute-start.1 = (bf16[1024,128]{1,0:T(8,128)(2,1)S(1)}, bf16[1024,128]{1,0:T(8,128)(2,1)S(1)}, u32[]{:S(2)}, u32[]{:S(2)}) collective-permute-start(bf16[1024,128]{1,0:T(8,128)(2,1)S(1)} %collective-permute-done.refs_1_), channel_id=1, source_target_pairs={{0,8},{8,16},{16,24},{24,28},{28,20},{20,12},{12,4},{4,0},{1,9},{9... | collective-permute-start | bytes 786440 | tf_op jit(solution)/shard_map/ppermute | solution.py:309
  43.9 34.7 %collective-permute-start.3 = (bf16[1024,128]{1,0:T(8,128)(2,1)}, bf16[1024,128]{1,0:T(8,128)(2,1)S(1)}, u32[]{:S(2)}, u32[]{:S(2)}) collective-permute-start(bf16[1024,128]{1,0:T(8,128)(2,1)} %collective-permute-done.2.refs_2_), channel_id=1, source_target_pairs={{0,8},{8,16},{16,24},{24,28},{28,20},{20,12},{12,4},{4,0},{1,9},{9... | collective-permute-start | bytes 786440 | tf_op jit(solution)/shard_map/ppermute | solution.py:309
  56.9 17.4 %copy-start.14 = (s32[8,8,8]{2,1,0:T(8,128)S(1)}, s32[8,8,8]{2,1,0:T(8,128)}, u32[]{:S(2)}) copy-start(s32[8,8,8]{2,1,0:T(8,128)} %param.14) | copy-start | bytes 6148
  76.6 18.5 %copy-start.2 = (bf16[2,2048,1024]{2,1,0:T(8,128)(2,1)S(1)}, bf16[2,2048,1024]{2,1,0:T(8,128)(2,1)}, u32[]{:S(2)}) copy-start(bf16[2,2048,1024]{2,1,0:T(8,128)(2,1)} %copy-done.1) | copy-start | bytes 25165828
  78.6 16.5 %slice-start = ((s8[8388608]{0:T(1024)(128)(4,1)}), s8[4194304]{0:T(1024)(128)(4,1)S(1)}, s32[]{:S(2)}) async-start(s8[8388608]{0:T(1024)(128)(4,1)} %bitcast.2), calls=%async_computation | async-start | bytes 8388608
  79.3 29.2 %collective-permute-start.4 = (bf16[1024,128]{1,0:T(8,128)(2,1)S(1)}, bf16[1024,128]{1,0:T(8,128)(2,1)S(1)}, u32[]{:S(2)}, u32[]{:S(2)}) collective-permute-start(bf16[1024,128]{1,0:T(8,128)(2,1)S(1)} %pick.4), channel_id=1, source_target_pairs={{0,8},{8,16},{16,24},{24,28},{28,20},{20,12},{12,4},{4,0},{1,9},{9... | collective-permute-start | bytes 786440 | tf_op jit(solution)/shard_map/ppermute | solution.py:309
  86.3 8.8 %slice-start.1 = ((s8[8388608]{0:T(1024)(128)(4,1)}), s8[4194304]{0:T(1024)(128)(4,1)S(1)}, s32[]{:S(2)}) async-start(s8[8388608]{0:T(1024)(128)(4,1)} %bitcast.2), calls=%async_computation.1 | async-start | bytes 8388608
  91.0 12.4 %collective-permute-start.16 = (bf16[1024,128]{1,0:T(8,128)(2,1)S(1)}, bf16[1024,128]{1,0:T(8,128)(2,1)S(1)}, u32[]{:S(2)}, u32[]{:S(2)}) collective-permute-start(bf16[1024,128]{1,0:T(8,128)(2,1)S(1)} %pick.6), channel_id=1, source_target_pairs={{0,4},{8,0},{16,8},{24,16},{28,24},{20,28},{12,20},{4,12},{1,5},{9... | collective-permute-start | bytes 786440 | tf_op jit(solution)/shard_map/ppermute | solution.py:309
  92.3 11.2 %collective-permute-start.17 = (bf16[1024,128]{1,0:T(8,128)(2,1)S(1)}, bf16[1024,128]{1,0:T(8,128)(2,1)S(1)}, u32[]{:S(2)}, u32[]{:S(2)}) collective-permute-start(bf16[1024,128]{1,0:T(8,128)(2,1)S(1)} %pick.7), channel_id=1, source_target_pairs={{0,8},{8,16},{16,24},{24,28},{28,20},{20,12},{12,4},{4,0},{1,9},{9... | collective-permute-start | bytes 786440 | tf_op jit(solution)/shard_map/ppermute | solution.py:309
  94.4 14.1 %collective-permute-start.8 = (bf16[1024,128]{1,0:T(8,128)(2,1)S(1)}, bf16[1024,128]{1,0:T(8,128)(2,1)S(1)}, u32[]{:S(2)}, u32[]{:S(2)}) collective-permute-start(bf16[1024,128]{1,0:T(8,128)(2,1)S(1)} %pick.5), channel_id=1, source_target_pairs={{0,4},{8,0},{16,8},{24,16},{28,24},{20,28},{12,20},{4,12},{1,5},{9... | collective-permute-start | bytes 786440 | tf_op jit(solution)/shard_map/ppermute | solution.py:309
  106.6 7.0 %collective-permute-start.18 = (bf16[512,128]{1,0:T(8,128)(2,1)S(1)}, bf16[512,128]{1,0:T(8,128)(2,1)S(1)}, u32[]{:S(2)}, u32[]{:S(2)}) collective-permute-start(bf16[512,128]{1,0:T(8,128)(2,1)S(1)} %get-tuple-element.39), channel_id=1, source_target_pairs={{0,1},{1,0},{2,3},{3,2},{4,5},{5,4},{6,7},{7,6},{8,9},{9,8},{10,11... | collective-permute-start | bytes 393224 | tf_op jit(solution)/shard_map/ppermute | solution.py:377
  106.6 6.9 %collective-permute-start.20 = (bf16[512,128]{1,0:T(8,128)(2,1)S(1)}, bf16[512,128]{1,0:T(8,128)(2,1)S(1)}, u32[]{:S(2)}, u32[]{:S(2)}) collective-permute-start(bf16[512,128]{1,0:T(8,128)(2,1)S(1)} %get-tuple-element.41), channel_id=1, source_target_pairs={{0,2},{1,3},{2,0},{3,1},{4,6},{5,7},{6,4},{7,5},{8,10},{9,11},{10,... | collective-permute-start | bytes 393224 | tf_op jit(solution)/shard_map/ppermute | solution.py:377
  108.2 6.7 %copy-start.7 = (bf16[1024,1024]{1,0:T(8,128)(2,1)S(1)}, bf16[1024,1024]{1,0:T(8,128)(2,1)}, u32[]{:S(2)}) copy-start(bf16[1024,1024]{1,0:T(8,128)(2,1)} %w.3) | copy-start | bytes 6291460
  108.2 6.7 %collective-permute-start.21 = (bf16[512,128]{1,0:T(8,128)(2,1)S(1)}, bf16[512,128]{1,0:T(8,128)(2,1)S(1)}, u32[]{:S(2)}, u32[]{:S(2)}) collective-permute-start(bf16[512,128]{1,0:T(8,128)(2,1)S(1)} %get-tuple-element.42), channel_id=1, source_target_pairs={{0,3},{1,2},{2,1},{3,0},{4,7},{5,6},{6,5},{7,4},{8,11},{9,10},{10,... | collective-permute-start | bytes 393224 | tf_op jit(solution)/shard_map/ppermute | solution.py:377
  111.6 3.3 %collective-permute-start.19 = (bf16[512,128]{1,0:T(8,128)(2,1)S(1)}, bf16[512,128]{1,0:T(8,128)(2,1)S(1)}, u32[]{:S(2)}, u32[]{:S(2)}) collective-permute-start(bf16[512,128]{1,0:T(8,128)(2,1)S(1)} %get-tuple-element.40), channel_id=1, source_target_pairs={{0,1},{1,0},{2,3},{3,2},{4,5},{5,4},{6,7},{7,6},{8,9},{9,8},{10,11... | collective-permute-start | bytes 393224 | tf_op jit(solution)/shard_map/ppermute | solution.py:377
  112.0 6.7 %collective-permute-start.14 = (bf16[512,128]{1,0:T(8,128)(2,1)S(1)}, bf16[512,128]{1,0:T(8,128)(2,1)S(1)}, u32[]{:S(2)}, u32[]{:S(2)}) collective-permute-start(bf16[512,128]{1,0:T(8,128)(2,1)S(1)} %get-tuple-element.34), channel_id=1, source_target_pairs={{0,2},{1,3},{2,0},{3,1},{4,6},{5,7},{6,4},{7,5},{8,10},{9,11},{10,... | collective-permute-start | bytes 393224 | tf_op jit(solution)/shard_map/ppermute | solution.py:377
  113.6 6.9 %collective-permute-start.15 = (bf16[512,128]{1,0:T(8,128)(2,1)S(1)}, bf16[512,128]{1,0:T(8,128)(2,1)S(1)}, u32[]{:S(2)}, u32[]{:S(2)}) collective-permute-start(bf16[512,128]{1,0:T(8,128)(2,1)S(1)} %get-tuple-element.35), channel_id=1, source_target_pairs={{0,3},{1,2},{2,1},{3,0},{4,7},{5,6},{6,5},{7,4},{8,11},{9,10},{10,... | collective-permute-start | bytes 393224 | tf_op jit(solution)/shard_map/ppermute | solution.py:377
  (10 other events, 25.0 us)

commit v3 on v2

--- a/solution.py
+++ b/solution.py
@@ -128,14 +128,12 @@
                 put(k, chunk[pl.ds(row, TILE), :])
 
 
-def aggregate_kernel(plan, groups, n_sources, n_dense, n_totals, widths, first, blocks, need, *refs):
+def aggregate_kernel(plan, groups, n_sources, n_dense, n_totals, widths, first, need, *refs):
     sources, refs = refs[:n_sources], refs[n_sources:]
     denses, refs = refs[:n_dense], refs[n_dense:]
     if not first:
         start_totals, refs = refs[:n_totals], refs[n_totals:]
-    n_outs = n_totals * max(1, blocks)
-    outs, (streamed, feats, *work, sem) = refs[:n_outs], refs[n_outs:]
-    totals = work if blocks else outs
+    totals, (streamed, feats, sem) = refs[:n_totals], refs[n_totals:]
     starts = [sum(widths[:t]) for t in range(n_totals)]
     fresh = [first] * n_totals
 
@@ -168,13 +166,66 @@
     for part in range(n_totals):
         if not first and plan_first(plan, part) is None:
             totals[part][...] = start_totals[part][...]
-    if blocks:
-        own = lax.axis_index("feat")
-        size = ROWS // blocks
-        for part in range(n_totals):
-            for m in range(blocks):
-                rows = pl.ds(pl.multiple_of((own ^ m) * size, size), size)
-                outs[part * blocks + m][...] = totals[part][rows, :].astype(jnp.bfloat16)
+
+
+def finish_kernel(plan, groups, n_sources, n_dense, blocks, pairs, need, *refs):
+    sources, refs = refs[:n_sources], refs[n_sources:]
+    denses, refs = refs[:n_dense], refs[n_dense:]
+    start_total, refs = refs[0], refs[1:]
+    outs, (streamed, feats, total, sem) = refs[: 2 * len(pairs)], refs[2 * len(pairs) :]
+    own = lax.axis_index("feat")
+    size = ROWS // blocks
+    for e, (operand, index, resident, offset, pieces) in enumerate(plan):
+        ((part, chunks, whole),) = pieces
+
+        def put(k, value):
+            feats[e, pl.ds(k * TILE, TILE), :] = value
+
+        gather_feats(need, groups, 0, offset, [sources[i] for i in chunks], whole, put)
+    for i, pair in enumerate(pairs):
+        rows = pl.ds(pl.multiple_of((lax.div(own, 2) ^ pair) * 2 * size, 2 * size), 2 * size)
+        total[...] = start_total[rows, :]
+        for e, (operand, index, resident, offset, pieces) in enumerate(plan):
+            if resident:
+                lhs = denses[operand][index, rows, :]
+            else:
+                copy = pltpu.make_async_copy(denses[operand].at[index, rows, :], streamed, sem)
+                copy.start()
+                copy.wait()
+                lhs = streamed[...]
+            total[...] += jnp.dot(lhs, feats[e], preferred_element_type=jnp.float32)
+        for low in range(2):
+            block = pl.ds(pl.multiple_of((lax.rem(own, 2) ^ low) * size, size), size)
+            outs[2 * i + low][...] = total[block, :].astype(jnp.bfloat16)
+
+
+def finish(plan, groups, need, sources, denses, start_total, blocks, pairs):
+    width = start_total.shape[1]
+    vmem = pl.BlockSpec(memory_space=pltpu.VMEM)
+    spaces = [None] * len(denses)
+    for operand, index, resident, offset, pieces in plan:
+        spaces[operand] = vmem if resident else pl.BlockSpec(memory_space=pl.ANY)
+    streams = any(not entry[2] for entry in plan)
+    rows = 2 * ROWS // blocks
+    return pl.pallas_call(
+        functools.partial(finish_kernel, plan, groups, len(sources), len(denses), blocks, pairs),
+        out_shape=[jax.ShapeDtypeStruct((ROWS // blocks, width), jnp.bfloat16)] * (2 * len(pairs)),
+        in_specs=[pl.BlockSpec(memory_space=pltpu.SMEM)] + [vmem] * len(sources) + spaces + [vmem],
+        out_specs=[vmem] * (2 * len(pairs)),
+        scratch_shapes=[
+            pltpu.VMEM((rows, DEPTH) if streams else (8, TILE), jnp.bfloat16),
+            pltpu.VMEM((len(plan), DEPTH, width), jnp.bfloat16),
+            pltpu.VMEM((rows, width), jnp.float32),
+            pltpu.SemaphoreType.DMA,
+        ],
+        compiler_params=pltpu.CompilerParams(vmem_limit_bytes=STREAM_LIMIT if streams else RESIDENT_LIMIT),
+        cost_estimate=pl.CostEstimate(
+            flops=2 * len(plan) * len(pairs) * rows * DEPTH * width,
+            bytes_accessed=2 * len(plan) * len(pairs) * rows * DEPTH,
+            transcendentals=0,
+        ),
+        name="finish",
+    )(need, *sources, *denses, start_total)
 
 
 def plan_first(plan, part):
@@ -184,7 +235,7 @@
     return None
 
 
-def aggregate(plan, groups, need, sources, denses, totals, widths, blocks=0):
+def aggregate(plan, groups, need, sources, denses, totals, widths):
     first = totals is None
     n_totals = len(widths)
     smem = pl.BlockSpec(memory_space=pltpu.SMEM)
@@ -197,15 +248,11 @@
         pltpu.VMEM((ROWS, DEPTH) if streams else (8, TILE), jnp.bfloat16),
         pltpu.VMEM((DEPTH, sum(widths)), jnp.bfloat16),
     ]
-    if blocks:
-        out_shape = [jax.ShapeDtypeStruct((ROWS // blocks, w), jnp.bfloat16) for w in widths for _ in range(blocks)]
-        scratch += [pltpu.VMEM((ROWS, w), jnp.float32) for w in widths]
-    else:
-        out_shape = [jax.ShapeDtypeStruct((ROWS, w), jnp.float32) for w in widths]
+    out_shape = [jax.ShapeDtypeStruct((ROWS, w), jnp.float32) for w in widths]
     flops = sum(2 * ROWS * DEPTH * sum(widths[p[0]] for p in entry[4]) for entry in plan)
     return pl.pallas_call(
         functools.partial(
-            aggregate_kernel, plan, groups, len(sources), len(denses), n_totals, widths, first, blocks
+            aggregate_kernel, plan, groups, len(sources), len(denses), n_totals, widths, first
         ),
         out_shape=out_shape,
         in_specs=[smem] + [vmem] * len(sources) + spaces + ([] if first else [vmem] * n_totals),
@@ -240,40 +287,53 @@
     )(need, *chunks)
 
 
-def product_kernel(terms, starts, shard, last, w, *refs):
+def product_kernel(terms, starts, shard, first, final, w, *refs):
     parts, refs = refs[:terms], refs[terms:]
+    start_total, refs = (None, refs) if first else (refs[0], refs[1:])
     own = lax.axis_index("feat")
-    total = None if last is None else refs[0][...]
-    out = refs[-1]
-    for i in range(0, terms, 2):
-        pair = range(i, min(i + 2, terms))
-        x = jnp.concatenate([parts[j][...] for j in pair], axis=1)
-        rows = []
-        for j in pair:
-            m, column = starts[j]
-            row = pl.multiple_of((own ^ m) * shard + column, TILE)
-            rows.append(w[pl.ds(row, parts[j].shape[1]), :])
-        term = jnp.dot(x, jnp.concatenate(rows, axis=0), preferred_element_type=jnp.float32)
-        total = term if total is None else total + term
-    out[...] = total if out.dtype == jnp.float32 else jnp.maximum(total, 0.0).astype(out.dtype)
-
-
-def product(operands, starts, shard, w, start_total, dtype):
+    cols = w.shape[1]
+    step = 2 * TILE
+
+    def write(j):
+        return pltpu.make_async_copy(refs[1].at[j], refs[0].at[:, pl.ds(j * step, step)], refs[2].at[j])
+
+    for j in range(cols // step):
+        band = pl.ds(j * step, step)
+        total = None if first else start_total[:, band]
+        for i in range(0, terms, 2):
+            pair = range(i, min(i + 2, terms))
+            x = jnp.concatenate([parts[t][...] for t in pair], axis=1)
+            rows = []
+            for t in pair:
+                m, column = starts[t]
+                row = pl.multiple_of((own ^ m) * shard + column, TILE)
+                rows.append(w[pl.ds(row, parts[t].shape[1]), band])
+            term = jnp.dot(x, jnp.concatenate(rows, axis=0), preferred_element_type=jnp.float32)
+            total = term if total is None else total + term
+        if final:
+            refs[1][j] = jnp.maximum(total, 0.0).astype(jnp.bfloat16)
+            write(j).start()
+        else:
+            refs[0][:, band] = total
+    if final:
+        for j in range(cols // step):
+            write(j).wait()
+
+
+def product(operands, starts, shard, w, start_total, final):
     rows = operands[0].shape[0]
-    depth, cols = w.shape
-    step = 256
+    _, cols = w.shape
+    bands = cols // (2 * TILE)
     vmem = pl.BlockSpec(memory_space=pltpu.VMEM)
-    band = pl.BlockSpec((rows, step), lambda j: (0, j))
     first = start_total is None
+    scratch = [pltpu.VMEM((bands, rows, 2 * TILE), jnp.bfloat16), pltpu.SemaphoreType.DMA((bands,))]
     return pl.pallas_call(
-        functools.partial(product_kernel, len(operands), starts, shard, None if first else 0),
-        grid=(cols // step,),
-        out_shape=jax.ShapeDtypeStruct((rows, cols), dtype),
-        in_specs=[pl.BlockSpec((depth, step), lambda j: (0, j))]
-        + [pl.BlockSpec(x.shape, lambda j: (0, 0)) for x in operands]
-        + ([] if first else [band]),
-        out_specs=band,
-        compiler_params=pltpu.CompilerParams(vmem_limit_bytes=16 * MIB),
+        functools.partial(product_kernel, len(operands), starts, shard, first, final),
+        out_shape=jax.ShapeDtypeStruct((rows, cols), jnp.bfloat16 if final else jnp.float32),
+        in_specs=[vmem] * (1 + len(operands) + (0 if first else 1)),
+        out_specs=pl.BlockSpec(memory_space=pl.ANY) if final else vmem,
+        scratch_shapes=scratch if final else [],
+        compiler_params=pltpu.CompilerParams(vmem_limit_bytes=10 * MIB),
         cost_estimate=pl.CostEstimate(
             flops=2 * rows * cols * sum(x.shape[1] for x in operands), bytes_accessed=8 * rows * cols, transcendentals=0
         ),
@@ -337,7 +397,7 @@
             upto = next((e for e in range(d + 1, far + 1) if e == 2 or is_resident(e) != is_resident(d)), far + 1)
             dense += densify(stages[d:upto], is_resident(d), groups, table, tiles)
 
-    def add(totals, entries, columns, final=0):
+    def add(totals, entries, columns, pairs=None):
         sources, operands, plan = [], [], []
         for way, d, parts in entries:
             if d not in operands:
@@ -351,7 +411,10 @@
             index = stages[d].index(offset) if d < far else 0
             plan.append((operands.index(d), index, is_resident(d), offset, tuple(pieces)))
         sizes = tuple(widths[c] for c in columns)
-        return aggregate(tuple(plan), groups, need, sources, [dense[d] for d in operands], totals, sizes, final)
+        if pairs is not None:
+            arrays = [dense[d] for d in operands]
+            return finish(tuple(plan), groups, need, sources, arrays, totals[0], blocks, pairs)
+        return aggregate(tuple(plan), groups, need, sources, [dense[d] for d in operands], totals, sizes)
 
     every = list(range(cuts))
     totals = add(None, [(1, 0, every)], every)
@@ -363,31 +426,41 @@
         totals = add(totals, early, every)
         rest = add([totals[1]], [(1, d, [1]), (-1, d + 1, [1])], [1])
         ends = [
-            add([totals[0]], [(-1, d + 1, [0]), (1, far, [0])], [0], blocks),
-            add(rest, [(1, d + 1, [1]), (-1, far, [1])], [1], blocks),
+            (totals[0], [(-1, d + 1, [0]), (1, far, [0])]),
+            (rest[0], [(1, d + 1, [1]), (-1, far, [1])]),
         ]
     else:
         totals = add(totals, [(1, d, every), (-1, d, every)], every)
         totals = add(totals, [(1, d + 1, every), (-1, d + 1, every)], every)
-        ends = [add(totals, [(1, far, every)], every, blocks)]
+        ends = [(totals[0], [(1, far, every)])]
+
+    finished = {}
+    for c, (total, entries) in enumerate(ends):
+        for pairs in (tuple(range(1, blocks // 2)), (0,)):
+            for pair, outs in zip(pairs, halves(add([total], entries, [c], pairs) if pairs else [])):
+                finished[c, 2 * pair], finished[c, 2 * pair + 1] = outs
 
     def exchange(c, m):
         if m == 0:
-            return ends[c][0]
-        return lax.ppermute(ends[c][m], "feat", [(f, f ^ m) for f in range(blocks)])
+            return finished[c, 0]
+        return lax.ppermute(finished[c, m], "feat", [(f, f ^ m) for f in range(blocks)])
 
     order = [(c, m) for c in range(cuts) for m in reversed(range(blocks))]
     arrived = {key: exchange(*key) for key in order}
     late = [(last, m) for m in range(2, blocks)]
     soon = [(c, m) for m in range(blocks) for c in range(cuts) if (c, m) not in late]
 
-    def multiply(keys, start_total, dtype):
+    def multiply(keys, start_total, final):
         starts = tuple((m, c * part) for c, m in keys)
-        return product([arrived[key] for key in keys], starts, width, weight, start_total, dtype)
+        return product([arrived[key] for key in keys], starts, width, weight, start_total, final)
 
     if not late:
-        return multiply(soon, None, jnp.bfloat16)
-    return multiply(late, multiply(soon, None, jnp.float32), jnp.bfloat16)
+        return multiply(soon, None, True)
+    return multiply(late, multiply(soon, None, False), True)
+
+
+def halves(outs):
+    return [(outs[i], outs[i + 1]) for i in range(0, len(outs), 2)]
 
 
 def part_count(width):

time: 124 us -> 124 us (level)
    pallas_call x0 -> x4, Pallas kernels: none -> 7.48 us  [finish(): pl.pallas_call(functools.partial(finish_kernel, plan, groups, len(sources...]
    pallas_call x6 -> x4, Pallas kernels: 20.6 us -> 14.4 us  [aggregate(): pl.pallas_call(functools.partial(aggregate_kernel, plan, groups, len(sour...]
    pallas_call x2, Pallas kernels: 4.45 us -> 2.29 us  [product(): pl.pallas_call(functools.partial(product_kernel, len(operands), starts, s...]
  transfers between devices with their start and end apart: 22 -> 22, of which waited for: 8 -> 7; matrix products, arithmetic and copies ran while one was open for 1% -> 1% of each run, Pallas kernels for 32% -> 32%
where the time goes in v3:
time: 124 us; the launch traced here: 123 us
  Pallas kernels  41.3 us (33%)
  waiting for transfers between devices  31.8 us (26%)
  starting transfers between devices  24.4 us (20%)
  local copies, waits for them, and re-layouts  24.2 us (20%)
    ppermute x16, waiting for transfers between devices, send(): return lax.ppermute(array, 'rows', ring_pairs(groups, way))  26.4 us
    unnamed x40, local copies, waits for them, and re-layouts  21.6 us
    ppermute x16, starting transfers between devices, send(): return lax.ppermute(array, 'rows', ring_pairs(groups, way))  20.1 us
    pallas_call x2, Pallas kernels, densify(): pl.pallas_call(functools.partial(densify_kernel, stages, resident, groups...  14.5 us
    pallas_call x4, Pallas kernels, aggregate(): pl.pallas_call(functools.partial(aggregate_kernel, plan, groups, len(sour...  14.4 us
    pallas_call x4, Pallas kernels, finish(): pl.pallas_call(functools.partial(finish_kernel, plan, groups, len(sources...  7.48 us
    ppermute x6, waiting for transfers between devices, exchange(): lax.ppermute(finished[c, m], 'feat', [(f, f ^ m) for f in range(blocks)])  5.37 us
    ppermute x6, starting transfers between devices, exchange(): lax.ppermute(finished[c, m], 'feat', [(f, f ^ m) for f in range(blocks)])  4.36 us
  transfers between devices with their start and end apart: 22, of which 7 were waited for; matrix products, arithmetic and copies ran while one was open for 1% of the time, Pallas kernels for 32%

profile of v3, /device:TPU:0, one launch (start us, length us, event | category | flops | bytes accessed | tf_op | source)
XLA Modules:
  0.0 123.3 jit_solution(3725244244982519952)
XLA Ops:
  1.3 3.1 %collective-permute-start.11 = (bf16[2048,128]{1,0:T(8,128)(2,1)S(1)}, bf16[2048,128]{1,0:T(8,128)(2,1)S(1)}, u32[]{:S(2)}, u32[]{:S(2)}) collective-permute-start(bf16[2048,128]{1,0:T(8,128)(2,1)S(1)} %get-tuple-element.43.refs_0_), channel_id=1, source_target_pairs={{0,8},{8,16},{16,24},{24,28},{28,20},{20,12},{12,4},{4,0},{1,9},{9... | collective-permute-start | bytes 1572872 | tf_op jit(solution)/shard_map/ppermute | solution.py:369
  4.4 2.0 %collective-permute-start.9 = (bf16[2048,128]{1,0:T(8,128)(2,1)S(1)}, bf16[2048,128]{1,0:T(8,128)(2,1)}, u32[]{:S(2)}, u32[]{:S(2)}) collective-permute-start(bf16[2048,128]{1,0:T(8,128)(2,1)S(1)} %get-tuple-element.43.refs_0_), channel_id=1, source_target_pairs={{0,4},{8,0},{16,8},{24,16},{28,24},{20,28},{12,20},{4,12},{1,5},{9... | collective-permute-start | bytes 1572872 | tf_op jit(solution)/shard_map/ppermute | solution.py:369
  6.4 9.9 %collective-permute-done.11.refs_0_ = bf16[2048,128]{1,0:T(8,128)(2,1)S(1)} collective-permute-done((bf16[2048,128]{1,0:T(8,128)(2,1)S(1)}, bf16[2048,128]{1,0:T(8,128)(2,1)S(1)}, u32[]{:S(2)}, u32[]{:S(2)}) %collective-permute-start.11) | collective-permute-done | bytes 524320 | tf_op jit(solution)/shard_map/ppermute | solution.py:369
  16.3 1.8 %collective-permute-start.12 = (bf16[2048,128]{1,0:T(8,128)(2,1)S(1)}, bf16[2048,128]{1,0:T(8,128)(2,1)}, u32[]{:S(2)}, u32[]{:S(2)}) collective-permute-start(bf16[2048,128]{1,0:T(8,128)(2,1)S(1)} %collective-permute-done.11.refs_0_), channel_id=1, source_target_pairs={{0,8},{8,16},{16,24},{24,28},{28,20},{20,12},{12,4},{4,0},{1,9},{9... | collective-permute-start | bytes 1572872 | tf_op jit(solution)/shard_map/ppermute | solution.py:369
  20.5 1.9 %collective-permute-start = (bf16[1024,128]{1,0:T(8,128)(2,1)S(1)}, bf16[1024,128]{1,0:T(8,128)(2,1)S(1)}, u32[]{:S(2)}, u32[]{:S(2)}) collective-permute-start(bf16[1024,128]{1,0:T(8,128)(2,1)S(1)} %get-tuple-element.46), channel_id=1, source_target_pairs={{0,8},{8,16},{16,24},{24,28},{28,20},{20,12},{12,4},{4,0},{1,9},{9... | collective-permute-start | bytes 786440 | tf_op jit(solution)/shard_map/ppermute | solution.py:369
  22.4 1.6 %collective-permute-start.2 = (bf16[1024,128]{1,0:T(8,128)(2,1)S(1)}, bf16[1024,128]{1,0:T(8,128)(2,1)}, u32[]{:S(2)}, u32[]{:S(2)}) collective-permute-start(bf16[1024,128]{1,0:T(8,128)(2,1)S(1)} %get-tuple-element.45), channel_id=1, source_target_pairs={{0,8},{8,16},{16,24},{24,28},{28,20},{20,12},{12,4},{4,0},{1,9},{9... | collective-permute-start | bytes 786440 | tf_op jit(solution)/shard_map/ppermute | solution.py:369
  24.6 6.0 %collective-permute-done.9.refs_3_ = bf16[2048,128]{1,0:T(8,128)(2,1)} collective-permute-done((bf16[2048,128]{1,0:T(8,128)(2,1)S(1)}, bf16[2048,128]{1,0:T(8,128)(2,1)}, u32[]{:S(2)}, u32[]{:S(2)}) %collective-permute-start.9) | collective-permute-done | bytes 524320 | tf_op jit(solution)/shard_map/ppermute | solution.py:369
  31.2 1.8 %collective-permute-start.13 = (bf16[2048,128]{1,0:T(8,128)(2,1)}, bf16[2048,128]{1,0:T(8,128)(2,1)S(1)}, u32[]{:S(2)}, u32[]{:S(2)}) collective-permute-start(bf16[2048,128]{1,0:T(8,128)(2,1)} %collective-permute-done.12.refs_2_), channel_id=1, source_target_pairs={{0,8},{8,16},{16,24},{24,28},{28,20},{20,12},{12,4},{4,0},{1,9},{9... | collective-permute-start | bytes 1572872 | tf_op jit(solution)/shard_map/ppermute | solution.py:369
  33.0 8.8 %collective-permute-done.6.refs_1_ = bf16[2048,128]{1,0:T(8,128)(2,1)} collective-permute-done((bf16[2048,128]{1,0:T(8,128)(2,1)S(1)}, bf16[2048,128]{1,0:T(8,128)(2,1)}, u32[]{:S(2)}, u32[]{:S(2)}) %collective-permute-start.6) | collective-permute-done | bytes 524320 | tf_op jit(solution)/shard_map/ppermute | solution.py:369
  41.8 2.1 %collective-permute-start.1 = (bf16[1024,128]{1,0:T(8,128)(2,1)S(1)}, bf16[1024,128]{1,0:T(8,128)(2,1)S(1)}, u32[]{:S(2)}, u32[]{:S(2)}) collective-permute-start(bf16[1024,128]{1,0:T(8,128)(2,1)S(1)} %collective-permute-done.refs_1_), channel_id=1, source_target_pairs={{0,8},{8,16},{16,24},{24,28},{28,20},{20,12},{12,4},{4,0},{1,9},{9... | collective-permute-start | bytes 786440 | tf_op jit(solution)/shard_map/ppermute | solution.py:369
  43.9 1.6 %collective-permute-start.3 = (bf16[1024,128]{1,0:T(8,128)(2,1)}, bf16[1024,128]{1,0:T(8,128)(2,1)S(1)}, u32[]{:S(2)}, u32[]{:S(2)}) collective-permute-start(bf16[1024,128]{1,0:T(8,128)(2,1)} %collective-permute-done.2.refs_2_), channel_id=1, source_target_pairs={{0,8},{8,16},{16,24},{24,28},{28,20},{20,12},{12,4},{4,0},{1,9},{9... | collective-permute-start | bytes 786440 | tf_op jit(solution)/shard_map/ppermute | solution.py:369
  45.9 5.7 %densify.3 = (bf16[1,2048,1024]{2,1,0:T(8,128)(2,1)S(1)}, bf16[2,2048,1024]{2,1,0:T(8,128)(2,1)S(1)}) custom-call(s32[1024]{0:T(1024)S(1)} %select_reduce_fusion.table, bf16[640,128,128]{2,1,0:T(8,128)(2,1)} %tiles.3), custom_call_target="tpu_custom_call" | custom-call | bytes 12582912 | tf_op jit(solution)/shard_map/densify/pallas_call | solution.py:86
  51.6 3.3 %copy-done.5 = bf16[2,2048,1024]{2,1,0:T(8,128)(2,1)} copy-done((bf16[2,2048,1024]{2,1,0:T(8,128)(2,1)}, bf16[2,2048,1024]{2,1,0:T(8,128)(2,1)S(1)}, u32[]{:S(2)}) %copy-start.5) | copy-done | bytes 8388632
  54.9 2.0 %copy-done.8 = bf16[1,2048,1024]{2,1,0:T(8,128)(2,1)} copy-done((bf16[1,2048,1024]{2,1,0:T(8,128)(2,1)}, bf16[1,2048,1024]{2,1,0:T(8,128)(2,1)S(1)}, u32[]{:S(2)}) %copy-start.8) | copy-done | bytes 4194328
  56.9 8.8 %densify.2 = (bf16[2,2048,1024]{2,1,0:T(8,128)(2,1)S(1)}, bf16[2,2048,1024]{2,1,0:T(8,128)(2,1)S(1)}, bf16[1,2048,1024]{2,1,0:T(8,128)(2,1)S(1)}) custom-call(s32[1024]{0:T(1024)S(1)} %select_reduce_fusion.table, bf16[640,128,128]{2,1,0:T(8,128)(2,1)} %tiles.3), custom_call_target="tpu_custom_call" | custom-call | bytes 20971520 | tf_op jit(solution)/shard_map/densify/pallas_call | solution.py:86
  65.7 3.3 %copy-done = bf16[2,2048,1024]{2,1,0:T(8,128)(2,1)} copy-done((bf16[2,2048,1024]{2,1,0:T(8,128)(2,1)}, bf16[2,2048,1024]{2,1,0:T(8,128)(2,1)S(1)}, u32[]{:S(2)}) %copy-start) | copy-done | bytes 8388632
  69.0 2.1 %copy-done.1 = bf16[1,2048,1024]{2,1,0:T(8,128)(2,1)} copy-done((bf16[1,2048,1024]{2,1,0:T(8,128)(2,1)}, bf16[1,2048,1024]{2,1,0:T(8,128)(2,1)S(1)}, u32[]{:S(2)}) %copy-start.1) | copy-done | bytes 4194328
  71.0 3.3 %copy-done.3 = bf16[2,2048,1024]{2,1,0:T(8,128)(2,1)} copy-done((bf16[2,2048,1024]{2,1,0:T(8,128)(2,1)}, bf16[2,2048,1024]{2,1,0:T(8,128)(2,1)S(1)}, u32[]{:S(2)}) %copy-start.3) | copy-done | bytes 8388632
  74.4 2.2 %copy-done.9 = bf16[1,2048,1024]{2,1,0:T(8,128)(2,1)S(1)} copy-done((bf16[1,2048,1024]{2,1,0:T(8,128)(2,1)S(1)}, bf16[1,2048,1024]{2,1,0:T(8,128)(2,1)}, u32[]{:S(2)}) %copy-start.9) | copy-done | bytes 4194328
  76.6 2.0 %aggregate.4 = (f32[2048,128]{1,0:T(8,128)S(1)}, f32[2048,128]{1,0:T(8,128)S(1)}) custom-call(s32[512]{0:T(512)S(1)} %reshape.9.need, bf16[2048,128]{1,0:T(8,128)(2,1)S(1)} %get-tuple-element.43.refs_0_, bf16[2048,128]{1,0:T(8,128)(2,1)S(1)} %get-tuple-element.44.refs_1_, bf16[1,2048,1024]{2,1,0:T(8,128)(2,1)S(1)} %copy-done.9), custom_call_target="tpu_custom_call" | custom-call | flops 1073741824 | bytes 4194304 | tf_op jit(solution)/shard_map/aggregate/pallas_call | solution.py:253
  80.9 3.4 %copy-done.6 = bf16[2,2048,1024]{2,1,0:T(8,128)(2,1)S(1)} copy-done((bf16[2,2048,1024]{2,1,0:T(8,128)(2,1)S(1)}, bf16[2,2048,1024]{2,1,0:T(8,128)(2,1)}, u32[]{:S(2)}) %copy-start.6) | copy-done | bytes 8388632
  86.3 4.1 %aggregate.5 = (f32[2048,128]{1,0:T(8,128)S(1)}, f32[2048,128]{1,0:T(8,128)S(1)}) custom-call(s32[512]{0:T(512)S(1)} %reshape.9.need, bf16[2048,128]{1,0:T(8,128)(2,1)S(1)} %copy-done.11, bf16[1024,128]{1,0:T(8,128)(2,1)S(1)} %collective-permute-done.refs_1_, bf16[1024,128]{1,0:T(8,128)(2,1)} %collective-permute-done.2.refs_2_, ...), custom_call_target="tpu_custom_call" | custom-call | flops 2147483648 | bytes 8388608 | tf_op jit(solution)/shard_map/aggregate/pallas_call | solution.py:253
  95.1 5.0 %aggregate.6 = (f32[2048,128]{1,0:T(8,128)S(1)}, f32[2048,128]{1,0:T(8,128)S(1)}) custom-call(s32[512]{0:T(512)S(1)} %reshape.9.need, bf16[2048,128]{1,0:T(8,128)(2,1)S(1)} %collective-permute-done.10.refs_0_, bf16[2048,128]{1,0:T(8,128)(2,1)} %collective-permute-done.6.refs_1_, bf16[2048,128]{1,0:T(8,128)(2,1)} %collective-permute-done.12.refs_2_, ...), custom_call_target="tpu_custom_call" | custom-call | flops 2147483648 | bytes 12582912 | tf_op jit(solution)/shard_map/aggregate/pallas_call | solution.py:253
  100.1 3.4 %aggregate.7.refs_4_ = f32[2048,128]{1,0:T(8,128)S(1)} custom-call(s32[512]{0:T(512)S(1)} %reshape.9.need, bf16[1024,128]{1,0:T(8,128)(2,1)S(1)} %collective-permute-done.1.refs_0_, bf16[1024,128]{1,0:T(8,128)(2,1)S(1)} %collective-permute-done.3.refs_1_, bf16[2048,128]{1,0:T(8,128)(2,1)S(1)} %collective-permute-done.7.refs_0_.refs_2_, ...), custom_call_target="tpu_custom_call" | custom-call | flops 1073741824 | bytes 8388608 | tf_op jit(solution)/shard_map/aggregate/pallas_call | solution.py:253
  103.5 1.9 %finish.7 = (bf16[512,128]{1,0:T(8,128)(2,1)S(1)}, bf16[512,128]{1,0:T(8,128)(2,1)S(1)}) custom-call(s32[512]{0:T(512)S(1)} %reshape.9.need, bf16[1024,128]{1,0:T(8,128)(2,1)S(1)} %collective-permute-done.16.refs_0_, bf16[1024,128]{1,0:T(8,128)(2,1)S(1)} %collective-permute-done.17.refs_1_, bf16[2,2048,1024]{2,1,0:T(8,128)(2,1)S(1)} %bitcast.3, ...), custom_call_target="tpu_custom_call" | custom-call | flops 536870912 | bytes 4194304 | tf_op jit(solution)/shard_map/finish/pallas_call | solution.py:210
  105.4 1.6 %collective-permute-start.20 = (bf16[512,128]{1,0:T(8,128)(2,1)S(1)}, bf16[512,128]{1,0:T(8,128)(2,1)S(1)}, u32[]{:S(2)}, u32[]{:S(2)}) collective-permute-start(bf16[512,128]{1,0:T(8,128)(2,1)S(1)} %get-tuple-element.41), channel_id=1, source_target_pairs={{0,2},{1,3},{2,0},{3,1},{4,6},{5,7},{6,4},{7,5},{8,10},{9,11},{10,... | collective-permute-start | bytes 393224 | tf_op jit(solution)/shard_map/ppermute | solution.py:446
  107.0 1.9 %finish.6 = (bf16[512,128]{1,0:T(8,128)(2,1)S(1)}, bf16[512,128]{1,0:T(8,128)(2,1)S(1)}) custom-call(s32[512]{0:T(512)S(1)} %reshape.9.need, bf16[1024,128]{1,0:T(8,128)(2,1)S(1)} %collective-permute-done.4.refs_0_, bf16[1024,128]{1,0:T(8,128)(2,1)S(1)} %collective-permute-done.8.refs_1_, bf16[2,2048,1024]{2,1,0:T(8,128)(2,1)S(1)} %bitcast.3, ...), custom_call_target="tpu_custom_call" | custom-call | flops 536870912 | bytes 4194304 | tf_op jit(solution)/shard_map/finish/pallas_call | solution.py:210
  109.6 1.9 %finish.5 = (bf16[512,128]{1,0:T(8,128)(2,1)S(1)}, bf16[512,128]{1,0:T(8,128)(2,1)S(1)}) custom-call(s32[512]{0:T(512)S(1)} %reshape.9.need, bf16[1024,128]{1,0:T(8,128)(2,1)S(1)} %collective-permute-done.16.refs_0_, bf16[1024,128]{1,0:T(8,128)(2,1)S(1)} %collective-permute-done.17.refs_1_, bf16[2,2048,1024]{2,1,0:T(8,128)(2,1)S(1)} %bitcast.3, ...), custom_call_target="tpu_custom_call" | custom-call | flops 536870912 | bytes 4194304 | tf_op jit(solution)/shard_map/finish/pallas_call | solution.py:210
  111.6 1.9 %finish.4 = (bf16[512,128]{1,0:T(8,128)(2,1)S(1)}, bf16[512,128]{1,0:T(8,128)(2,1)S(1)}) custom-call(s32[512]{0:T(512)S(1)} %reshape.9.need, bf16[1024,128]{1,0:T(8,128)(2,1)S(1)} %collective-permute-done.4.refs_0_, bf16[1024,128]{1,0:T(8,128)(2,1)S(1)} %collective-permute-done.8.refs_1_, bf16[2,2048,1024]{2,1,0:T(8,128)(2,1)S(1)} %bitcast.3, ...), custom_call_target="tpu_custom_call" | custom-call | flops 536870912 | bytes 4194304 | tf_op jit(solution)/shard_map/finish/pallas_call | solution.py:210
  113.5 1.6 %collective-permute-start.14 = (bf16[512,128]{1,0:T(8,128)(2,1)S(1)}, bf16[512,128]{1,0:T(8,128)(2,1)S(1)}, u32[]{:S(2)}, u32[]{:S(2)}) collective-permute-start(bf16[512,128]{1,0:T(8,128)(2,1)S(1)} %get-tuple-element.34), channel_id=1, source_target_pairs={{0,2},{1,3},{2,0},{3,1},{4,6},{5,7},{6,4},{7,5},{8,10},{9,11},{10,... | collective-permute-start | bytes 393224 | tf_op jit(solution)/shard_map/ppermute | solution.py:446
  116.4 3.5 %collective-permute-done.14.refs_0_ = bf16[512,128]{1,0:T(8,128)(2,1)S(1)} collective-permute-done((bf16[512,128]{1,0:T(8,128)(2,1)S(1)}, bf16[512,128]{1,0:T(8,128)(2,1)S(1)}, u32[]{:S(2)}, u32[]{:S(2)}) %collective-permute-start.14) | collective-permute-done | bytes 131104 | tf_op jit(solution)/shard_map/ppermute | solution.py:446
  119.9 1.9 %collective-permute-done.15.refs_1_ = bf16[512,128]{1,0:T(8,128)(2,1)S(1)} collective-permute-done((bf16[512,128]{1,0:T(8,128)(2,1)S(1)}, bf16[512,128]{1,0:T(8,128)(2,1)S(1)}, u32[]{:S(2)}, u32[]{:S(2)}) %collective-permute-start.15) | collective-permute-done | bytes 131104 | tf_op jit(solution)/shard_map/ppermute | solution.py:446
  (74 shorter events, 17.4 us)
Async XLA Ops:
  0.0 41.8 %copy-start.16 = (s32[640]{0:T(1024)S(1)}, s32[640]{0:T(1024)}, u32[]{:S(2)}) copy-start(s32[640]{0:T(1024)} %param.10) | copy-start | bytes 7684
  0.0 41.8 %copy-start.17 = (s32[640]{0:T(1024)S(1)}, s32[640]{0:T(1024)}, u32[]{:S(2)}) copy-start(s32[640]{0:T(1024)} %param.11) | copy-start | bytes 7684
  0.0 41.8 %copy-start.15 = (s32[640]{0:T(1024)S(1)}, s32[640]{0:T(1024)}, u32[]{:S(2)}) copy-start(s32[640]{0:T(1024)} %param.12) | copy-start | bytes 7684
  1.3 15.0 %collective-permute-start.11 = (bf16[2048,128]{1,0:T(8,128)(2,1)S(1)}, bf16[2048,128]{1,0:T(8,128)(2,1)S(1)}, u32[]{:S(2)}, u32[]{:S(2)}) collective-permute-start(bf16[2048,128]{1,0:T(8,128)(2,1)S(1)} %get-tuple-element.43.refs_0_), channel_id=1, source_target_pairs={{0,8},{8,16},{16,24},{24,28},{28,20},{20,12},{12,4},{4,0},{1,9},{9... | collective-permute-start | bytes 1572872 | tf_op jit(solution)/shard_map/ppermute | solution.py:369
  4.4 14.8 %collective-permute-start.5 = (bf16[2048,128]{1,0:T(8,128)(2,1)S(1)}, bf16[2048,128]{1,0:T(8,128)(2,1)S(1)}, u32[]{:S(2)}, u32[]{:S(2)}) collective-permute-start(bf16[2048,128]{1,0:T(8,128)(2,1)S(1)} %get-tuple-element.44.refs_1_), channel_id=1, source_target_pairs={{0,4},{8,0},{16,8},{24,16},{28,24},{20,28},{12,20},{4,12},{1,5},{9... | collective-permute-start | bytes 1572872 | tf_op jit(solution)/shard_map/ppermute | solution.py:369
  4.4 26.1 %collective-permute-start.9 = (bf16[2048,128]{1,0:T(8,128)(2,1)S(1)}, bf16[2048,128]{1,0:T(8,128)(2,1)}, u32[]{:S(2)}, u32[]{:S(2)}) collective-permute-start(bf16[2048,128]{1,0:T(8,128)(2,1)S(1)} %get-tuple-element.43.refs_0_), channel_id=1, source_target_pairs={{0,4},{8,0},{16,8},{24,16},{28,24},{20,28},{12,20},{4,12},{1,5},{9... | collective-permute-start | bytes 1572872 | tf_op jit(solution)/shard_map/ppermute | solution.py:369
  16.3 14.3 %copy-start.10 = (bf16[2048,128]{1,0:T(8,128)(2,1)}, bf16[2048,128]{1,0:T(8,128)(2,1)S(1)}, u32[]{:S(2)}) copy-start(bf16[2048,128]{1,0:T(8,128)(2,1)S(1)} %collective-permute-done.11.refs_0_) | copy-start | bytes 1572868
  16.3 14.9 %collective-permute-start.12 = (bf16[2048,128]{1,0:T(8,128)(2,1)S(1)}, bf16[2048,128]{1,0:T(8,128)(2,1)}, u32[]{:S(2)}, u32[]{:S(2)}) collective-permute-start(bf16[2048,128]{1,0:T(8,128)(2,1)S(1)} %collective-permute-done.11.refs_0_), channel_id=1, source_target_pairs={{0,8},{8,16},{16,24},{24,28},{28,20},{20,12},{12,4},{4,0},{1,9},{9... | collective-permute-start | bytes 1572872 | tf_op jit(solution)/shard_map/ppermute | solution.py:369
  19.2 13.8 %copy-start.12 = (bf16[2048,128]{1,0:T(8,128)(2,1)}, bf16[2048,128]{1,0:T(8,128)(2,1)S(1)}, u32[]{:S(2)}) copy-start(bf16[2048,128]{1,0:T(8,128)(2,1)S(1)} %collective-permute-done.5.refs_4_) | copy-start | bytes 1572868
  19.2 22.6 %collective-permute-start.6 = (bf16[2048,128]{1,0:T(8,128)(2,1)S(1)}, bf16[2048,128]{1,0:T(8,128)(2,1)}, u32[]{:S(2)}, u32[]{:S(2)}) collective-permute-start(bf16[2048,128]{1,0:T(8,128)(2,1)S(1)} %collective-permute-done.5.refs_4_), channel_id=1, source_target_pairs={{0,4},{8,0},{16,8},{24,16},{28,24},{20,28},{12,20},{4,12},{1,5},{9... | collective-permute-start | bytes 1572872 | tf_op jit(solution)/shard_map/ppermute | solution.py:369
  20.5 21.3 %collective-permute-start = (bf16[1024,128]{1,0:T(8,128)(2,1)S(1)}, bf16[1024,128]{1,0:T(8,128)(2,1)S(1)}, u32[]{:S(2)}, u32[]{:S(2)}) collective-permute-start(bf16[1024,128]{1,0:T(8,128)(2,1)S(1)} %get-tuple-element.46), channel_id=1, source_target_pairs={{0,8},{8,16},{16,24},{24,28},{28,20},{20,12},{12,4},{4,0},{1,9},{9... | collective-permute-start | bytes 786440 | tf_op jit(solution)/shard_map/ppermute | solution.py:369
  22.4 21.5 %collective-permute-start.2 = (bf16[1024,128]{1,0:T(8,128)(2,1)S(1)}, bf16[1024,128]{1,0:T(8,128)(2,1)}, u32[]{:S(2)}, u32[]{:S(2)}) collective-permute-start(bf16[1024,128]{1,0:T(8,128)(2,1)S(1)} %get-tuple-element.45), channel_id=1, source_target_pairs={{0,8},{8,16},{16,24},{24,28},{28,20},{20,12},{12,4},{4,0},{1,9},{9... | collective-permute-start | bytes 786440 | tf_op jit(solution)/shard_map/ppermute | solution.py:369
  30.6 59.9 %collective-permute-start.10 = (bf16[2048,128]{1,0:T(8,128)(2,1)}, bf16[2048,128]{1,0:T(8,128)(2,1)S(1)}, u32[]{:S(2)}, u32[]{:S(2)}) collective-permute-start(bf16[2048,128]{1,0:T(8,128)(2,1)} %collective-permute-done.9.refs_3_), channel_id=1, source_target_pairs={{0,4},{8,0},{16,8},{24,16},{28,24},{20,28},{12,20},{4,12},{1,5},{9... | collective-permute-start | bytes 1572872 | tf_op jit(solution)/shard_map/ppermute | solution.py:369
  31.2 60.5 %collective-permute-start.13 = (bf16[2048,128]{1,0:T(8,128)(2,1)}, bf16[2048,128]{1,0:T(8,128)(2,1)S(1)}, u32[]{:S(2)}, u32[]{:S(2)}) collective-permute-start(bf16[2048,128]{1,0:T(8,128)(2,1)} %collective-permute-done.12.refs_2_), channel_id=1, source_target_pairs={{0,8},{8,16},{16,24},{24,28},{28,20},{20,12},{12,4},{4,0},{1,9},{9... | collective-permute-start | bytes 1572872 | tf_op jit(solution)/shard_map/ppermute | solution.py:369
  41.8 52.0 %collective-permute-start.7 = (bf16[2048,128]{1,0:T(8,128)(2,1)}, bf16[2048,128]{1,0:T(8,128)(2,1)S(1)}, u32[]{:S(2)}, u32[]{:S(2)}) collective-permute-start(bf16[2048,128]{1,0:T(8,128)(2,1)} %collective-permute-done.6.refs_1_), channel_id=1, source_target_pairs={{0,4},{8,0},{16,8},{24,16},{28,24},{20,28},{12,20},{4,12},{1,5},{9... | collective-permute-start | bytes 1572872 | tf_op jit(solution)/shard_map/ppermute | solution.py:369
  41.8 36.7 %collective-permute-start.1 = (bf16[1024,128]{1,0:T(8,128)(2,1)S(1)}, bf16[1024,128]{1,0:T(8,128)(2,1)S(1)}, u32[]{:S(2)}, u32[]{:S(2)}) collective-permute-start(bf16[1024,128]{1,0:T(8,128)(2,1)S(1)} %collective-permute-done.refs_1_), channel_id=1, source_target_pairs={{0,8},{8,16},{16,24},{24,28},{28,20},{20,12},{12,4},{4,0},{1,9},{9... | collective-permute-start | bytes 786440 | tf_op jit(solution)/shard_map/ppermute | solution.py:369
  43.9 34.7 %collective-permute-start.3 = (bf16[1024,128]{1,0:T(8,128)(2,1)}, bf16[1024,128]{1,0:T(8,128)(2,1)S(1)}, u32[]{:S(2)}, u32[]{:S(2)}) collective-permute-start(bf16[1024,128]{1,0:T(8,128)(2,1)} %collective-permute-done.2.refs_2_), channel_id=1, source_target_pairs={{0,8},{8,16},{16,24},{24,28},{28,20},{20,12},{12,4},{4,0},{1,9},{9... | collective-permute-start | bytes 786440 | tf_op jit(solution)/shard_map/ppermute | solution.py:369
  56.9 17.4 %copy-start.14 = (s32[8,8,8]{2,1,0:T(8,128)S(1)}, s32[8,8,8]{2,1,0:T(8,128)}, u32[]{:S(2)}) copy-start(s32[8,8,8]{2,1,0:T(8,128)} %param.14) | copy-start | bytes 6148
  76.6 18.5 %copy-start.4 = (bf16[2,2048,1024]{2,1,0:T(8,128)(2,1)S(1)}, bf16[2,2048,1024]{2,1,0:T(8,128)(2,1)}, u32[]{:S(2)}) copy-start(bf16[2,2048,1024]{2,1,0:T(8,128)(2,1)} %copy-done.3) | copy-start | bytes 25165828
  78.6 16.5 %slice-start = ((s8[8388608]{0:T(1024)(128)(4,1)}), s8[4194304]{0:T(1024)(128)(4,1)S(1)}, s32[]{:S(2)}) async-start(s8[8388608]{0:T(1024)(128)(4,1)} %bitcast.2), calls=%async_computation | async-start | bytes 8388608
  79.4 27.6 %collective-permute-start.4 = (bf16[1024,128]{1,0:T(8,128)(2,1)S(1)}, bf16[1024,128]{1,0:T(8,128)(2,1)S(1)}, u32[]{:S(2)}, u32[]{:S(2)}) collective-permute-start(bf16[1024,128]{1,0:T(8,128)(2,1)S(1)} %pick.4), channel_id=1, source_target_pairs={{0,8},{8,16},{16,24},{24,28},{28,20},{20,12},{12,4},{4,0},{1,9},{9... | collective-permute-start | bytes 786440 | tf_op jit(solution)/shard_map/ppermute | solution.py:369
  86.3 8.8 %slice-start.1 = ((s8[8388608]{0:T(1024)(128)(4,1)}), s8[4194304]{0:T(1024)(128)(4,1)S(1)}, s32[]{:S(2)}) async-start(s8[8388608]{0:T(1024)(128)(4,1)} %bitcast.2), calls=%async_computation.1 | async-start | bytes 8388608
  91.0 12.4 %collective-permute-start.16 = (bf16[1024,128]{1,0:T(8,128)(2,1)S(1)}, bf16[1024,128]{1,0:T(8,128)(2,1)S(1)}, u32[]{:S(2)}, u32[]{:S(2)}) collective-permute-start(bf16[1024,128]{1,0:T(8,128)(2,1)S(1)} %pick.6), channel_id=1, source_target_pairs={{0,4},{8,0},{16,8},{24,16},{28,24},{20,28},{12,20},{4,12},{1,5},{9... | collective-permute-start | bytes 786440 | tf_op jit(solution)/shard_map/ppermute | solution.py:369
  92.3 11.2 %collective-permute-start.17 = (bf16[1024,128]{1,0:T(8,128)(2,1)S(1)}, bf16[1024,128]{1,0:T(8,128)(2,1)S(1)}, u32[]{:S(2)}, u32[]{:S(2)}) collective-permute-start(bf16[1024,128]{1,0:T(8,128)(2,1)S(1)} %pick.7), channel_id=1, source_target_pairs={{0,8},{8,16},{16,24},{24,28},{28,20},{20,12},{12,4},{4,0},{1,9},{9... | collective-permute-start | bytes 786440 | tf_op jit(solution)/shard_map/ppermute | solution.py:369
  94.4 12.5 %collective-permute-start.8 = (bf16[1024,128]{1,0:T(8,128)(2,1)S(1)}, bf16[1024,128]{1,0:T(8,128)(2,1)S(1)}, u32[]{:S(2)}, u32[]{:S(2)}) collective-permute-start(bf16[1024,128]{1,0:T(8,128)(2,1)S(1)} %pick.5), channel_id=1, source_target_pairs={{0,4},{8,0},{16,8},{24,16},{28,24},{20,28},{12,20},{4,12},{1,5},{9... | collective-permute-start | bytes 786440 | tf_op jit(solution)/shard_map/ppermute | solution.py:369
  105.4 9.7 %collective-permute-start.20 = (bf16[512,128]{1,0:T(8,128)(2,1)S(1)}, bf16[512,128]{1,0:T(8,128)(2,1)S(1)}, u32[]{:S(2)}, u32[]{:S(2)}) collective-permute-start(bf16[512,128]{1,0:T(8,128)(2,1)S(1)} %get-tuple-element.41), channel_id=1, source_target_pairs={{0,2},{1,3},{2,0},{3,1},{4,6},{5,7},{6,4},{7,5},{8,10},{9,11},{10,... | collective-permute-start | bytes 393224 | tf_op jit(solution)/shard_map/ppermute | solution.py:446
  106.9 8.5 %collective-permute-start.21 = (bf16[512,128]{1,0:T(8,128)(2,1)S(1)}, bf16[512,128]{1,0:T(8,128)(2,1)S(1)}, u32[]{:S(2)}, u32[]{:S(2)}) collective-permute-start(bf16[512,128]{1,0:T(8,128)(2,1)S(1)} %get-tuple-element.42), channel_id=1, source_target_pairs={{0,3},{1,2},{2,1},{3,0},{4,7},{5,6},{6,5},{7,4},{8,11},{9,10},{10,... | collective-permute-start | bytes 393224 | tf_op jit(solution)/shard_map/ppermute | solution.py:446
  108.8 6.6 %collective-permute-start.19 = (bf16[512,128]{1,0:T(8,128)(2,1)S(1)}, bf16[512,128]{1,0:T(8,128)(2,1)S(1)}, u32[]{:S(2)}, u32[]{:S(2)}) collective-permute-start(bf16[512,128]{1,0:T(8,128)(2,1)S(1)} %get-tuple-element.40), channel_id=1, source_target_pairs={{0,1},{1,0},{2,3},{3,2},{4,5},{5,4},{6,7},{7,6},{8,9},{9,8},{10,11... | collective-permute-start | bytes 393224 | tf_op jit(solution)/shard_map/ppermute | solution.py:446
  111.5 4.0 %copy-start.7 = (bf16[1024,1024]{1,0:T(8,128)(2,1)S(1)}, bf16[1024,1024]{1,0:T(8,128)(2,1)}, u32[]{:S(2)}) copy-start(bf16[1024,1024]{1,0:T(8,128)(2,1)} %w.3) | copy-start | bytes 6291460
  111.5 3.9 %collective-permute-start.18 = (bf16[512,128]{1,0:T(8,128)(2,1)S(1)}, bf16[512,128]{1,0:T(8,128)(2,1)S(1)}, u32[]{:S(2)}, u32[]{:S(2)}) collective-permute-start(bf16[512,128]{1,0:T(8,128)(2,1)S(1)} %get-tuple-element.39), channel_id=1, source_target_pairs={{0,1},{1,0},{2,3},{3,2},{4,5},{5,4},{6,7},{7,6},{8,9},{9,8},{10,11... | collective-permute-start | bytes 393224 | tf_op jit(solution)/shard_map/ppermute | solution.py:446
  113.5 6.4 %collective-permute-start.14 = (bf16[512,128]{1,0:T(8,128)(2,1)S(1)}, bf16[512,128]{1,0:T(8,128)(2,1)S(1)}, u32[]{:S(2)}, u32[]{:S(2)}) collective-permute-start(bf16[512,128]{1,0:T(8,128)(2,1)S(1)} %get-tuple-element.34), channel_id=1, source_target_pairs={{0,2},{1,3},{2,0},{3,1},{4,6},{5,7},{6,4},{7,5},{8,10},{9,11},{10,... | collective-permute-start | bytes 393224 | tf_op jit(solution)/shard_map/ppermute | solution.py:446
  115.1 6.7 %collective-permute-start.15 = (bf16[512,128]{1,0:T(8,128)(2,1)S(1)}, bf16[512,128]{1,0:T(8,128)(2,1)S(1)}, u32[]{:S(2)}, u32[]{:S(2)}) collective-permute-start(bf16[512,128]{1,0:T(8,128)(2,1)S(1)} %get-tuple-element.35), channel_id=1, source_target_pairs={{0,3},{1,2},{2,1},{3,0},{4,7},{5,6},{6,5},{7,4},{8,11},{9,10},{10,... | collective-permute-start | bytes 393224 | tf_op jit(solution)/shard_map/ppermute | solution.py:446
  (10 other events, 25.0 us)

commit v4 on v3

--- a/solution.py
+++ b/solution.py
@@ -447,15 +447,13 @@
 
     order = [(c, m) for c in range(cuts) for m in reversed(range(blocks))]
     arrived = {key: exchange(*key) for key in order}
-    late = [(last, m) for m in range(2, blocks)]
-    soon = [(c, m) for m in range(blocks) for c in range(cuts) if (c, m) not in late]
+    soon = [(c, 0) for c in range(cuts)] + [(c, m) for c in range(last) for m in range(2, blocks)]
+    late = [(c, 1) for c in range(cuts)] + [(last, m) for m in range(2, blocks)]
 
     def multiply(keys, start_total, final):
         starts = tuple((m, c * part) for c, m in keys)
         return product([arrived[key] for key in keys], starts, width, weight, start_total, final)
 
-    if not late:
-        return multiply(soon, None, True)
     return multiply(late, multiply(soon, None, False), True)
 
 

time: 124 us -> 121 us (0.976)
  waiting for transfers between devices: 31.8 us -> 28.7 us
    ppermute x6, waiting for transfers between devices: 5.37 us -> 2.23 us  [exchange(): lax.ppermute(finished[c, m], 'feat', [(f, f ^ m) for f in range(blocks)])]
  transfers between devices with their start and end apart: 22 -> 22, of which waited for: 7 -> 7; matrix products, arithmetic and copies ran while one was open for 1% -> 1% of each run, Pallas kernels for 32% -> 33%
where the time goes in v4:
time: 121 us; the launch traced here: 120 us
  Pallas kernels  41.2 us (34%)
  waiting for transfers between devices  28.7 us (24%)
  starting transfers between devices  24.4 us (20%)
  local copies, waits for them, and re-layouts  24.2 us (20%)
    ppermute x16, waiting for transfers between devices, send(): return lax.ppermute(array, 'rows', ring_pairs(groups, way))  26.4 us
    unnamed x40, local copies, waits for them, and re-layouts  21.6 us
    ppermute x16, starting transfers between devices, send(): return lax.ppermute(array, 'rows', ring_pairs(groups, way))  20.1 us
    pallas_call x2, Pallas kernels, densify(): pl.pallas_call(functools.partial(densify_kernel, stages, resident, groups...  14.5 us
    pallas_call x4, Pallas kernels, aggregate(): pl.pallas_call(functools.partial(aggregate_kernel, plan, groups, len(sour...  14.4 us
    pallas_call x4, Pallas kernels, finish(): pl.pallas_call(functools.partial(finish_kernel, plan, groups, len(sources...  7.48 us
    ppermute x6, starting transfers between devices, exchange(): lax.ppermute(finished[c, m], 'feat', [(f, f ^ m) for f in range(blocks)])  4.36 us
    pallas_call x4, Pallas kernels, pick(): pl.pallas_call(functools.partial(pick_kernel, reader, offset, groups), ou...  2.58 us
  transfers between devices with their start and end apart: 22, of which 7 were waited for; matrix products, arithmetic and copies ran while one was open for 1% of the time, Pallas kernels for 33%

profile of v4, /device:TPU:0, one launch (start us, length us, event | category | flops | bytes accessed | tf_op | source)
XLA Modules:
  0.0 120.1 jit_solution(183330768866562418)
XLA Ops:
  1.3 3.1 %collective-permute-start.3 = (bf16[2048,128]{1,0:T(8,128)(2,1)S(1)}, bf16[2048,128]{1,0:T(8,128)(2,1)S(1)}, u32[]{:S(2)}, u32[]{:S(2)}) collective-permute-start(bf16[2048,128]{1,0:T(8,128)(2,1)S(1)} %get-tuple-element.46.refs_0_), channel_id=1, source_target_pairs={{0,8},{8,16},{16,24},{24,28},{28,20},{20,12},{12,4},{4,0},{1,9},{9... | collective-permute-start | bytes 1572872 | tf_op jit(solution)/shard_map/ppermute | solution.py:369
  4.4 2.0 %collective-permute-start = (bf16[2048,128]{1,0:T(8,128)(2,1)S(1)}, bf16[2048,128]{1,0:T(8,128)(2,1)}, u32[]{:S(2)}, u32[]{:S(2)}) collective-permute-start(bf16[2048,128]{1,0:T(8,128)(2,1)S(1)} %get-tuple-element.46.refs_0_), channel_id=1, source_target_pairs={{0,4},{8,0},{16,8},{24,16},{28,24},{20,28},{12,20},{4,12},{1,5},{9... | collective-permute-start | bytes 1572872 | tf_op jit(solution)/shard_map/ppermute | solution.py:369
  6.4 9.9 %collective-permute-done.3.refs_0_ = bf16[2048,128]{1,0:T(8,128)(2,1)S(1)} collective-permute-done((bf16[2048,128]{1,0:T(8,128)(2,1)S(1)}, bf16[2048,128]{1,0:T(8,128)(2,1)S(1)}, u32[]{:S(2)}, u32[]{:S(2)}) %collective-permute-start.3) | collective-permute-done | bytes 524320 | tf_op jit(solution)/shard_map/ppermute | solution.py:369
  16.3 1.8 %collective-permute-start.4 = (bf16[2048,128]{1,0:T(8,128)(2,1)S(1)}, bf16[2048,128]{1,0:T(8,128)(2,1)}, u32[]{:S(2)}, u32[]{:S(2)}) collective-permute-start(bf16[2048,128]{1,0:T(8,128)(2,1)S(1)} %collective-permute-done.3.refs_0_), channel_id=1, source_target_pairs={{0,8},{8,16},{16,24},{24,28},{28,20},{20,12},{12,4},{4,0},{1,9},{9... | collective-permute-start | bytes 1572872 | tf_op jit(solution)/shard_map/ppermute | solution.py:369
  20.5 1.9 %collective-permute-start.9 = (bf16[1024,128]{1,0:T(8,128)(2,1)S(1)}, bf16[1024,128]{1,0:T(8,128)(2,1)S(1)}, u32[]{:S(2)}, u32[]{:S(2)}) collective-permute-start(bf16[1024,128]{1,0:T(8,128)(2,1)S(1)} %get-tuple-element.44), channel_id=1, source_target_pairs={{0,8},{8,16},{16,24},{24,28},{28,20},{20,12},{12,4},{4,0},{1,9},{9... | collective-permute-start | bytes 786440 | tf_op jit(solution)/shard_map/ppermute | solution.py:369
  22.4 1.6 %collective-permute-start.10 = (bf16[1024,128]{1,0:T(8,128)(2,1)S(1)}, bf16[1024,128]{1,0:T(8,128)(2,1)}, u32[]{:S(2)}, u32[]{:S(2)}) collective-permute-start(bf16[1024,128]{1,0:T(8,128)(2,1)S(1)} %get-tuple-element.43), channel_id=1, source_target_pairs={{0,8},{8,16},{16,24},{24,28},{28,20},{20,12},{12,4},{4,0},{1,9},{9... | collective-permute-start | bytes 786440 | tf_op jit(solution)/shard_map/ppermute | solution.py:369
  24.6 6.0 %collective-permute-done.refs_3_ = bf16[2048,128]{1,0:T(8,128)(2,1)} collective-permute-done((bf16[2048,128]{1,0:T(8,128)(2,1)S(1)}, bf16[2048,128]{1,0:T(8,128)(2,1)}, u32[]{:S(2)}, u32[]{:S(2)}) %collective-permute-start) | collective-permute-done | bytes 524320 | tf_op jit(solution)/shard_map/ppermute | solution.py:369
  31.2 1.8 %collective-permute-start.5 = (bf16[2048,128]{1,0:T(8,128)(2,1)}, bf16[2048,128]{1,0:T(8,128)(2,1)S(1)}, u32[]{:S(2)}, u32[]{:S(2)}) collective-permute-start(bf16[2048,128]{1,0:T(8,128)(2,1)} %collective-permute-done.4.refs_2_), channel_id=1, source_target_pairs={{0,8},{8,16},{16,24},{24,28},{28,20},{20,12},{12,4},{4,0},{1,9},{9... | collective-permute-start | bytes 1572872 | tf_op jit(solution)/shard_map/ppermute | solution.py:369
  33.0 8.8 %collective-permute-done.8.refs_1_ = bf16[2048,128]{1,0:T(8,128)(2,1)} collective-permute-done((bf16[2048,128]{1,0:T(8,128)(2,1)S(1)}, bf16[2048,128]{1,0:T(8,128)(2,1)}, u32[]{:S(2)}, u32[]{:S(2)}) %collective-permute-start.8) | collective-permute-done | bytes 524320 | tf_op jit(solution)/shard_map/ppermute | solution.py:369
  41.8 2.1 %collective-permute-start.12 = (bf16[1024,128]{1,0:T(8,128)(2,1)S(1)}, bf16[1024,128]{1,0:T(8,128)(2,1)S(1)}, u32[]{:S(2)}, u32[]{:S(2)}) collective-permute-start(bf16[1024,128]{1,0:T(8,128)(2,1)S(1)} %collective-permute-done.9.refs_1_), channel_id=1, source_target_pairs={{0,8},{8,16},{16,24},{24,28},{28,20},{20,12},{12,4},{4,0},{1,9},{9... | collective-permute-start | bytes 786440 | tf_op jit(solution)/shard_map/ppermute | solution.py:369
  43.9 1.6 %collective-permute-start.13 = (bf16[1024,128]{1,0:T(8,128)(2,1)}, bf16[1024,128]{1,0:T(8,128)(2,1)S(1)}, u32[]{:S(2)}, u32[]{:S(2)}) collective-permute-start(bf16[1024,128]{1,0:T(8,128)(2,1)} %collective-permute-done.10.refs_2_), channel_id=1, source_target_pairs={{0,8},{8,16},{16,24},{24,28},{28,20},{20,12},{12,4},{4,0},{1,9},{9... | collective-permute-start | bytes 786440 | tf_op jit(solution)/shard_map/ppermute | solution.py:369
  45.9 5.7 %densify.3 = (bf16[1,2048,1024]{2,1,0:T(8,128)(2,1)S(1)}, bf16[2,2048,1024]{2,1,0:T(8,128)(2,1)S(1)}) custom-call(s32[1024]{0:T(1024)S(1)} %select_reduce_fusion.table, bf16[640,128,128]{2,1,0:T(8,128)(2,1)} %tiles.3), custom_call_target="tpu_custom_call" | custom-call | bytes 12582912 | tf_op jit(solution)/shard_map/densify/pallas_call | solution.py:86
  51.6 3.3 %copy-done.5 = bf16[2,2048,1024]{2,1,0:T(8,128)(2,1)} copy-done((bf16[2,2048,1024]{2,1,0:T(8,128)(2,1)}, bf16[2,2048,1024]{2,1,0:T(8,128)(2,1)S(1)}, u32[]{:S(2)}) %copy-start.5) | copy-done | bytes 8388632
  54.9 2.0 %copy-done.8 = bf16[1,2048,1024]{2,1,0:T(8,128)(2,1)} copy-done((bf16[1,2048,1024]{2,1,0:T(8,128)(2,1)}, bf16[1,2048,1024]{2,1,0:T(8,128)(2,1)S(1)}, u32[]{:S(2)}) %copy-start.8) | copy-done | bytes 4194328
  56.9 8.8 %densify.2 = (bf16[2,2048,1024]{2,1,0:T(8,128)(2,1)S(1)}, bf16[2,2048,1024]{2,1,0:T(8,128)(2,1)S(1)}, bf16[1,2048,1024]{2,1,0:T(8,128)(2,1)S(1)}) custom-call(s32[1024]{0:T(1024)S(1)} %select_reduce_fusion.table, bf16[640,128,128]{2,1,0:T(8,128)(2,1)} %tiles.3), custom_call_target="tpu_custom_call" | custom-call | bytes 20971520 | tf_op jit(solution)/shard_map/densify/pallas_call | solution.py:86
  65.7 3.3 %copy-done = bf16[2,2048,1024]{2,1,0:T(8,128)(2,1)} copy-done((bf16[2,2048,1024]{2,1,0:T(8,128)(2,1)}, bf16[2,2048,1024]{2,1,0:T(8,128)(2,1)S(1)}, u32[]{:S(2)}) %copy-start) | copy-done | bytes 8388632
  69.0 2.1 %copy-done.1 = bf16[1,2048,1024]{2,1,0:T(8,128)(2,1)} copy-done((bf16[1,2048,1024]{2,1,0:T(8,128)(2,1)}, bf16[1,2048,1024]{2,1,0:T(8,128)(2,1)S(1)}, u32[]{:S(2)}) %copy-start.1) | copy-done | bytes 4194328
  71.0 3.3 %copy-done.3 = bf16[2,2048,1024]{2,1,0:T(8,128)(2,1)} copy-done((bf16[2,2048,1024]{2,1,0:T(8,128)(2,1)}, bf16[2,2048,1024]{2,1,0:T(8,128)(2,1)S(1)}, u32[]{:S(2)}) %copy-start.3) | copy-done | bytes 8388632
  74.4 2.2 %copy-done.9 = bf16[1,2048,1024]{2,1,0:T(8,128)(2,1)S(1)} copy-done((bf16[1,2048,1024]{2,1,0:T(8,128)(2,1)S(1)}, bf16[1,2048,1024]{2,1,0:T(8,128)(2,1)}, u32[]{:S(2)}) %copy-start.9) | copy-done | bytes 4194328
  76.6 2.0 %aggregate.4 = (f32[2048,128]{1,0:T(8,128)S(1)}, f32[2048,128]{1,0:T(8,128)S(1)}) custom-call(s32[512]{0:T(512)S(1)} %reshape.9.need, bf16[2048,128]{1,0:T(8,128)(2,1)S(1)} %get-tuple-element.46.refs_0_, bf16[2048,128]{1,0:T(8,128)(2,1)S(1)} %get-tuple-element.45.refs_1_, bf16[1,2048,1024]{2,1,0:T(8,128)(2,1)S(1)} %copy-done.9), custom_call_target="tpu_custom_call" | custom-call | flops 1073741824 | bytes 4194304 | tf_op jit(solution)/shard_map/aggregate/pallas_call | solution.py:253
  80.9 3.4 %copy-done.6 = bf16[2,2048,1024]{2,1,0:T(8,128)(2,1)S(1)} copy-done((bf16[2,2048,1024]{2,1,0:T(8,128)(2,1)S(1)}, bf16[2,2048,1024]{2,1,0:T(8,128)(2,1)}, u32[]{:S(2)}) %copy-start.6) | copy-done | bytes 8388632
  86.3 4.1 %aggregate.5 = (f32[2048,128]{1,0:T(8,128)S(1)}, f32[2048,128]{1,0:T(8,128)S(1)}) custom-call(s32[512]{0:T(512)S(1)} %reshape.9.need, bf16[2048,128]{1,0:T(8,128)(2,1)S(1)} %copy-done.11, bf16[1024,128]{1,0:T(8,128)(2,1)S(1)} %collective-permute-done.9.refs_1_, bf16[1024,128]{1,0:T(8,128)(2,1)} %collective-permute-done.10.refs_2_, ...), custom_call_target="tpu_custom_call" | custom-call | flops 2147483648 | bytes 8388608 | tf_op jit(solution)/shard_map/aggregate/pallas_call | solution.py:253
  95.1 5.0 %aggregate.6 = (f32[2048,128]{1,0:T(8,128)S(1)}, f32[2048,128]{1,0:T(8,128)S(1)}) custom-call(s32[512]{0:T(512)S(1)} %reshape.9.need, bf16[2048,128]{1,0:T(8,128)(2,1)S(1)} %collective-permute-done.1.refs_0_, bf16[2048,128]{1,0:T(8,128)(2,1)} %collective-permute-done.8.refs_1_, bf16[2048,128]{1,0:T(8,128)(2,1)} %collective-permute-done.4.refs_2_, ...), custom_call_target="tpu_custom_call" | custom-call | flops 2147483648 | bytes 12582912 | tf_op jit(solution)/shard_map/aggregate/pallas_call | solution.py:253
  100.1 3.4 %aggregate.7.refs_4_ = f32[2048,128]{1,0:T(8,128)S(1)} custom-call(s32[512]{0:T(512)S(1)} %reshape.9.need, bf16[1024,128]{1,0:T(8,128)(2,1)S(1)} %collective-permute-done.12.refs_0_, bf16[1024,128]{1,0:T(8,128)(2,1)S(1)} %collective-permute-done.13.refs_1_, bf16[2048,128]{1,0:T(8,128)(2,1)S(1)} %collective-permute-done.15.refs_0_.refs_2_, ...), custom_call_target="tpu_custom_call" | custom-call | flops 1073741824 | bytes 8388608 | tf_op jit(solution)/shard_map/aggregate/pallas_call | solution.py:253
  103.5 1.9 %finish.7 = (bf16[512,128]{1,0:T(8,128)(2,1)S(1)}, bf16[512,128]{1,0:T(8,128)(2,1)S(1)}) custom-call(s32[512]{0:T(512)S(1)} %reshape.9.need, bf16[1024,128]{1,0:T(8,128)(2,1)S(1)} %collective-permute-done.2.refs_0_, bf16[1024,128]{1,0:T(8,128)(2,1)S(1)} %collective-permute-done.6.refs_1_, bf16[2,2048,1024]{2,1,0:T(8,128)(2,1)S(1)} %bitcast.3, ...), custom_call_target="tpu_custom_call" | custom-call | flops 536870912 | bytes 4194304 | tf_op jit(solution)/shard_map/finish/pallas_call | solution.py:210
  105.4 1.6 %collective-permute-start.20 = (bf16[512,128]{1,0:T(8,128)(2,1)S(1)}, bf16[512,128]{1,0:T(8,128)(2,1)S(1)}, u32[]{:S(2)}, u32[]{:S(2)}) collective-permute-start(bf16[512,128]{1,0:T(8,128)(2,1)S(1)} %get-tuple-element.41), channel_id=1, source_target_pairs={{0,2},{1,3},{2,0},{3,1},{4,6},{5,7},{6,4},{7,5},{8,10},{9,11},{10,... | collective-permute-start | bytes 393224 | tf_op jit(solution)/shard_map/ppermute | solution.py:446
  107.0 1.9 %finish.6 = (bf16[512,128]{1,0:T(8,128)(2,1)S(1)}, bf16[512,128]{1,0:T(8,128)(2,1)S(1)}) custom-call(s32[512]{0:T(512)S(1)} %reshape.9.need, bf16[1024,128]{1,0:T(8,128)(2,1)S(1)} %collective-permute-done.14.refs_0_, bf16[1024,128]{1,0:T(8,128)(2,1)S(1)} %collective-permute-done.16.refs_1_, bf16[2,2048,1024]{2,1,0:T(8,128)(2,1)S(1)} %bitcast.3, ...), custom_call_target="tpu_custom_call" | custom-call | flops 536870912 | bytes 4194304 | tf_op jit(solution)/shard_map/finish/pallas_call | solution.py:210
  109.4 1.5 %collective-permute-start.19 = (bf16[512,128]{1,0:T(8,128)(2,1)S(1)}, bf16[512,128]{1,0:T(8,128)(2,1)S(1)}, u32[]{:S(2)}, u32[]{:S(2)}) collective-permute-start(bf16[512,128]{1,0:T(8,128)(2,1)S(1)} %get-tuple-element.38), channel_id=1, source_target_pairs={{0,3},{1,2},{2,1},{3,0},{4,7},{5,6},{6,5},{7,4},{8,11},{9,10},{10,... | collective-permute-start | bytes 393224 | tf_op jit(solution)/shard_map/ppermute | solution.py:446
  110.9 1.9 %finish.5 = (bf16[512,128]{1,0:T(8,128)(2,1)S(1)}, bf16[512,128]{1,0:T(8,128)(2,1)S(1)}) custom-call(s32[512]{0:T(512)S(1)} %reshape.9.need, bf16[1024,128]{1,0:T(8,128)(2,1)S(1)} %collective-permute-done.14.refs_0_, bf16[1024,128]{1,0:T(8,128)(2,1)S(1)} %collective-permute-done.16.refs_1_, bf16[2,2048,1024]{2,1,0:T(8,128)(2,1)S(1)} %bitcast.3, ...), custom_call_target="tpu_custom_call" | custom-call | flops 536870912 | bytes 4194304 | tf_op jit(solution)/shard_map/finish/pallas_call | solution.py:210
  113.1 1.9 %finish.4 = (bf16[512,128]{1,0:T(8,128)(2,1)S(1)}, bf16[512,128]{1,0:T(8,128)(2,1)S(1)}) custom-call(s32[512]{0:T(512)S(1)} %reshape.9.need, bf16[1024,128]{1,0:T(8,128)(2,1)S(1)} %collective-permute-done.2.refs_0_, bf16[1024,128]{1,0:T(8,128)(2,1)S(1)} %collective-permute-done.6.refs_1_, bf16[2,2048,1024]{2,1,0:T(8,128)(2,1)S(1)} %bitcast.3, ...), custom_call_target="tpu_custom_call" | custom-call | flops 536870912 | bytes 4194304 | tf_op jit(solution)/shard_map/finish/pallas_call | solution.py:210
  116.5 1.8 %collective-permute-done.19.refs_3_ = bf16[512,128]{1,0:T(8,128)(2,1)S(1)} collective-permute-done((bf16[512,128]{1,0:T(8,128)(2,1)S(1)}, bf16[512,128]{1,0:T(8,128)(2,1)S(1)}, u32[]{:S(2)}, u32[]{:S(2)}) %collective-permute-start.19) | collective-permute-done | bytes 131104 | tf_op jit(solution)/shard_map/ppermute | solution.py:446
  118.4 1.6 %product.3 = bf16[512,1024]{1,0:T(8,128)(2,1)} custom-call(bf16[1024,1024]{1,0:T(8,128)(2,1)S(1)} %copy-done.7, bf16[512,128]{1,0:T(8,128)(2,1)S(1)} %collective-permute-done.11.refs_0_, bf16[512,128]{1,0:T(8,128)(2,1)S(1)} %collective-permute-done.17.refs_1_, bf16[512,128]{1,0:T(8,128)(2,1)S(1)} %collective-permute-done.18.refs_2_, ...), custom_call_target="tpu_custom_call" | custom-call | flops 536870912 | bytes 4194304 | tf_op jit(solution)/shard_map/product/pallas_call | solution.py:330
  (74 shorter events, 16.3 us)
Async XLA Ops:
  0.0 41.8 %copy-start.16 = (s32[640]{0:T(1024)S(1)}, s32[640]{0:T(1024)}, u32[]{:S(2)}) copy-start(s32[640]{0:T(1024)} %param.10) | copy-start | bytes 7684
  0.0 41.8 %copy-start.17 = (s32[640]{0:T(1024)S(1)}, s32[640]{0:T(1024)}, u32[]{:S(2)}) copy-start(s32[640]{0:T(1024)} %param.11) | copy-start | bytes 7684
  0.0 41.8 %copy-start.15 = (s32[640]{0:T(1024)S(1)}, s32[640]{0:T(1024)}, u32[]{:S(2)}) copy-start(s32[640]{0:T(1024)} %param.12) | copy-start | bytes 7684
  1.3 15.0 %collective-permute-start.3 = (bf16[2048,128]{1,0:T(8,128)(2,1)S(1)}, bf16[2048,128]{1,0:T(8,128)(2,1)S(1)}, u32[]{:S(2)}, u32[]{:S(2)}) collective-permute-start(bf16[2048,128]{1,0:T(8,128)(2,1)S(1)} %get-tuple-element.46.refs_0_), channel_id=1, source_target_pairs={{0,8},{8,16},{16,24},{24,28},{28,20},{20,12},{12,4},{4,0},{1,9},{9... | collective-permute-start | bytes 1572872 | tf_op jit(solution)/shard_map/ppermute | solution.py:369
  4.4 14.8 %collective-permute-start.7 = (bf16[2048,128]{1,0:T(8,128)(2,1)S(1)}, bf16[2048,128]{1,0:T(8,128)(2,1)S(1)}, u32[]{:S(2)}, u32[]{:S(2)}) collective-permute-start(bf16[2048,128]{1,0:T(8,128)(2,1)S(1)} %get-tuple-element.45.refs_1_), channel_id=1, source_target_pairs={{0,4},{8,0},{16,8},{24,16},{28,24},{20,28},{12,20},{4,12},{1,5},{9... | collective-permute-start | bytes 1572872 | tf_op jit(solution)/shard_map/ppermute | solution.py:369
  4.4 26.1 %collective-permute-start = (bf16[2048,128]{1,0:T(8,128)(2,1)S(1)}, bf16[2048,128]{1,0:T(8,128)(2,1)}, u32[]{:S(2)}, u32[]{:S(2)}) collective-permute-start(bf16[2048,128]{1,0:T(8,128)(2,1)S(1)} %get-tuple-element.46.refs_0_), channel_id=1, source_target_pairs={{0,4},{8,0},{16,8},{24,16},{28,24},{20,28},{12,20},{4,12},{1,5},{9... | collective-permute-start | bytes 1572872 | tf_op jit(solution)/shard_map/ppermute | solution.py:369
  16.3 14.3 %copy-start.10 = (bf16[2048,128]{1,0:T(8,128)(2,1)}, bf16[2048,128]{1,0:T(8,128)(2,1)S(1)}, u32[]{:S(2)}) copy-start(bf16[2048,128]{1,0:T(8,128)(2,1)S(1)} %collective-permute-done.3.refs_0_) | copy-start | bytes 1572868
  16.3 14.9 %collective-permute-start.4 = (bf16[2048,128]{1,0:T(8,128)(2,1)S(1)}, bf16[2048,128]{1,0:T(8,128)(2,1)}, u32[]{:S(2)}, u32[]{:S(2)}) collective-permute-start(bf16[2048,128]{1,0:T(8,128)(2,1)S(1)} %collective-permute-done.3.refs_0_), channel_id=1, source_target_pairs={{0,8},{8,16},{16,24},{24,28},{28,20},{20,12},{12,4},{4,0},{1,9},{9... | collective-permute-start | bytes 1572872 | tf_op jit(solution)/shard_map/ppermute | solution.py:369
  19.2 13.8 %copy-start.12 = (bf16[2048,128]{1,0:T(8,128)(2,1)}, bf16[2048,128]{1,0:T(8,128)(2,1)S(1)}, u32[]{:S(2)}) copy-start(bf16[2048,128]{1,0:T(8,128)(2,1)S(1)} %collective-permute-done.7.refs_4_) | copy-start | bytes 1572868
  19.2 22.6 %collective-permute-start.8 = (bf16[2048,128]{1,0:T(8,128)(2,1)S(1)}, bf16[2048,128]{1,0:T(8,128)(2,1)}, u32[]{:S(2)}, u32[]{:S(2)}) collective-permute-start(bf16[2048,128]{1,0:T(8,128)(2,1)S(1)} %collective-permute-done.7.refs_4_), channel_id=1, source_target_pairs={{0,4},{8,0},{16,8},{24,16},{28,24},{20,28},{12,20},{4,12},{1,5},{9... | collective-permute-start | bytes 1572872 | tf_op jit(solution)/shard_map/ppermute | solution.py:369
  20.5 21.3 %collective-permute-start.9 = (bf16[1024,128]{1,0:T(8,128)(2,1)S(1)}, bf16[1024,128]{1,0:T(8,128)(2,1)S(1)}, u32[]{:S(2)}, u32[]{:S(2)}) collective-permute-start(bf16[1024,128]{1,0:T(8,128)(2,1)S(1)} %get-tuple-element.44), channel_id=1, source_target_pairs={{0,8},{8,16},{16,24},{24,28},{28,20},{20,12},{12,4},{4,0},{1,9},{9... | collective-permute-start | bytes 786440 | tf_op jit(solution)/shard_map/ppermute | solution.py:369
  22.4 21.5 %collective-permute-start.10 = (bf16[1024,128]{1,0:T(8,128)(2,1)S(1)}, bf16[1024,128]{1,0:T(8,128)(2,1)}, u32[]{:S(2)}, u32[]{:S(2)}) collective-permute-start(bf16[1024,128]{1,0:T(8,128)(2,1)S(1)} %get-tuple-element.43), channel_id=1, source_target_pairs={{0,8},{8,16},{16,24},{24,28},{28,20},{20,12},{12,4},{4,0},{1,9},{9... | collective-permute-start | bytes 786440 | tf_op jit(solution)/shard_map/ppermute | solution.py:369
  30.6 59.9 %collective-permute-start.1 = (bf16[2048,128]{1,0:T(8,128)(2,1)}, bf16[2048,128]{1,0:T(8,128)(2,1)S(1)}, u32[]{:S(2)}, u32[]{:S(2)}) collective-permute-start(bf16[2048,128]{1,0:T(8,128)(2,1)} %collective-permute-done.refs_3_), channel_id=1, source_target_pairs={{0,4},{8,0},{16,8},{24,16},{28,24},{20,28},{12,20},{4,12},{1,5},{9... | collective-permute-start | bytes 1572872 | tf_op jit(solution)/shard_map/ppermute | solution.py:369
  31.2 60.5 %collective-permute-start.5 = (bf16[2048,128]{1,0:T(8,128)(2,1)}, bf16[2048,128]{1,0:T(8,128)(2,1)S(1)}, u32[]{:S(2)}, u32[]{:S(2)}) collective-permute-start(bf16[2048,128]{1,0:T(8,128)(2,1)} %collective-permute-done.4.refs_2_), channel_id=1, source_target_pairs={{0,8},{8,16},{16,24},{24,28},{28,20},{20,12},{12,4},{4,0},{1,9},{9... | collective-permute-start | bytes 1572872 | tf_op jit(solution)/shard_map/ppermute | solution.py:369
  41.8 52.0 %collective-permute-start.15 = (bf16[2048,128]{1,0:T(8,128)(2,1)}, bf16[2048,128]{1,0:T(8,128)(2,1)S(1)}, u32[]{:S(2)}, u32[]{:S(2)}) collective-permute-start(bf16[2048,128]{1,0:T(8,128)(2,1)} %collective-permute-done.8.refs_1_), channel_id=1, source_target_pairs={{0,4},{8,0},{16,8},{24,16},{28,24},{20,28},{12,20},{4,12},{1,5},{9... | collective-permute-start | bytes 1572872 | tf_op jit(solution)/shard_map/ppermute | solution.py:369
  41.8 36.7 %collective-permute-start.12 = (bf16[1024,128]{1,0:T(8,128)(2,1)S(1)}, bf16[1024,128]{1,0:T(8,128)(2,1)S(1)}, u32[]{:S(2)}, u32[]{:S(2)}) collective-permute-start(bf16[1024,128]{1,0:T(8,128)(2,1)S(1)} %collective-permute-done.9.refs_1_), channel_id=1, source_target_pairs={{0,8},{8,16},{16,24},{24,28},{28,20},{20,12},{12,4},{4,0},{1,9},{9... | collective-permute-start | bytes 786440 | tf_op jit(solution)/shard_map/ppermute | solution.py:369
  43.9 34.7 %collective-permute-start.13 = (bf16[1024,128]{1,0:T(8,128)(2,1)}, bf16[1024,128]{1,0:T(8,128)(2,1)S(1)}, u32[]{:S(2)}, u32[]{:S(2)}) collective-permute-start(bf16[1024,128]{1,0:T(8,128)(2,1)} %collective-permute-done.10.refs_2_), channel_id=1, source_target_pairs={{0,8},{8,16},{16,24},{24,28},{28,20},{20,12},{12,4},{4,0},{1,9},{9... | collective-permute-start | bytes 786440 | tf_op jit(solution)/shard_map/ppermute | solution.py:369
  56.9 17.4 %copy-start.14 = (s32[8,8,8]{2,1,0:T(8,128)S(1)}, s32[8,8,8]{2,1,0:T(8,128)}, u32[]{:S(2)}) copy-start(s32[8,8,8]{2,1,0:T(8,128)} %param.14) | copy-start | bytes 6148
  76.6 18.5 %copy-start.4 = (bf16[2,2048,1024]{2,1,0:T(8,128)(2,1)S(1)}, bf16[2,2048,1024]{2,1,0:T(8,128)(2,1)}, u32[]{:S(2)}) copy-start(bf16[2,2048,1024]{2,1,0:T(8,128)(2,1)} %copy-done.3) | copy-start | bytes 25165828
  78.6 16.5 %slice-start = ((s8[8388608]{0:T(1024)(128)(4,1)}), s8[4194304]{0:T(1024)(128)(4,1)S(1)}, s32[]{:S(2)}) async-start(s8[8388608]{0:T(1024)(128)(4,1)} %bitcast.2), calls=%async_computation | async-start | bytes 8388608
  79.4 27.6 %collective-permute-start.14 = (bf16[1024,128]{1,0:T(8,128)(2,1)S(1)}, bf16[1024,128]{1,0:T(8,128)(2,1)S(1)}, u32[]{:S(2)}, u32[]{:S(2)}) collective-permute-start(bf16[1024,128]{1,0:T(8,128)(2,1)S(1)} %pick.6), channel_id=1, source_target_pairs={{0,8},{8,16},{16,24},{24,28},{28,20},{20,12},{12,4},{4,0},{1,9},{9... | collective-permute-start | bytes 786440 | tf_op jit(solution)/shard_map/ppermute | solution.py:369
  86.3 8.8 %slice-start.1 = ((s8[8388608]{0:T(1024)(128)(4,1)}), s8[4194304]{0:T(1024)(128)(4,1)S(1)}, s32[]{:S(2)}) async-start(s8[8388608]{0:T(1024)(128)(4,1)} %bitcast.2), calls=%async_computation.1 | async-start | bytes 8388608
  91.0 12.4 %collective-permute-start.2 = (bf16[1024,128]{1,0:T(8,128)(2,1)S(1)}, bf16[1024,128]{1,0:T(8,128)(2,1)S(1)}, u32[]{:S(2)}, u32[]{:S(2)}) collective-permute-start(bf16[1024,128]{1,0:T(8,128)(2,1)S(1)} %pick.4), channel_id=1, source_target_pairs={{0,4},{8,0},{16,8},{24,16},{28,24},{20,28},{12,20},{4,12},{1,5},{9... | collective-permute-start | bytes 786440 | tf_op jit(solution)/shard_map/ppermute | solution.py:369
  92.3 11.2 %collective-permute-start.6 = (bf16[1024,128]{1,0:T(8,128)(2,1)S(1)}, bf16[1024,128]{1,0:T(8,128)(2,1)S(1)}, u32[]{:S(2)}, u32[]{:S(2)}) collective-permute-start(bf16[1024,128]{1,0:T(8,128)(2,1)S(1)} %pick.5), channel_id=1, source_target_pairs={{0,8},{8,16},{16,24},{24,28},{28,20},{20,12},{12,4},{4,0},{1,9},{9... | collective-permute-start | bytes 786440 | tf_op jit(solution)/shard_map/ppermute | solution.py:369
  94.4 12.5 %collective-permute-start.16 = (bf16[1024,128]{1,0:T(8,128)(2,1)S(1)}, bf16[1024,128]{1,0:T(8,128)(2,1)S(1)}, u32[]{:S(2)}, u32[]{:S(2)}) collective-permute-start(bf16[1024,128]{1,0:T(8,128)(2,1)S(1)} %pick.7), channel_id=1, source_target_pairs={{0,4},{8,0},{16,8},{24,16},{28,24},{20,28},{12,20},{4,12},{1,5},{9... | collective-permute-start | bytes 786440 | tf_op jit(solution)/shard_map/ppermute | solution.py:369
  100.1 3.4 %copy-start.2 = (bf16[1,2048,1024]{2,1,0:T(8,128)(2,1)S(1)}, bf16[1,2048,1024]{2,1,0:T(8,128)(2,1)}, u32[]{:S(2)}) copy-start(bf16[1,2048,1024]{2,1,0:T(8,128)(2,1)} %copy-done.1) | copy-start | bytes 12582916
  105.4 9.5 %collective-permute-start.20 = (bf16[512,128]{1,0:T(8,128)(2,1)S(1)}, bf16[512,128]{1,0:T(8,128)(2,1)S(1)}, u32[]{:S(2)}, u32[]{:S(2)}) collective-permute-start(bf16[512,128]{1,0:T(8,128)(2,1)S(1)} %get-tuple-element.41), channel_id=1, source_target_pairs={{0,2},{1,3},{2,0},{3,1},{4,6},{5,7},{6,4},{7,5},{8,10},{9,11},{10,... | collective-permute-start | bytes 393224 | tf_op jit(solution)/shard_map/ppermute | solution.py:446
  106.9 8.5 %collective-permute-start.21 = (bf16[512,128]{1,0:T(8,128)(2,1)S(1)}, bf16[512,128]{1,0:T(8,128)(2,1)S(1)}, u32[]{:S(2)}, u32[]{:S(2)}) collective-permute-start(bf16[512,128]{1,0:T(8,128)(2,1)S(1)} %get-tuple-element.42), channel_id=1, source_target_pairs={{0,3},{1,2},{2,1},{3,0},{4,7},{5,6},{6,5},{7,4},{8,11},{9,10},{10,... | collective-permute-start | bytes 393224 | tf_op jit(solution)/shard_map/ppermute | solution.py:446
  108.8 7.7 %collective-permute-start.18 = (bf16[512,128]{1,0:T(8,128)(2,1)S(1)}, bf16[512,128]{1,0:T(8,128)(2,1)S(1)}, u32[]{:S(2)}, u32[]{:S(2)}) collective-permute-start(bf16[512,128]{1,0:T(8,128)(2,1)S(1)} %get-tuple-element.37), channel_id=1, source_target_pairs={{0,2},{1,3},{2,0},{3,1},{4,6},{5,7},{6,4},{7,5},{8,10},{9,11},{10,... | collective-permute-start | bytes 393224 | tf_op jit(solution)/shard_map/ppermute | solution.py:446
  109.4 8.9 %collective-permute-start.19 = (bf16[512,128]{1,0:T(8,128)(2,1)S(1)}, bf16[512,128]{1,0:T(8,128)(2,1)S(1)}, u32[]{:S(2)}, u32[]{:S(2)}) collective-permute-start(bf16[512,128]{1,0:T(8,128)(2,1)S(1)} %get-tuple-element.38), channel_id=1, source_target_pairs={{0,3},{1,2},{2,1},{3,0},{4,7},{5,6},{6,5},{7,4},{8,11},{9,10},{10,... | collective-permute-start | bytes 393224 | tf_op jit(solution)/shard_map/ppermute | solution.py:446
  112.8 5.5 %collective-permute-start.17 = (bf16[512,128]{1,0:T(8,128)(2,1)S(1)}, bf16[512,128]{1,0:T(8,128)(2,1)S(1)}, u32[]{:S(2)}, u32[]{:S(2)}) collective-permute-start(bf16[512,128]{1,0:T(8,128)(2,1)S(1)} %get-tuple-element.36), channel_id=1, source_target_pairs={{0,1},{1,0},{2,3},{3,2},{4,5},{5,4},{6,7},{7,6},{8,9},{9,8},{10,11... | collective-permute-start | bytes 393224 | tf_op jit(solution)/shard_map/ppermute | solution.py:446
  114.9 3.4 %collective-permute-start.11 = (bf16[512,128]{1,0:T(8,128)(2,1)S(1)}, bf16[512,128]{1,0:T(8,128)(2,1)S(1)}, u32[]{:S(2)}, u32[]{:S(2)}) collective-permute-start(bf16[512,128]{1,0:T(8,128)(2,1)S(1)} %get-tuple-element.34), channel_id=1, source_target_pairs={{0,1},{1,0},{2,3},{3,2},{4,5},{5,4},{6,7},{7,6},{8,9},{9,8},{10,11... | collective-permute-start | bytes 393224 | tf_op jit(solution)/shard_map/ppermute | solution.py:446
  (10 other events, 24.2 us)

commit v5 on v4

--- a/solution.py
+++ b/solution.py
@@ -168,11 +168,11 @@
             totals[part][...] = start_totals[part][...]
 
 
-def finish_kernel(plan, groups, n_sources, n_dense, blocks, pairs, need, *refs):
+def finish_kernel(plan, groups, n_sources, n_dense, blocks, firsts, run, need, *refs):
     sources, refs = refs[:n_sources], refs[n_sources:]
     denses, refs = refs[:n_dense], refs[n_dense:]
     start_total, refs = refs[0], refs[1:]
-    outs, (streamed, feats, total, sem) = refs[: 2 * len(pairs)], refs[2 * len(pairs) :]
+    outs, (streamed, feats, total, sem) = refs[: run * len(firsts)], refs[run * len(firsts) :]
     own = lax.axis_index("feat")
     size = ROWS // blocks
     for e, (operand, index, resident, offset, pieces) in enumerate(plan):
@@ -182,8 +182,8 @@
             feats[e, pl.ds(k * TILE, TILE), :] = value
 
         gather_feats(need, groups, 0, offset, [sources[i] for i in chunks], whole, put)
-    for i, pair in enumerate(pairs):
-        rows = pl.ds(pl.multiple_of((lax.div(own, 2) ^ pair) * 2 * size, 2 * size), 2 * size)
+    for i, first in enumerate(firsts):
+        rows = pl.ds(pl.multiple_of((lax.div(own, run) ^ (first // run)) * run * size, run * size), run * size)
         total[...] = start_total[rows, :]
         for e, (operand, index, resident, offset, pieces) in enumerate(plan):
             if resident:
@@ -194,24 +194,24 @@
                 copy.wait()
                 lhs = streamed[...]
             total[...] += jnp.dot(lhs, feats[e], preferred_element_type=jnp.float32)
-        for low in range(2):
-            block = pl.ds(pl.multiple_of((lax.rem(own, 2) ^ low) * size, size), size)
-            outs[2 * i + low][...] = total[block, :].astype(jnp.bfloat16)
-
-
-def finish(plan, groups, need, sources, denses, start_total, blocks, pairs):
+        for low in range(run):
+            block = pl.ds(pl.multiple_of((lax.rem(own, run) ^ low) * size, size), size)
+            outs[run * i + low][...] = total[block, :].astype(jnp.bfloat16)
+
+
+def finish(plan, groups, need, sources, denses, start_total, blocks, firsts, run):
     width = start_total.shape[1]
     vmem = pl.BlockSpec(memory_space=pltpu.VMEM)
     spaces = [None] * len(denses)
     for operand, index, resident, offset, pieces in plan:
         spaces[operand] = vmem if resident else pl.BlockSpec(memory_space=pl.ANY)
     streams = any(not entry[2] for entry in plan)
-    rows = 2 * ROWS // blocks
+    rows = run * ROWS // blocks
     return pl.pallas_call(
-        functools.partial(finish_kernel, plan, groups, len(sources), len(denses), blocks, pairs),
-        out_shape=[jax.ShapeDtypeStruct((ROWS // blocks, width), jnp.bfloat16)] * (2 * len(pairs)),
+        functools.partial(finish_kernel, plan, groups, len(sources), len(denses), blocks, firsts, run),
+        out_shape=[jax.ShapeDtypeStruct((ROWS // blocks, width), jnp.bfloat16)] * (run * len(firsts)),
         in_specs=[pl.BlockSpec(memory_space=pltpu.SMEM)] + [vmem] * len(sources) + spaces + [vmem],
-        out_specs=[vmem] * (2 * len(pairs)),
+        out_specs=[vmem] * (run * len(firsts)),
         scratch_shapes=[
             pltpu.VMEM((rows, DEPTH) if streams else (8, TILE), jnp.bfloat16),
             pltpu.VMEM((len(plan), DEPTH, width), jnp.bfloat16),
@@ -220,8 +220,8 @@
         ],
         compiler_params=pltpu.CompilerParams(vmem_limit_bytes=STREAM_LIMIT if streams else RESIDENT_LIMIT),
         cost_estimate=pl.CostEstimate(
-            flops=2 * len(plan) * len(pairs) * rows * DEPTH * width,
-            bytes_accessed=2 * len(plan) * len(pairs) * rows * DEPTH,
+            flops=2 * len(plan) * len(firsts) * rows * DEPTH * width,
+            bytes_accessed=2 * len(plan) * len(firsts) * rows * DEPTH,
             transcendentals=0,
         ),
         name="finish",
@@ -397,7 +397,7 @@
             upto = next((e for e in range(d + 1, far + 1) if e == 2 or is_resident(e) != is_resident(d)), far + 1)
             dense += densify(stages[d:upto], is_resident(d), groups, table, tiles)
 
-    def add(totals, entries, columns, pairs=None):
+    def add(totals, entries, columns, firsts=None, run=1):
         sources, operands, plan = [], [], []
         for way, d, parts in entries:
             if d not in operands:
@@ -411,9 +411,9 @@
             index = stages[d].index(offset) if d < far else 0
             plan.append((operands.index(d), index, is_resident(d), offset, tuple(pieces)))
         sizes = tuple(widths[c] for c in columns)
-        if pairs is not None:
+        if firsts is not None:
             arrays = [dense[d] for d in operands]
-            return finish(tuple(plan), groups, need, sources, arrays, totals[0], blocks, pairs)
+            return finish(tuple(plan), groups, need, sources, arrays, totals[0], blocks, firsts, run)
         return aggregate(tuple(plan), groups, need, sources, [dense[d] for d in operands], totals, sizes)
 
     every = list(range(cuts))
@@ -435,10 +435,19 @@
         ends = [(totals[0], [(1, far, every)])]
 
     finished = {}
-    for c, (total, entries) in enumerate(ends):
-        for pairs in (tuple(range(1, blocks // 2)), (0,)):
-            for pair, outs in zip(pairs, halves(add([total], entries, [c], pairs) if pairs else [])):
-                finished[c, 2 * pair], finished[c, 2 * pair + 1] = outs
+
+    def complete(c, firsts, run):
+        if firsts:
+            outs = add([ends[c][0]], ends[c][1], [c], firsts, run)
+            finished.update({(c, m + low): outs[run * i + low] for i, m in enumerate(firsts) for low in range(run)})
+
+    for c in range(cuts):
+        if c < last:
+            for m in reversed(range(2, blocks)):
+                complete(c, (m,), 1)
+        else:
+            complete(c, tuple(range(2, blocks, 2)), 2)
+        complete(c, (0,), 2)
 
     def exchange(c, m):
         if m == 0:
@@ -447,18 +456,14 @@
 
     order = [(c, m) for c in range(cuts) for m in reversed(range(blocks))]
     arrived = {key: exchange(*key) for key in order}
-    soon = [(c, 0) for c in range(cuts)] + [(c, m) for c in range(last) for m in range(2, blocks)]
-    late = [(c, 1) for c in range(cuts)] + [(last, m) for m in range(2, blocks)]
+    soon = [(c, m) for m in range(2) for c in range(cuts)] + [(c, m) for c in range(last) for m in range(2, blocks)]
+    late = [(last, m) for m in range(2, blocks)]
 
     def multiply(keys, start_total, final):
         starts = tuple((m, c * part) for c, m in keys)
         return product([arrived[key] for key in keys], starts, width, weight, start_total, final)
 
     return multiply(late, multiply(soon, None, False), True)
-
-
-def halves(outs):
-    return [(outs[i], outs[i + 1]) for i in range(0, len(outs), 2)]
 
 
 def part_count(width):

time: 121 us -> 124 us (1.025)
  waiting for transfers between devices: 28.7 us -> 31.7 us
    ppermute x6, waiting for transfers between devices: 2.23 us -> 5.29 us  [exchange(): lax.ppermute(finished[c, m], 'feat', [(f, f ^ m) for f in range(blocks)])]
    pallas_call x4 -> x5, Pallas kernels: 7.48 us -> 8.25 us  [finish(): pl.pallas_call(functools.partial(finish_kernel, plan, groups, len(sources...]
where the time goes in v5:
time: 124 us
  Pallas kernels  42 us (34%)
  waiting for transfers between devices  31.7 us (26%)
  local copies, waits for them, and re-layouts  24.2 us (20%)
  starting transfers between devices  24.2 us (20%)
    ppermute x16, waiting for transfers between devices, send(): return lax.ppermute(array, 'rows', ring_pairs(groups, way))  26.4 us
    unnamed x40, local copies, waits for them, and re-layouts  21.6 us
    ppermute x16, starting transfers between devices, send(): return lax.ppermute(array, 'rows', ring_pairs(groups, way))  20.1 us
    pallas_call x2, Pallas kernels, densify(): pl.pallas_call(functools.partial(densify_kernel, stages, resident, groups...  14.5 us
    pallas_call x4, Pallas kernels, aggregate(): pl.pallas_call(functools.partial(aggregate_kernel, plan, groups, len(sour...  14.4 us
    pallas_call x5, Pallas kernels, finish(): pl.pallas_call(functools.partial(finish_kernel, plan, groups, len(sources...  8.25 us
    ppermute x6, waiting for transfers between devices, exchange(): lax.ppermute(finished[c, m], 'feat', [(f, f ^ m) for f in range(blocks)])  5.29 us
    ppermute x6, starting transfers between devices, exchange(): lax.ppermute(finished[c, m], 'feat', [(f, f ^ m) for f in range(blocks)])  4.14 us
  transfers between devices with their start and end apart: 22, of which 7 were waited for; matrix products, arithmetic and copies ran while one was open for 1% of the time, Pallas kernels for 33%

profile of v5, /device:TPU:0, one launch (start us, length us, event | category | flops | bytes accessed | tf_op | source)
XLA Modules:
  0.0 123.7 jit_solution(9325499914816553622)
XLA Ops:
  1.3 3.1 %collective-permute-start.11 = (bf16[2048,128]{1,0:T(8,128)(2,1)S(1)}, bf16[2048,128]{1,0:T(8,128)(2,1)S(1)}, u32[]{:S(2)}, u32[]{:S(2)}) collective-permute-start(bf16[2048,128]{1,0:T(8,128)(2,1)S(1)} %get-tuple-element.39.refs_0_), channel_id=1, source_target_pairs={{0,8},{8,16},{16,24},{24,28},{28,20},{20,12},{12,4},{4,0},{1,9},{9... | collective-permute-start | bytes 1572872 | tf_op jit(solution)/shard_map/ppermute | solution.py:369
  4.4 2.0 %collective-permute-start.9 = (bf16[2048,128]{1,0:T(8,128)(2,1)S(1)}, bf16[2048,128]{1,0:T(8,128)(2,1)}, u32[]{:S(2)}, u32[]{:S(2)}) collective-permute-start(bf16[2048,128]{1,0:T(8,128)(2,1)S(1)} %get-tuple-element.39.refs_0_), channel_id=1, source_target_pairs={{0,4},{8,0},{16,8},{24,16},{28,24},{20,28},{12,20},{4,12},{1,5},{9... | collective-permute-start | bytes 1572872 | tf_op jit(solution)/shard_map/ppermute | solution.py:369
  6.4 9.9 %collective-permute-done.11.refs_0_ = bf16[2048,128]{1,0:T(8,128)(2,1)S(1)} collective-permute-done((bf16[2048,128]{1,0:T(8,128)(2,1)S(1)}, bf16[2048,128]{1,0:T(8,128)(2,1)S(1)}, u32[]{:S(2)}, u32[]{:S(2)}) %collective-permute-start.11) | collective-permute-done | bytes 524320 | tf_op jit(solution)/shard_map/ppermute | solution.py:369
  16.3 1.8 %collective-permute-start.12 = (bf16[2048,128]{1,0:T(8,128)(2,1)S(1)}, bf16[2048,128]{1,0:T(8,128)(2,1)}, u32[]{:S(2)}, u32[]{:S(2)}) collective-permute-start(bf16[2048,128]{1,0:T(8,128)(2,1)S(1)} %collective-permute-done.11.refs_0_), channel_id=1, source_target_pairs={{0,8},{8,16},{16,24},{24,28},{28,20},{20,12},{12,4},{4,0},{1,9},{9... | collective-permute-start | bytes 1572872 | tf_op jit(solution)/shard_map/ppermute | solution.py:369
  20.5 1.9 %collective-permute-start = (bf16[1024,128]{1,0:T(8,128)(2,1)S(1)}, bf16[1024,128]{1,0:T(8,128)(2,1)S(1)}, u32[]{:S(2)}, u32[]{:S(2)}) collective-permute-start(bf16[1024,128]{1,0:T(8,128)(2,1)S(1)} %get-tuple-element.42), channel_id=1, source_target_pairs={{0,8},{8,16},{16,24},{24,28},{28,20},{20,12},{12,4},{4,0},{1,9},{9... | collective-permute-start | bytes 786440 | tf_op jit(solution)/shard_map/ppermute | solution.py:369
  22.4 1.6 %collective-permute-start.2 = (bf16[1024,128]{1,0:T(8,128)(2,1)S(1)}, bf16[1024,128]{1,0:T(8,128)(2,1)}, u32[]{:S(2)}, u32[]{:S(2)}) collective-permute-start(bf16[1024,128]{1,0:T(8,128)(2,1)S(1)} %get-tuple-element.41), channel_id=1, source_target_pairs={{0,8},{8,16},{16,24},{24,28},{28,20},{20,12},{12,4},{4,0},{1,9},{9... | collective-permute-start | bytes 786440 | tf_op jit(solution)/shard_map/ppermute | solution.py:369
  24.6 6.0 %collective-permute-done.9.refs_3_ = bf16[2048,128]{1,0:T(8,128)(2,1)} collective-permute-done((bf16[2048,128]{1,0:T(8,128)(2,1)S(1)}, bf16[2048,128]{1,0:T(8,128)(2,1)}, u32[]{:S(2)}, u32[]{:S(2)}) %collective-permute-start.9) | collective-permute-done | bytes 524320 | tf_op jit(solution)/shard_map/ppermute | solution.py:369
  31.2 1.8 %collective-permute-start.13 = (bf16[2048,128]{1,0:T(8,128)(2,1)}, bf16[2048,128]{1,0:T(8,128)(2,1)S(1)}, u32[]{:S(2)}, u32[]{:S(2)}) collective-permute-start(bf16[2048,128]{1,0:T(8,128)(2,1)} %collective-permute-done.12.refs_2_), channel_id=1, source_target_pairs={{0,8},{8,16},{16,24},{24,28},{28,20},{20,12},{12,4},{4,0},{1,9},{9... | collective-permute-start | bytes 1572872 | tf_op jit(solution)/shard_map/ppermute | solution.py:369
  33.0 8.8 %collective-permute-done.6.refs_1_ = bf16[2048,128]{1,0:T(8,128)(2,1)} collective-permute-done((bf16[2048,128]{1,0:T(8,128)(2,1)S(1)}, bf16[2048,128]{1,0:T(8,128)(2,1)}, u32[]{:S(2)}, u32[]{:S(2)}) %collective-permute-start.6) | collective-permute-done | bytes 524320 | tf_op jit(solution)/shard_map/ppermute | solution.py:369
  41.8 2.1 %collective-permute-start.1 = (bf16[1024,128]{1,0:T(8,128)(2,1)S(1)}, bf16[1024,128]{1,0:T(8,128)(2,1)S(1)}, u32[]{:S(2)}, u32[]{:S(2)}) collective-permute-start(bf16[1024,128]{1,0:T(8,128)(2,1)S(1)} %collective-permute-done.refs_1_), channel_id=1, source_target_pairs={{0,8},{8,16},{16,24},{24,28},{28,20},{20,12},{12,4},{4,0},{1,9},{9... | collective-permute-start | bytes 786440 | tf_op jit(solution)/shard_map/ppermute | solution.py:369
  43.9 1.6 %collective-permute-start.3 = (bf16[1024,128]{1,0:T(8,128)(2,1)}, bf16[1024,128]{1,0:T(8,128)(2,1)S(1)}, u32[]{:S(2)}, u32[]{:S(2)}) collective-permute-start(bf16[1024,128]{1,0:T(8,128)(2,1)} %collective-permute-done.2.refs_2_), channel_id=1, source_target_pairs={{0,8},{8,16},{16,24},{24,28},{28,20},{20,12},{12,4},{4,0},{1,9},{9... | collective-permute-start | bytes 786440 | tf_op jit(solution)/shard_map/ppermute | solution.py:369
  45.9 5.7 %densify.3 = (bf16[1,2048,1024]{2,1,0:T(8,128)(2,1)S(1)}, bf16[2,2048,1024]{2,1,0:T(8,128)(2,1)S(1)}) custom-call(s32[1024]{0:T(1024)S(1)} %select_reduce_fusion.table, bf16[640,128,128]{2,1,0:T(8,128)(2,1)} %tiles.3), custom_call_target="tpu_custom_call" | custom-call | bytes 12582912 | tf_op jit(solution)/shard_map/densify/pallas_call | solution.py:86
  51.6 3.3 %copy-done.5 = bf16[2,2048,1024]{2,1,0:T(8,128)(2,1)} copy-done((bf16[2,2048,1024]{2,1,0:T(8,128)(2,1)}, bf16[2,2048,1024]{2,1,0:T(8,128)(2,1)S(1)}, u32[]{:S(2)}) %copy-start.5) | copy-done | bytes 8388632
  54.9 2.0 %copy-done.8 = bf16[1,2048,1024]{2,1,0:T(8,128)(2,1)} copy-done((bf16[1,2048,1024]{2,1,0:T(8,128)(2,1)}, bf16[1,2048,1024]{2,1,0:T(8,128)(2,1)S(1)}, u32[]{:S(2)}) %copy-start.8) | copy-done | bytes 4194328
  56.9 8.8 %densify.2 = (bf16[2,2048,1024]{2,1,0:T(8,128)(2,1)S(1)}, bf16[2,2048,1024]{2,1,0:T(8,128)(2,1)S(1)}, bf16[1,2048,1024]{2,1,0:T(8,128)(2,1)S(1)}) custom-call(s32[1024]{0:T(1024)S(1)} %select_reduce_fusion.table, bf16[640,128,128]{2,1,0:T(8,128)(2,1)} %tiles.3), custom_call_target="tpu_custom_call" | custom-call | bytes 20971520 | tf_op jit(solution)/shard_map/densify/pallas_call | solution.py:86
  65.7 3.3 %copy-done = bf16[2,2048,1024]{2,1,0:T(8,128)(2,1)} copy-done((bf16[2,2048,1024]{2,1,0:T(8,128)(2,1)}, bf16[2,2048,1024]{2,1,0:T(8,128)(2,1)S(1)}, u32[]{:S(2)}) %copy-start) | copy-done | bytes 8388632
  68.9 2.1 %copy-done.1 = bf16[1,2048,1024]{2,1,0:T(8,128)(2,1)} copy-done((bf16[1,2048,1024]{2,1,0:T(8,128)(2,1)}, bf16[1,2048,1024]{2,1,0:T(8,128)(2,1)S(1)}, u32[]{:S(2)}) %copy-start.1) | copy-done | bytes 4194328
  71.0 3.3 %copy-done.3 = bf16[2,2048,1024]{2,1,0:T(8,128)(2,1)} copy-done((bf16[2,2048,1024]{2,1,0:T(8,128)(2,1)}, bf16[2,2048,1024]{2,1,0:T(8,128)(2,1)S(1)}, u32[]{:S(2)}) %copy-start.3) | copy-done | bytes 8388632
  74.4 2.2 %copy-done.9 = bf16[1,2048,1024]{2,1,0:T(8,128)(2,1)S(1)} copy-done((bf16[1,2048,1024]{2,1,0:T(8,128)(2,1)S(1)}, bf16[1,2048,1024]{2,1,0:T(8,128)(2,1)}, u32[]{:S(2)}) %copy-start.9) | copy-done | bytes 4194328
  76.6 2.0 %aggregate.4 = (f32[2048,128]{1,0:T(8,128)S(1)}, f32[2048,128]{1,0:T(8,128)S(1)}) custom-call(s32[512]{0:T(512)S(1)} %reshape.9.need, bf16[2048,128]{1,0:T(8,128)(2,1)S(1)} %get-tuple-element.39.refs_0_, bf16[2048,128]{1,0:T(8,128)(2,1)S(1)} %get-tuple-element.40.refs_1_, bf16[1,2048,1024]{2,1,0:T(8,128)(2,1)S(1)} %copy-done.9), custom_call_target="tpu_custom_call" | custom-call | flops 1073741824 | bytes 4194304 | tf_op jit(solution)/shard_map/aggregate/pallas_call | solution.py:253
  79.3 1.5 %collective-permute-start.4 = (bf16[1024,128]{1,0:T(8,128)(2,1)S(1)}, bf16[1024,128]{1,0:T(8,128)(2,1)S(1)}, u32[]{:S(2)}, u32[]{:S(2)}) collective-permute-start(bf16[1024,128]{1,0:T(8,128)(2,1)S(1)} %pick.4), channel_id=1, source_target_pairs={{0,8},{8,16},{16,24},{24,28},{28,20},{20,12},{12,4},{4,0},{1,9},{9... | collective-permute-start | bytes 786440 | tf_op jit(solution)/shard_map/ppermute | solution.py:369
  80.8 3.4 %copy-done.6 = bf16[2,2048,1024]{2,1,0:T(8,128)(2,1)S(1)} copy-done((bf16[2,2048,1024]{2,1,0:T(8,128)(2,1)S(1)}, bf16[2,2048,1024]{2,1,0:T(8,128)(2,1)}, u32[]{:S(2)}) %copy-start.6) | copy-done | bytes 8388632
  86.3 4.1 %aggregate.5 = (f32[2048,128]{1,0:T(8,128)S(1)}, f32[2048,128]{1,0:T(8,128)S(1)}) custom-call(s32[512]{0:T(512)S(1)} %reshape.9.need, bf16[2048,128]{1,0:T(8,128)(2,1)S(1)} %copy-done.11, bf16[1024,128]{1,0:T(8,128)(2,1)S(1)} %collective-permute-done.refs_1_, bf16[1024,128]{1,0:T(8,128)(2,1)} %collective-permute-done.2.refs_2_, ...), custom_call_target="tpu_custom_call" | custom-call | flops 2147483648 | bytes 8388608 | tf_op jit(solution)/shard_map/aggregate/pallas_call | solution.py:253
  92.3 1.5 %collective-permute-start.17 = (bf16[1024,128]{1,0:T(8,128)(2,1)S(1)}, bf16[1024,128]{1,0:T(8,128)(2,1)S(1)}, u32[]{:S(2)}, u32[]{:S(2)}) collective-permute-start(bf16[1024,128]{1,0:T(8,128)(2,1)S(1)} %pick.7), channel_id=1, source_target_pairs={{0,8},{8,16},{16,24},{24,28},{28,20},{20,12},{12,4},{4,0},{1,9},{9... | collective-permute-start | bytes 786440 | tf_op jit(solution)/shard_map/ppermute | solution.py:369
  95.1 5.0 %aggregate.6 = (f32[2048,128]{1,0:T(8,128)S(1)}, f32[2048,128]{1,0:T(8,128)S(1)}) custom-call(s32[512]{0:T(512)S(1)} %reshape.9.need, bf16[2048,128]{1,0:T(8,128)(2,1)S(1)} %collective-permute-done.10.refs_0_, bf16[2048,128]{1,0:T(8,128)(2,1)} %collective-permute-done.6.refs_1_, bf16[2048,128]{1,0:T(8,128)(2,1)} %collective-permute-done.12.refs_2_, ...), custom_call_target="tpu_custom_call" | custom-call | flops 2147483648 | bytes 12582912 | tf_op jit(solution)/shard_map/aggregate/pallas_call | solution.py:253
  100.1 3.4 %aggregate.7.refs_4_ = f32[2048,128]{1,0:T(8,128)S(1)} custom-call(s32[512]{0:T(512)S(1)} %reshape.9.need, bf16[1024,128]{1,0:T(8,128)(2,1)S(1)} %collective-permute-done.1.refs_0_, bf16[1024,128]{1,0:T(8,128)(2,1)S(1)} %collective-permute-done.3.refs_1_, bf16[2048,128]{1,0:T(8,128)(2,1)S(1)} %collective-permute-done.7.refs_0_.refs_2_, ...), custom_call_target="tpu_custom_call" | custom-call | flops 1073741824 | bytes 8388608 | tf_op jit(solution)/shard_map/aggregate/pallas_call | solution.py:253
  106.2 1.6 %collective-permute-start.20 = (bf16[512,128]{1,0:T(8,128)(2,1)S(1)}, bf16[512,128]{1,0:T(8,128)(2,1)S(1)}, u32[]{:S(2)}, u32[]{:S(2)}) collective-permute-start(bf16[512,128]{1,0:T(8,128)(2,1)S(1)} %finish.8), channel_id=1, source_target_pairs={{0,2},{1,3},{2,0},{3,1},{4,6},{5,7},{6,4},{7,5},{8,10},{9,11},{10,... | collective-permute-start | bytes 393224 | tf_op jit(solution)/shard_map/ppermute | solution.py:455
  107.8 1.9 %finish.7 = (bf16[512,128]{1,0:T(8,128)(2,1)S(1)}, bf16[512,128]{1,0:T(8,128)(2,1)S(1)}) custom-call(s32[512]{0:T(512)S(1)} %reshape.9.need, bf16[1024,128]{1,0:T(8,128)(2,1)S(1)} %collective-permute-done.4.refs_0_, bf16[1024,128]{1,0:T(8,128)(2,1)S(1)} %collective-permute-done.8.refs_1_, bf16[2,2048,1024]{2,1,0:T(8,128)(2,1)S(1)} %bitcast.3, ...), custom_call_target="tpu_custom_call" | custom-call | flops 536870912 | bytes 4194304 | tf_op jit(solution)/shard_map/finish/pallas_call | solution.py:210
  110.1 1.9 %finish.6 = (bf16[512,128]{1,0:T(8,128)(2,1)S(1)}, bf16[512,128]{1,0:T(8,128)(2,1)S(1)}) custom-call(s32[512]{0:T(512)S(1)} %reshape.9.need, bf16[1024,128]{1,0:T(8,128)(2,1)S(1)} %collective-permute-done.16.refs_0_, bf16[1024,128]{1,0:T(8,128)(2,1)S(1)} %collective-permute-done.17.refs_1_, bf16[2,2048,1024]{2,1,0:T(8,128)(2,1)S(1)} %bitcast.3, ...), custom_call_target="tpu_custom_call" | custom-call | flops 536870912 | bytes 4194304 | tf_op jit(solution)/shard_map/finish/pallas_call | solution.py:210
  112.2 1.9 %finish.5 = (bf16[512,128]{1,0:T(8,128)(2,1)S(1)}, bf16[512,128]{1,0:T(8,128)(2,1)S(1)}) custom-call(s32[512]{0:T(512)S(1)} %reshape.9.need, bf16[1024,128]{1,0:T(8,128)(2,1)S(1)} %collective-permute-done.4.refs_0_, bf16[1024,128]{1,0:T(8,128)(2,1)S(1)} %collective-permute-done.8.refs_1_, bf16[2,2048,1024]{2,1,0:T(8,128)(2,1)S(1)} %bitcast.3, ...), custom_call_target="tpu_custom_call" | custom-call | flops 536870912 | bytes 4194304 | tf_op jit(solution)/shard_map/finish/pallas_call | solution.py:210
  117.0 3.6 %collective-permute-done.14.refs_0_ = bf16[512,128]{1,0:T(8,128)(2,1)S(1)} collective-permute-done((bf16[512,128]{1,0:T(8,128)(2,1)S(1)}, bf16[512,128]{1,0:T(8,128)(2,1)S(1)}, u32[]{:S(2)}, u32[]{:S(2)}) %collective-permute-start.14) | collective-permute-done | bytes 131104 | tf_op jit(solution)/shard_map/ppermute | solution.py:455
  120.6 1.7 %collective-permute-done.15.refs_1_ = bf16[512,128]{1,0:T(8,128)(2,1)S(1)} collective-permute-done((bf16[512,128]{1,0:T(8,128)(2,1)S(1)}, bf16[512,128]{1,0:T(8,128)(2,1)S(1)}, u32[]{:S(2)}, u32[]{:S(2)}) %collective-permute-start.15) | collective-permute-done | bytes 131104 | tf_op jit(solution)/shard_map/ppermute | solution.py:455
  (75 shorter events, 18.4 us)
Async XLA Ops:
  0.0 41.8 %copy-start.16 = (s32[640]{0:T(1024)S(1)}, s32[640]{0:T(1024)}, u32[]{:S(2)}) copy-start(s32[640]{0:T(1024)} %param.10) | copy-start | bytes 7684
  0.0 41.8 %copy-start.17 = (s32[640]{0:T(1024)S(1)}, s32[640]{0:T(1024)}, u32[]{:S(2)}) copy-start(s32[640]{0:T(1024)} %param.11) | copy-start | bytes 7684
  0.0 41.8 %copy-start.15 = (s32[640]{0:T(1024)S(1)}, s32[640]{0:T(1024)}, u32[]{:S(2)}) copy-start(s32[640]{0:T(1024)} %param.12) | copy-start | bytes 7684
  1.3 15.0 %collective-permute-start.11 = (bf16[2048,128]{1,0:T(8,128)(2,1)S(1)}, bf16[2048,128]{1,0:T(8,128)(2,1)S(1)}, u32[]{:S(2)}, u32[]{:S(2)}) collective-permute-start(bf16[2048,128]{1,0:T(8,128)(2,1)S(1)} %get-tuple-element.39.refs_0_), channel_id=1, source_target_pairs={{0,8},{8,16},{16,24},{24,28},{28,20},{20,12},{12,4},{4,0},{1,9},{9... | collective-permute-start | bytes 1572872 | tf_op jit(solution)/shard_map/ppermute | solution.py:369
  4.4 14.8 %collective-permute-start.5 = (bf16[2048,128]{1,0:T(8,128)(2,1)S(1)}, bf16[2048,128]{1,0:T(8,128)(2,1)S(1)}, u32[]{:S(2)}, u32[]{:S(2)}) collective-permute-start(bf16[2048,128]{1,0:T(8,128)(2,1)S(1)} %get-tuple-element.40.refs_1_), channel_id=1, source_target_pairs={{0,4},{8,0},{16,8},{24,16},{28,24},{20,28},{12,20},{4,12},{1,5},{9... | collective-permute-start | bytes 1572872 | tf_op jit(solution)/shard_map/ppermute | solution.py:369
  4.4 26.1 %collective-permute-start.9 = (bf16[2048,128]{1,0:T(8,128)(2,1)S(1)}, bf16[2048,128]{1,0:T(8,128)(2,1)}, u32[]{:S(2)}, u32[]{:S(2)}) collective-permute-start(bf16[2048,128]{1,0:T(8,128)(2,1)S(1)} %get-tuple-element.39.refs_0_), channel_id=1, source_target_pairs={{0,4},{8,0},{16,8},{24,16},{28,24},{20,28},{12,20},{4,12},{1,5},{9... | collective-permute-start | bytes 1572872 | tf_op jit(solution)/shard_map/ppermute | solution.py:369
  16.3 14.3 %copy-start.10 = (bf16[2048,128]{1,0:T(8,128)(2,1)}, bf16[2048,128]{1,0:T(8,128)(2,1)S(1)}, u32[]{:S(2)}) copy-start(bf16[2048,128]{1,0:T(8,128)(2,1)S(1)} %collective-permute-done.11.refs_0_) | copy-start | bytes 1572868
  16.3 14.9 %collective-permute-start.12 = (bf16[2048,128]{1,0:T(8,128)(2,1)S(1)}, bf16[2048,128]{1,0:T(8,128)(2,1)}, u32[]{:S(2)}, u32[]{:S(2)}) collective-permute-start(bf16[2048,128]{1,0:T(8,128)(2,1)S(1)} %collective-permute-done.11.refs_0_), channel_id=1, source_target_pairs={{0,8},{8,16},{16,24},{24,28},{28,20},{20,12},{12,4},{4,0},{1,9},{9... | collective-permute-start | bytes 1572872 | tf_op jit(solution)/shard_map/ppermute | solution.py:369
  19.2 13.8 %copy-start.12 = (bf16[2048,128]{1,0:T(8,128)(2,1)}, bf16[2048,128]{1,0:T(8,128)(2,1)S(1)}, u32[]{:S(2)}) copy-start(bf16[2048,128]{1,0:T(8,128)(2,1)S(1)} %collective-permute-done.5.refs_4_) | copy-start | bytes 1572868
  19.2 22.6 %collective-permute-start.6 = (bf16[2048,128]{1,0:T(8,128)(2,1)S(1)}, bf16[2048,128]{1,0:T(8,128)(2,1)}, u32[]{:S(2)}, u32[]{:S(2)}) collective-permute-start(bf16[2048,128]{1,0:T(8,128)(2,1)S(1)} %collective-permute-done.5.refs_4_), channel_id=1, source_target_pairs={{0,4},{8,0},{16,8},{24,16},{28,24},{20,28},{12,20},{4,12},{1,5},{9... | collective-permute-start | bytes 1572872 | tf_op jit(solution)/shard_map/ppermute | solution.py:369
  20.5 21.3 %collective-permute-start = (bf16[1024,128]{1,0:T(8,128)(2,1)S(1)}, bf16[1024,128]{1,0:T(8,128)(2,1)S(1)}, u32[]{:S(2)}, u32[]{:S(2)}) collective-permute-start(bf16[1024,128]{1,0:T(8,128)(2,1)S(1)} %get-tuple-element.42), channel_id=1, source_target_pairs={{0,8},{8,16},{16,24},{24,28},{28,20},{20,12},{12,4},{4,0},{1,9},{9... | collective-permute-start | bytes 786440 | tf_op jit(solution)/shard_map/ppermute | solution.py:369
  22.4 21.5 %collective-permute-start.2 = (bf16[1024,128]{1,0:T(8,128)(2,1)S(1)}, bf16[1024,128]{1,0:T(8,128)(2,1)}, u32[]{:S(2)}, u32[]{:S(2)}) collective-permute-start(bf16[1024,128]{1,0:T(8,128)(2,1)S(1)} %get-tuple-element.41), channel_id=1, source_target_pairs={{0,8},{8,16},{16,24},{24,28},{28,20},{20,12},{12,4},{4,0},{1,9},{9... | collective-permute-start | bytes 786440 | tf_op jit(solution)/shard_map/ppermute | solution.py:369
  30.6 59.8 %collective-permute-start.10 = (bf16[2048,128]{1,0:T(8,128)(2,1)}, bf16[2048,128]{1,0:T(8,128)(2,1)S(1)}, u32[]{:S(2)}, u32[]{:S(2)}) collective-permute-start(bf16[2048,128]{1,0:T(8,128)(2,1)} %collective-permute-done.9.refs_3_), channel_id=1, source_target_pairs={{0,4},{8,0},{16,8},{24,16},{28,24},{20,28},{12,20},{4,12},{1,5},{9... | collective-permute-start | bytes 1572872 | tf_op jit(solution)/shard_map/ppermute | solution.py:369
  31.2 60.5 %collective-permute-start.13 = (bf16[2048,128]{1,0:T(8,128)(2,1)}, bf16[2048,128]{1,0:T(8,128)(2,1)S(1)}, u32[]{:S(2)}, u32[]{:S(2)}) collective-permute-start(bf16[2048,128]{1,0:T(8,128)(2,1)} %collective-permute-done.12.refs_2_), channel_id=1, source_target_pairs={{0,8},{8,16},{16,24},{24,28},{28,20},{20,12},{12,4},{4,0},{1,9},{9... | collective-permute-start | bytes 1572872 | tf_op jit(solution)/shard_map/ppermute | solution.py:369
  41.8 52.0 %collective-permute-start.7 = (bf16[2048,128]{1,0:T(8,128)(2,1)}, bf16[2048,128]{1,0:T(8,128)(2,1)S(1)}, u32[]{:S(2)}, u32[]{:S(2)}) collective-permute-start(bf16[2048,128]{1,0:T(8,128)(2,1)} %collective-permute-done.6.refs_1_), channel_id=1, source_target_pairs={{0,4},{8,0},{16,8},{24,16},{28,24},{20,28},{12,20},{4,12},{1,5},{9... | collective-permute-start | bytes 1572872 | tf_op jit(solution)/shard_map/ppermute | solution.py:369
  41.8 36.7 %collective-permute-start.1 = (bf16[1024,128]{1,0:T(8,128)(2,1)S(1)}, bf16[1024,128]{1,0:T(8,128)(2,1)S(1)}, u32[]{:S(2)}, u32[]{:S(2)}) collective-permute-start(bf16[1024,128]{1,0:T(8,128)(2,1)S(1)} %collective-permute-done.refs_1_), channel_id=1, source_target_pairs={{0,8},{8,16},{16,24},{24,28},{28,20},{20,12},{12,4},{4,0},{1,9},{9... | collective-permute-start | bytes 786440 | tf_op jit(solution)/shard_map/ppermute | solution.py:369
  43.9 34.7 %collective-permute-start.3 = (bf16[1024,128]{1,0:T(8,128)(2,1)}, bf16[1024,128]{1,0:T(8,128)(2,1)S(1)}, u32[]{:S(2)}, u32[]{:S(2)}) collective-permute-start(bf16[1024,128]{1,0:T(8,128)(2,1)} %collective-permute-done.2.refs_2_), channel_id=1, source_target_pairs={{0,8},{8,16},{16,24},{24,28},{28,20},{20,12},{12,4},{4,0},{1,9},{9... | collective-permute-start | bytes 786440 | tf_op jit(solution)/shard_map/ppermute | solution.py:369
  56.9 17.4 %copy-start.14 = (s32[8,8,8]{2,1,0:T(8,128)S(1)}, s32[8,8,8]{2,1,0:T(8,128)}, u32[]{:S(2)}) copy-start(s32[8,8,8]{2,1,0:T(8,128)} %param.14) | copy-start | bytes 6148
  76.6 18.5 %copy-start.4 = (bf16[2,2048,1024]{2,1,0:T(8,128)(2,1)S(1)}, bf16[2,2048,1024]{2,1,0:T(8,128)(2,1)}, u32[]{:S(2)}) copy-start(bf16[2,2048,1024]{2,1,0:T(8,128)(2,1)} %copy-done.3) | copy-start | bytes 25165828
  78.6 16.5 %slice-start = ((s8[8388608]{0:T(1024)(128)(4,1)}), s8[4194304]{0:T(1024)(128)(4,1)S(1)}, s32[]{:S(2)}) async-start(s8[8388608]{0:T(1024)(128)(4,1)} %bitcast.2), calls=%async_computation | async-start | bytes 8388608
  79.3 28.4 %collective-permute-start.4 = (bf16[1024,128]{1,0:T(8,128)(2,1)S(1)}, bf16[1024,128]{1,0:T(8,128)(2,1)S(1)}, u32[]{:S(2)}, u32[]{:S(2)}) collective-permute-start(bf16[1024,128]{1,0:T(8,128)(2,1)S(1)} %pick.4), channel_id=1, source_target_pairs={{0,8},{8,16},{16,24},{24,28},{28,20},{20,12},{12,4},{4,0},{1,9},{9... | collective-permute-start | bytes 786440 | tf_op jit(solution)/shard_map/ppermute | solution.py:369
  86.3 8.8 %slice-start.1 = ((s8[8388608]{0:T(1024)(128)(4,1)}), s8[4194304]{0:T(1024)(128)(4,1)S(1)}, s32[]{:S(2)}) async-start(s8[8388608]{0:T(1024)(128)(4,1)} %bitcast.2), calls=%async_computation.1 | async-start | bytes 8388608
  91.0 12.4 %collective-permute-start.16 = (bf16[1024,128]{1,0:T(8,128)(2,1)S(1)}, bf16[1024,128]{1,0:T(8,128)(2,1)S(1)}, u32[]{:S(2)}, u32[]{:S(2)}) collective-permute-start(bf16[1024,128]{1,0:T(8,128)(2,1)S(1)} %pick.6), channel_id=1, source_target_pairs={{0,4},{8,0},{16,8},{24,16},{28,24},{20,28},{12,20},{4,12},{1,5},{9... | collective-permute-start | bytes 786440 | tf_op jit(solution)/shard_map/ppermute | solution.py:369
  92.3 11.2 %collective-permute-start.17 = (bf16[1024,128]{1,0:T(8,128)(2,1)S(1)}, bf16[1024,128]{1,0:T(8,128)(2,1)S(1)}, u32[]{:S(2)}, u32[]{:S(2)}) collective-permute-start(bf16[1024,128]{1,0:T(8,128)(2,1)S(1)} %pick.7), channel_id=1, source_target_pairs={{0,8},{8,16},{16,24},{24,28},{28,20},{20,12},{12,4},{4,0},{1,9},{9... | collective-permute-start | bytes 786440 | tf_op jit(solution)/shard_map/ppermute | solution.py:369
  94.4 13.4 %collective-permute-start.8 = (bf16[1024,128]{1,0:T(8,128)(2,1)S(1)}, bf16[1024,128]{1,0:T(8,128)(2,1)S(1)}, u32[]{:S(2)}, u32[]{:S(2)}) collective-permute-start(bf16[1024,128]{1,0:T(8,128)(2,1)S(1)} %pick.5), channel_id=1, source_target_pairs={{0,4},{8,0},{16,8},{24,16},{28,24},{20,28},{12,20},{4,12},{1,5},{9... | collective-permute-start | bytes 786440 | tf_op jit(solution)/shard_map/ppermute | solution.py:369
  104.8 10.8 %collective-permute-start.21 = (bf16[512,128]{1,0:T(8,128)(2,1)S(1)}, bf16[512,128]{1,0:T(8,128)(2,1)S(1)}, u32[]{:S(2)}, u32[]{:S(2)}) collective-permute-start(bf16[512,128]{1,0:T(8,128)(2,1)S(1)} %finish.9), channel_id=1, source_target_pairs={{0,3},{1,2},{2,1},{3,0},{4,7},{5,6},{6,5},{7,4},{8,11},{9,10},{10,... | collective-permute-start | bytes 393224 | tf_op jit(solution)/shard_map/ppermute | solution.py:455
  106.2 9.7 %collective-permute-start.20 = (bf16[512,128]{1,0:T(8,128)(2,1)S(1)}, bf16[512,128]{1,0:T(8,128)(2,1)S(1)}, u32[]{:S(2)}, u32[]{:S(2)}) collective-permute-start(bf16[512,128]{1,0:T(8,128)(2,1)S(1)} %finish.8), channel_id=1, source_target_pairs={{0,2},{1,3},{2,0},{3,1},{4,6},{5,7},{6,4},{7,5},{8,10},{9,11},{10,... | collective-permute-start | bytes 393224 | tf_op jit(solution)/shard_map/ppermute | solution.py:455
  109.7 6.3 %collective-permute-start.19 = (bf16[512,128]{1,0:T(8,128)(2,1)S(1)}, bf16[512,128]{1,0:T(8,128)(2,1)S(1)}, u32[]{:S(2)}, u32[]{:S(2)}) collective-permute-start(bf16[512,128]{1,0:T(8,128)(2,1)S(1)} %get-tuple-element.38), channel_id=1, source_target_pairs={{0,1},{1,0},{2,3},{3,2},{4,5},{5,4},{6,7},{7,6},{8,9},{9,8},{10,11... | collective-permute-start | bytes 393224 | tf_op jit(solution)/shard_map/ppermute | solution.py:455
  112.0 4.0 %copy-start.7 = (bf16[1024,1024]{1,0:T(8,128)(2,1)S(1)}, bf16[1024,1024]{1,0:T(8,128)(2,1)}, u32[]{:S(2)}) copy-start(bf16[1024,1024]{1,0:T(8,128)(2,1)} %w.3) | copy-start | bytes 6291460
  112.0 3.9 %collective-permute-start.18 = (bf16[512,128]{1,0:T(8,128)(2,1)S(1)}, bf16[512,128]{1,0:T(8,128)(2,1)S(1)}, u32[]{:S(2)}, u32[]{:S(2)}) collective-permute-start(bf16[512,128]{1,0:T(8,128)(2,1)S(1)} %get-tuple-element.37), channel_id=1, source_target_pairs={{0,1},{1,0},{2,3},{3,2},{4,5},{5,4},{6,7},{7,6},{8,9},{9,8},{10,11... | collective-permute-start | bytes 393224 | tf_op jit(solution)/shard_map/ppermute | solution.py:455
  114.1 6.4 %collective-permute-start.14 = (bf16[512,128]{1,0:T(8,128)(2,1)S(1)}, bf16[512,128]{1,0:T(8,128)(2,1)S(1)}, u32[]{:S(2)}, u32[]{:S(2)}) collective-permute-start(bf16[512,128]{1,0:T(8,128)(2,1)S(1)} %get-tuple-element.32), channel_id=1, source_target_pairs={{0,2},{1,3},{2,0},{3,1},{4,6},{5,7},{6,4},{7,5},{8,10},{9,11},{10,... | collective-permute-start | bytes 393224 | tf_op jit(solution)/shard_map/ppermute | solution.py:455
  115.6 6.6 %collective-permute-start.15 = (bf16[512,128]{1,0:T(8,128)(2,1)S(1)}, bf16[512,128]{1,0:T(8,128)(2,1)S(1)}, u32[]{:S(2)}, u32[]{:S(2)}) collective-permute-start(bf16[512,128]{1,0:T(8,128)(2,1)S(1)} %get-tuple-element.33), channel_id=1, source_target_pairs={{0,3},{1,2},{2,1},{3,0},{4,7},{5,6},{6,5},{7,4},{8,11},{9,10},{10,... | collective-permute-start | bytes 393224 | tf_op jit(solution)/shard_map/ppermute | solution.py:455
  (10 other events, 25.0 us)

commit v6 on v5

--- a/solution.py
+++ b/solution.py
@@ -168,64 +168,52 @@
             totals[part][...] = start_totals[part][...]
 
 
-def finish_kernel(plan, groups, n_sources, n_dense, blocks, firsts, run, need, *refs):
+def finish_kernel(jobs, n_sources, n_dense, blocks, partners, *refs):
     sources, refs = refs[:n_sources], refs[n_sources:]
     denses, refs = refs[:n_dense], refs[n_dense:]
-    start_total, refs = refs[0], refs[1:]
-    outs, (streamed, feats, total, sem) = refs[: run * len(firsts)], refs[run * len(firsts) :]
+    totals, refs = refs[: len(jobs)], refs[len(jobs) :]
+    outs, (streamed, sem) = refs[: len(jobs) * len(partners)], refs[len(jobs) * len(partners) :]
     own = lax.axis_index("feat")
     size = ROWS // blocks
-    for e, (operand, index, resident, offset, pieces) in enumerate(plan):
-        ((part, chunks, whole),) = pieces
-
-        def put(k, value):
-            feats[e, pl.ds(k * TILE, TILE), :] = value
-
-        gather_feats(need, groups, 0, offset, [sources[i] for i in chunks], whole, put)
-    for i, first in enumerate(firsts):
-        rows = pl.ds(pl.multiple_of((lax.div(own, run) ^ (first // run)) * run * size, run * size), run * size)
-        total[...] = start_total[rows, :]
-        for e, (operand, index, resident, offset, pieces) in enumerate(plan):
-            if resident:
-                lhs = denses[operand][index, rows, :]
-            else:
-                copy = pltpu.make_async_copy(denses[operand].at[index, rows, :], streamed, sem)
-                copy.start()
-                copy.wait()
-                lhs = streamed[...]
-            total[...] += jnp.dot(lhs, feats[e], preferred_element_type=jnp.float32)
-        for low in range(run):
-            block = pl.ds(pl.multiple_of((lax.rem(own, run) ^ low) * size, size), size)
-            outs[run * i + low][...] = total[block, :].astype(jnp.bfloat16)
-
-
-def finish(plan, groups, need, sources, denses, start_total, blocks, firsts, run):
-    width = start_total.shape[1]
+    for c, plan in enumerate(jobs):
+        for i, m in enumerate(partners):
+            rows = pl.ds(pl.multiple_of((own ^ m) * size, size), size)
+            total = totals[c][rows, :]
+            for operand, index, resident, source in plan:
+                if resident:
+                    lhs = denses[operand][index, rows, :]
+                else:
+                    copy = pltpu.make_async_copy(denses[operand].at[index, rows, :], streamed, sem)
+                    copy.start()
+                    copy.wait()
+                    lhs = streamed[...]
+                total = total + jnp.dot(lhs, sources[source][...], preferred_element_type=jnp.float32)
+            outs[c * len(partners) + i][...] = total.astype(jnp.bfloat16)
+
+
+def finish(jobs, sources, denses, totals, blocks, partners):
     vmem = pl.BlockSpec(memory_space=pltpu.VMEM)
+    entries = [entry for plan in jobs for entry in plan]
     spaces = [None] * len(denses)
-    for operand, index, resident, offset, pieces in plan:
+    for operand, index, resident, source in entries:
         spaces[operand] = vmem if resident else pl.BlockSpec(memory_space=pl.ANY)
-    streams = any(not entry[2] for entry in plan)
-    rows = run * ROWS // blocks
+    streams = any(not entry[2] for entry in entries)
+    rows = ROWS // blocks
+    width = totals[0].shape[1]
+    work = len(entries) * len(partners) * rows * DEPTH
     return pl.pallas_call(
-        functools.partial(finish_kernel, plan, groups, len(sources), len(denses), blocks, firsts, run),
-        out_shape=[jax.ShapeDtypeStruct((ROWS // blocks, width), jnp.bfloat16)] * (run * len(firsts)),
-        in_specs=[pl.BlockSpec(memory_space=pltpu.SMEM)] + [vmem] * len(sources) + spaces + [vmem],
-        out_specs=[vmem] * (run * len(firsts)),
+        functools.partial(finish_kernel, jobs, len(sources), len(denses), blocks, partners),
+        out_shape=[jax.ShapeDtypeStruct((rows, width), jnp.bfloat16)] * (len(jobs) * len(partners)),
+        in_specs=[vmem] * len(sources) + spaces + [vmem] * len(totals),
+        out_specs=[vmem] * (len(jobs) * len(partners)),
         scratch_shapes=[
             pltpu.VMEM((rows, DEPTH) if streams else (8, TILE), jnp.bfloat16),
-            pltpu.VMEM((len(plan), DEPTH, width), jnp.bfloat16),
-            pltpu.VMEM((rows, width), jnp.float32),
             pltpu.SemaphoreType.DMA,
         ],
-        compiler_params=pltpu.CompilerParams(vmem_limit_bytes=STREAM_LIMIT if streams else RESIDENT_LIMIT),
-        cost_estimate=pl.CostEstimate(
-            flops=2 * len(plan) * len(firsts) * rows * DEPTH * width,
-            bytes_accessed=2 * len(plan) * len(firsts) * rows * DEPTH,
-            transcendentals=0,
-        ),
+        compiler_params=pltpu.CompilerParams(vmem_limit_bytes=RESIDENT_LIMIT),
+        cost_estimate=pl.CostEstimate(flops=2 * work * width, bytes_accessed=2 * work, transcendentals=0),
         name="finish",
-    )(need, *sources, *denses, start_total)
+    )(*sources, *denses, *totals)
 
 
 def plan_first(plan, part):
@@ -397,7 +385,7 @@
             upto = next((e for e in range(d + 1, far + 1) if e == 2 or is_resident(e) != is_resident(d)), far + 1)
             dense += densify(stages[d:upto], is_resident(d), groups, table, tiles)
 
-    def add(totals, entries, columns, firsts=None, run=1):
+    def add(totals, entries, columns):
         sources, operands, plan = [], [], []
         for way, d, parts in entries:
             if d not in operands:
@@ -411,9 +399,6 @@
             index = stages[d].index(offset) if d < far else 0
             plan.append((operands.index(d), index, is_resident(d), offset, tuple(pieces)))
         sizes = tuple(widths[c] for c in columns)
-        if firsts is not None:
-            arrays = [dense[d] for d in operands]
-            return finish(tuple(plan), groups, need, sources, arrays, totals[0], blocks, firsts, run)
         return aggregate(tuple(plan), groups, need, sources, [dense[d] for d in operands], totals, sizes)
 
     every = list(range(cuts))
@@ -436,18 +421,25 @@
 
     finished = {}
 
-    def complete(c, firsts, run):
-        if firsts:
-            outs = add([ends[c][0]], ends[c][1], [c], firsts, run)
-            finished.update({(c, m + low): outs[run * i + low] for i, m in enumerate(firsts) for low in range(run)})
+    def complete(columns, partners):
+        sources, operands, jobs = [], [], []
+        for c in columns:
+            plan = []
+            for way, d, parts in ends[c][1]:
+                if d not in operands:
+                    operands.append(d)
+                index = stages[d].index(-way * d) if d < far else 0
+                plan.append((operands.index(d), index, is_resident(d), len(sources)))
+                sources += held[way, d, c][0]
+            jobs.append(tuple(plan))
+        totals = [ends[c][0] for c in columns]
+        outs = finish(tuple(jobs), sources, [dense[d] for d in operands], totals, blocks, partners)
+        finished.update({(c, m): outs[i * len(partners) + j] for i, c in enumerate(columns) for j, m in enumerate(partners)})
 
     for c in range(cuts):
-        if c < last:
-            for m in reversed(range(2, blocks)):
-                complete(c, (m,), 1)
-        else:
-            complete(c, tuple(range(2, blocks, 2)), 2)
-        complete(c, (0,), 2)
+        for m in reversed(range(2, blocks)):
+            complete([c], (m,))
+    complete(every, (0, 1))
 
     def exchange(c, m):
         if m == 0:

time: 124 us -> 121 us (0.976)
  Pallas kernels: 42 us -> 39 us
    pallas_call x5, Pallas kernels: 8.25 us -> 5.25 us  [finish(): pl.pallas_call(functools.partial(finish_kernel, jobs, len(sources), len(d...]
  transfers between devices with their start and end apart: 22 -> 22, of which waited for: 7 -> 7; matrix products, arithmetic and copies ran while one was open for 1% -> 1% of each run, Pallas kernels for 33% -> 31%
where the time goes in v6:
time: 121 us; the launch traced here: 120 us
  Pallas kernels  39 us (32%)
  waiting for transfers between devices  31.2 us (26%)
  starting transfers between devices  24.4 us (20%)
  local copies, waits for them, and re-layouts  24.2 us (20%)
    ppermute x16, waiting for transfers between devices, send(): return lax.ppermute(array, 'rows', ring_pairs(groups, way))  26.4 us
    unnamed x40, local copies, waits for them, and re-layouts  21.6 us
    ppermute x16, starting transfers between devices, send(): return lax.ppermute(array, 'rows', ring_pairs(groups, way))  20 us
    pallas_call x2, Pallas kernels, densify(): pl.pallas_call(functools.partial(densify_kernel, stages, resident, groups...  14.5 us
    pallas_call x4, Pallas kernels, aggregate(): pl.pallas_call(functools.partial(aggregate_kernel, plan, groups, len(sour...  14.4 us
    pallas_call x5, Pallas kernels, finish(): pl.pallas_call(functools.partial(finish_kernel, jobs, len(sources), len(d...  5.25 us
    ppermute x6, waiting for transfers between devices, exchange(): lax.ppermute(finished[c, m], 'feat', [(f, f ^ m) for f in range(blocks)])  4.81 us
    ppermute x6, starting transfers between devices, exchange(): lax.ppermute(finished[c, m], 'feat', [(f, f ^ m) for f in range(blocks)])  4.32 us
  transfers between devices with their start and end apart: 22, of which 7 were waited for; matrix products, arithmetic and copies ran while one was open for 1% of the time, Pallas kernels for 31%

profile of v6, /device:TPU:0, one launch (start us, length us, event | category | flops | bytes accessed | tf_op | source)
XLA Modules:
  0.0 120.4 jit_solution(1773885977311383654)
XLA Ops:
  0.0 1.3 %fusion = (bf16[2048,128]{1,0:T(8,128)(2,1)S(1)}, bf16[2048,128]{1,0:T(8,128)(2,1)S(1)}) fusion(bf16[2048,256]{1,0:T(8,128)(2,1)} %param.8), kind=kLoop, calls=%fused_computation.5 | loop fusion | bytes 2097152 | tf_op jit(solution)/shard_map/slice | solution.py:361
  1.3 3.1 %collective-permute-start.11 = (bf16[2048,128]{1,0:T(8,128)(2,1)S(1)}, bf16[2048,128]{1,0:T(8,128)(2,1)S(1)}, u32[]{:S(2)}, u32[]{:S(2)}) collective-permute-start(bf16[2048,128]{1,0:T(8,128)(2,1)S(1)} %get-tuple-element.35.refs_0_), channel_id=1, source_target_pairs={{0,8},{8,16},{16,24},{24,28},{28,20},{20,12},{12,4},{4,0},{1,9},{9... | collective-permute-start | bytes 1572872 | tf_op jit(solution)/shard_map/ppermute | solution.py:357
  4.4 2.0 %collective-permute-start.9 = (bf16[2048,128]{1,0:T(8,128)(2,1)S(1)}, bf16[2048,128]{1,0:T(8,128)(2,1)}, u32[]{:S(2)}, u32[]{:S(2)}) collective-permute-start(bf16[2048,128]{1,0:T(8,128)(2,1)S(1)} %get-tuple-element.35.refs_0_), channel_id=1, source_target_pairs={{0,4},{8,0},{16,8},{24,16},{28,24},{20,28},{12,20},{4,12},{1,5},{9... | collective-permute-start | bytes 1572872 | tf_op jit(solution)/shard_map/ppermute | solution.py:357
  6.4 9.9 %collective-permute-done.11.refs_0_ = bf16[2048,128]{1,0:T(8,128)(2,1)S(1)} collective-permute-done((bf16[2048,128]{1,0:T(8,128)(2,1)S(1)}, bf16[2048,128]{1,0:T(8,128)(2,1)S(1)}, u32[]{:S(2)}, u32[]{:S(2)}) %collective-permute-start.11) | collective-permute-done | bytes 524320 | tf_op jit(solution)/shard_map/ppermute | solution.py:357
  16.3 1.8 %collective-permute-start.12 = (bf16[2048,128]{1,0:T(8,128)(2,1)S(1)}, bf16[2048,128]{1,0:T(8,128)(2,1)}, u32[]{:S(2)}, u32[]{:S(2)}) collective-permute-start(bf16[2048,128]{1,0:T(8,128)(2,1)S(1)} %collective-permute-done.11.refs_0_), channel_id=1, source_target_pairs={{0,8},{8,16},{16,24},{24,28},{28,20},{20,12},{12,4},{4,0},{1,9},{9... | collective-permute-start | bytes 1572872 | tf_op jit(solution)/shard_map/ppermute | solution.py:357
  20.5 1.9 %collective-permute-start = (bf16[1024,128]{1,0:T(8,128)(2,1)S(1)}, bf16[1024,128]{1,0:T(8,128)(2,1)S(1)}, u32[]{:S(2)}, u32[]{:S(2)}) collective-permute-start(bf16[1024,128]{1,0:T(8,128)(2,1)S(1)} %get-tuple-element.38), channel_id=1, source_target_pairs={{0,8},{8,16},{16,24},{24,28},{28,20},{20,12},{12,4},{4,0},{1,9},{9... | collective-permute-start | bytes 786440 | tf_op jit(solution)/shard_map/ppermute | solution.py:357
  22.4 1.6 %collective-permute-start.2 = (bf16[1024,128]{1,0:T(8,128)(2,1)S(1)}, bf16[1024,128]{1,0:T(8,128)(2,1)}, u32[]{:S(2)}, u32[]{:S(2)}) collective-permute-start(bf16[1024,128]{1,0:T(8,128)(2,1)S(1)} %get-tuple-element.37), channel_id=1, source_target_pairs={{0,8},{8,16},{16,24},{24,28},{28,20},{20,12},{12,4},{4,0},{1,9},{9... | collective-permute-start | bytes 786440 | tf_op jit(solution)/shard_map/ppermute | solution.py:357
  24.6 6.0 %collective-permute-done.9.refs_3_ = bf16[2048,128]{1,0:T(8,128)(2,1)} collective-permute-done((bf16[2048,128]{1,0:T(8,128)(2,1)S(1)}, bf16[2048,128]{1,0:T(8,128)(2,1)}, u32[]{:S(2)}, u32[]{:S(2)}) %collective-permute-start.9) | collective-permute-done | bytes 524320 | tf_op jit(solution)/shard_map/ppermute | solution.py:357
  31.2 1.8 %collective-permute-start.13 = (bf16[2048,128]{1,0:T(8,128)(2,1)}, bf16[2048,128]{1,0:T(8,128)(2,1)S(1)}, u32[]{:S(2)}, u32[]{:S(2)}) collective-permute-start(bf16[2048,128]{1,0:T(8,128)(2,1)} %collective-permute-done.12.refs_2_), channel_id=1, source_target_pairs={{0,8},{8,16},{16,24},{24,28},{28,20},{20,12},{12,4},{4,0},{1,9},{9... | collective-permute-start | bytes 1572872 | tf_op jit(solution)/shard_map/ppermute | solution.py:357
  33.0 8.8 %collective-permute-done.6.refs_1_ = bf16[2048,128]{1,0:T(8,128)(2,1)} collective-permute-done((bf16[2048,128]{1,0:T(8,128)(2,1)S(1)}, bf16[2048,128]{1,0:T(8,128)(2,1)}, u32[]{:S(2)}, u32[]{:S(2)}) %collective-permute-start.6) | collective-permute-done | bytes 524320 | tf_op jit(solution)/shard_map/ppermute | solution.py:357
  41.8 2.1 %collective-permute-start.1 = (bf16[1024,128]{1,0:T(8,128)(2,1)S(1)}, bf16[1024,128]{1,0:T(8,128)(2,1)S(1)}, u32[]{:S(2)}, u32[]{:S(2)}) collective-permute-start(bf16[1024,128]{1,0:T(8,128)(2,1)S(1)} %collective-permute-done.refs_1_), channel_id=1, source_target_pairs={{0,8},{8,16},{16,24},{24,28},{28,20},{20,12},{12,4},{4,0},{1,9},{9... | collective-permute-start | bytes 786440 | tf_op jit(solution)/shard_map/ppermute | solution.py:357
  43.9 1.6 %collective-permute-start.3 = (bf16[1024,128]{1,0:T(8,128)(2,1)}, bf16[1024,128]{1,0:T(8,128)(2,1)S(1)}, u32[]{:S(2)}, u32[]{:S(2)}) collective-permute-start(bf16[1024,128]{1,0:T(8,128)(2,1)} %collective-permute-done.2.refs_2_), channel_id=1, source_target_pairs={{0,8},{8,16},{16,24},{24,28},{28,20},{20,12},{12,4},{4,0},{1,9},{9... | collective-permute-start | bytes 786440 | tf_op jit(solution)/shard_map/ppermute | solution.py:357
  45.9 5.7 %densify.3 = (bf16[1,2048,1024]{2,1,0:T(8,128)(2,1)S(1)}, bf16[2,2048,1024]{2,1,0:T(8,128)(2,1)S(1)}) custom-call(s32[1024]{0:T(1024)S(1)} %select_reduce_fusion.table, bf16[640,128,128]{2,1,0:T(8,128)(2,1)} %tiles.3), custom_call_target="tpu_custom_call" | custom-call | bytes 12582912 | tf_op jit(solution)/shard_map/densify/pallas_call | solution.py:86
  51.6 3.3 %copy-done.5 = bf16[2,2048,1024]{2,1,0:T(8,128)(2,1)} copy-done((bf16[2,2048,1024]{2,1,0:T(8,128)(2,1)}, bf16[2,2048,1024]{2,1,0:T(8,128)(2,1)S(1)}, u32[]{:S(2)}) %copy-start.5) | copy-done | bytes 8388632
  54.9 2.0 %copy-done.8 = bf16[1,2048,1024]{2,1,0:T(8,128)(2,1)} copy-done((bf16[1,2048,1024]{2,1,0:T(8,128)(2,1)}, bf16[1,2048,1024]{2,1,0:T(8,128)(2,1)S(1)}, u32[]{:S(2)}) %copy-start.8) | copy-done | bytes 4194328
  56.9 8.8 %densify.2 = (bf16[2,2048,1024]{2,1,0:T(8,128)(2,1)S(1)}, bf16[2,2048,1024]{2,1,0:T(8,128)(2,1)S(1)}, bf16[1,2048,1024]{2,1,0:T(8,128)(2,1)S(1)}) custom-call(s32[1024]{0:T(1024)S(1)} %select_reduce_fusion.table, bf16[640,128,128]{2,1,0:T(8,128)(2,1)} %tiles.3), custom_call_target="tpu_custom_call" | custom-call | bytes 20971520 | tf_op jit(solution)/shard_map/densify/pallas_call | solution.py:86
  65.7 3.3 %copy-done = bf16[2,2048,1024]{2,1,0:T(8,128)(2,1)} copy-done((bf16[2,2048,1024]{2,1,0:T(8,128)(2,1)}, bf16[2,2048,1024]{2,1,0:T(8,128)(2,1)S(1)}, u32[]{:S(2)}) %copy-start) | copy-done | bytes 8388632
  69.0 2.1 %copy-done.1 = bf16[1,2048,1024]{2,1,0:T(8,128)(2,1)} copy-done((bf16[1,2048,1024]{2,1,0:T(8,128)(2,1)}, bf16[1,2048,1024]{2,1,0:T(8,128)(2,1)S(1)}, u32[]{:S(2)}) %copy-start.1) | copy-done | bytes 4194328
  71.0 3.2 %copy-done.3 = bf16[2,2048,1024]{2,1,0:T(8,128)(2,1)} copy-done((bf16[2,2048,1024]{2,1,0:T(8,128)(2,1)}, bf16[2,2048,1024]{2,1,0:T(8,128)(2,1)S(1)}, u32[]{:S(2)}) %copy-start.3) | copy-done | bytes 8388632
  74.4 2.2 %copy-done.9 = bf16[1,2048,1024]{2,1,0:T(8,128)(2,1)S(1)} copy-done((bf16[1,2048,1024]{2,1,0:T(8,128)(2,1)S(1)}, bf16[1,2048,1024]{2,1,0:T(8,128)(2,1)}, u32[]{:S(2)}) %copy-start.9) | copy-done | bytes 4194328
  76.6 2.0 %aggregate.4 = (f32[2048,128]{1,0:T(8,128)S(1)}, f32[2048,128]{1,0:T(8,128)S(1)}) custom-call(s32[512]{0:T(512)S(1)} %reshape.9.need, bf16[2048,128]{1,0:T(8,128)(2,1)S(1)} %get-tuple-element.35.refs_0_, bf16[2048,128]{1,0:T(8,128)(2,1)S(1)} %get-tuple-element.36.refs_1_, bf16[1,2048,1024]{2,1,0:T(8,128)(2,1)S(1)} %copy-done.9), custom_call_target="tpu_custom_call" | custom-call | flops 1073741824 | bytes 4194304 | tf_op jit(solution)/shard_map/aggregate/pallas_call | solution.py:241
  79.3 1.5 %collective-permute-start.4 = (bf16[1024,128]{1,0:T(8,128)(2,1)S(1)}, bf16[1024,128]{1,0:T(8,128)(2,1)S(1)}, u32[]{:S(2)}, u32[]{:S(2)}) collective-permute-start(bf16[1024,128]{1,0:T(8,128)(2,1)S(1)} %pick.4), channel_id=1, source_target_pairs={{0,8},{8,16},{16,24},{24,28},{28,20},{20,12},{12,4},{4,0},{1,9},{9... | collective-permute-start | bytes 786440 | tf_op jit(solution)/shard_map/ppermute | solution.py:357
  80.8 3.4 %copy-done.6 = bf16[2,2048,1024]{2,1,0:T(8,128)(2,1)S(1)} copy-done((bf16[2,2048,1024]{2,1,0:T(8,128)(2,1)S(1)}, bf16[2,2048,1024]{2,1,0:T(8,128)(2,1)}, u32[]{:S(2)}) %copy-start.6) | copy-done | bytes 8388632
  86.3 4.1 %aggregate.5 = (f32[2048,128]{1,0:T(8,128)S(1)}, f32[2048,128]{1,0:T(8,128)S(1)}) custom-call(s32[512]{0:T(512)S(1)} %reshape.9.need, bf16[2048,128]{1,0:T(8,128)(2,1)S(1)} %copy-done.11, bf16[1024,128]{1,0:T(8,128)(2,1)S(1)} %collective-permute-done.refs_1_, bf16[1024,128]{1,0:T(8,128)(2,1)} %collective-permute-done.2.refs_2_, ...), custom_call_target="tpu_custom_call" | custom-call | flops 2147483648 | bytes 8388608 | tf_op jit(solution)/shard_map/aggregate/pallas_call | solution.py:241
  92.3 1.5 %collective-permute-start.17 = (bf16[1024,128]{1,0:T(8,128)(2,1)S(1)}, bf16[1024,128]{1,0:T(8,128)(2,1)S(1)}, u32[]{:S(2)}, u32[]{:S(2)}) collective-permute-start(bf16[1024,128]{1,0:T(8,128)(2,1)S(1)} %pick.7), channel_id=1, source_target_pairs={{0,8},{8,16},{16,24},{24,28},{28,20},{20,12},{12,4},{4,0},{1,9},{9... | collective-permute-start | bytes 786440 | tf_op jit(solution)/shard_map/ppermute | solution.py:357
  95.1 5.0 %aggregate.6 = (f32[2048,128]{1,0:T(8,128)S(1)}, f32[2048,128]{1,0:T(8,128)S(1)}) custom-call(s32[512]{0:T(512)S(1)} %reshape.9.need, bf16[2048,128]{1,0:T(8,128)(2,1)S(1)} %collective-permute-done.10.refs_0_, bf16[2048,128]{1,0:T(8,128)(2,1)} %collective-permute-done.6.refs_1_, bf16[2048,128]{1,0:T(8,128)(2,1)} %collective-permute-done.12.refs_2_, ...), custom_call_target="tpu_custom_call" | custom-call | flops 2147483648 | bytes 12582912 | tf_op jit(solution)/shard_map/aggregate/pallas_call | solution.py:241
  100.1 3.4 %aggregate.7.refs_4_.refs_7_ = f32[2048,128]{1,0:T(8,128)S(1)} custom-call(s32[512]{0:T(512)S(1)} %reshape.9.need, bf16[1024,128]{1,0:T(8,128)(2,1)S(1)} %collective-permute-done.1.refs_0_, bf16[1024,128]{1,0:T(8,128)(2,1)S(1)} %collective-permute-done.3.refs_1_, bf16[2048,128]{1,0:T(8,128)(2,1)S(1)} %collective-permute-done.7.refs_0_.refs_2_, ...), custom_call_target="tpu_custom_call" | custom-call | flops 1073741824 | bytes 8388608 | tf_op jit(solution)/shard_map/aggregate/pallas_call | solution.py:241
  105.0 1.6 %collective-permute-start.20 = (bf16[512,128]{1,0:T(8,128)(2,1)S(1)}, bf16[512,128]{1,0:T(8,128)(2,1)S(1)}, u32[]{:S(2)}, u32[]{:S(2)}) collective-permute-start(bf16[512,128]{1,0:T(8,128)(2,1)S(1)} %finish.8), channel_id=1, source_target_pairs={{0,2},{1,3},{2,0},{3,1},{4,6},{5,7},{6,4},{7,5},{8,10},{9,11},{10,... | collective-permute-start | bytes 393224 | tf_op jit(solution)/shard_map/ppermute | solution.py:447
  106.6 2.3 %finish.7 = (bf16[512,128]{1,0:T(8,128)(2,1)S(1)}, bf16[512,128]{1,0:T(8,128)(2,1)S(1)}, bf16[512,128]{1,0:T(8,128)(2,1)S(1)}, bf16[512,128]{1,0:T(8,128)(2,1)S(1)}) custom-call(bf16[1024,128]{1,0:T(8,128)(2,1)S(1)} %collective-permute-done.16.refs_0_, bf16[1024,128]{1,0:T(8,128)(2,1)S(1)} %collective-permute-done.17.refs_1_, ...), custom_call_target="tpu_custom_call" | custom-call | flops 1073741824 | bytes 8388608 | tf_op jit(solution)/shard_map/finish/pallas_call | solution.py:204
  110.3 1.5 %collective-permute-start.15 = (bf16[512,128]{1,0:T(8,128)(2,1)S(1)}, bf16[512,128]{1,0:T(8,128)(2,1)S(1)}, u32[]{:S(2)}, u32[]{:S(2)}) collective-permute-start(bf16[512,128]{1,0:T(8,128)(2,1)S(1)} %finish.6), channel_id=1, source_target_pairs={{0,3},{1,2},{2,1},{3,0},{4,7},{5,6},{6,5},{7,4},{8,11},{9,10},{10,... | collective-permute-start | bytes 393224 | tf_op jit(solution)/shard_map/ppermute | solution.py:447
  114.2 1.5 %collective-permute-done.15.refs_1_ = bf16[512,128]{1,0:T(8,128)(2,1)S(1)} collective-permute-done((bf16[512,128]{1,0:T(8,128)(2,1)S(1)}, bf16[512,128]{1,0:T(8,128)(2,1)S(1)}, u32[]{:S(2)}, u32[]{:S(2)}) %collective-permute-start.15) | collective-permute-done | bytes 131104 | tf_op jit(solution)/shard_map/ppermute | solution.py:447
  115.7 3.3 %collective-permute-done.14.refs_0_ = bf16[512,128]{1,0:T(8,128)(2,1)S(1)} collective-permute-done((bf16[512,128]{1,0:T(8,128)(2,1)S(1)}, bf16[512,128]{1,0:T(8,128)(2,1)S(1)}, u32[]{:S(2)}, u32[]{:S(2)}) %collective-permute-start.14) | collective-permute-done | bytes 131104 | tf_op jit(solution)/shard_map/ppermute | solution.py:447
  (75 shorter events, 16.0 us)
Async XLA Ops:
  0.0 41.8 %copy-start.16 = (s32[640]{0:T(1024)S(1)}, s32[640]{0:T(1024)}, u32[]{:S(2)}) copy-start(s32[640]{0:T(1024)} %param.10) | copy-start | bytes 7684
  0.0 41.8 %copy-start.17 = (s32[640]{0:T(1024)S(1)}, s32[640]{0:T(1024)}, u32[]{:S(2)}) copy-start(s32[640]{0:T(1024)} %param.11) | copy-start | bytes 7684
  0.0 41.8 %copy-start.15 = (s32[640]{0:T(1024)S(1)}, s32[640]{0:T(1024)}, u32[]{:S(2)}) copy-start(s32[640]{0:T(1024)} %param.12) | copy-start | bytes 7684
  1.3 15.0 %collective-permute-start.11 = (bf16[2048,128]{1,0:T(8,128)(2,1)S(1)}, bf16[2048,128]{1,0:T(8,128)(2,1)S(1)}, u32[]{:S(2)}, u32[]{:S(2)}) collective-permute-start(bf16[2048,128]{1,0:T(8,128)(2,1)S(1)} %get-tuple-element.35.refs_0_), channel_id=1, source_target_pairs={{0,8},{8,16},{16,24},{24,28},{28,20},{20,12},{12,4},{4,0},{1,9},{9... | collective-permute-start | bytes 1572872 | tf_op jit(solution)/shard_map/ppermute | solution.py:357
  4.4 14.8 %collective-permute-start.5 = (bf16[2048,128]{1,0:T(8,128)(2,1)S(1)}, bf16[2048,128]{1,0:T(8,128)(2,1)S(1)}, u32[]{:S(2)}, u32[]{:S(2)}) collective-permute-start(bf16[2048,128]{1,0:T(8,128)(2,1)S(1)} %get-tuple-element.36.refs_1_), channel_id=1, source_target_pairs={{0,4},{8,0},{16,8},{24,16},{28,24},{20,28},{12,20},{4,12},{1,5},{9... | collective-permute-start | bytes 1572872 | tf_op jit(solution)/shard_map/ppermute | solution.py:357
  4.4 26.1 %collective-permute-start.9 = (bf16[2048,128]{1,0:T(8,128)(2,1)S(1)}, bf16[2048,128]{1,0:T(8,128)(2,1)}, u32[]{:S(2)}, u32[]{:S(2)}) collective-permute-start(bf16[2048,128]{1,0:T(8,128)(2,1)S(1)} %get-tuple-element.35.refs_0_), channel_id=1, source_target_pairs={{0,4},{8,0},{16,8},{24,16},{28,24},{20,28},{12,20},{4,12},{1,5},{9... | collective-permute-start | bytes 1572872 | tf_op jit(solution)/shard_map/ppermute | solution.py:357
  16.3 14.3 %copy-start.10 = (bf16[2048,128]{1,0:T(8,128)(2,1)}, bf16[2048,128]{1,0:T(8,128)(2,1)S(1)}, u32[]{:S(2)}) copy-start(bf16[2048,128]{1,0:T(8,128)(2,1)S(1)} %collective-permute-done.11.refs_0_) | copy-start | bytes 1572868
  16.3 14.9 %collective-permute-start.12 = (bf16[2048,128]{1,0:T(8,128)(2,1)S(1)}, bf16[2048,128]{1,0:T(8,128)(2,1)}, u32[]{:S(2)}, u32[]{:S(2)}) collective-permute-start(bf16[2048,128]{1,0:T(8,128)(2,1)S(1)} %collective-permute-done.11.refs_0_), channel_id=1, source_target_pairs={{0,8},{8,16},{16,24},{24,28},{28,20},{20,12},{12,4},{4,0},{1,9},{9... | collective-permute-start | bytes 1572872 | tf_op jit(solution)/shard_map/ppermute | solution.py:357
  19.2 13.8 %copy-start.12 = (bf16[2048,128]{1,0:T(8,128)(2,1)}, bf16[2048,128]{1,0:T(8,128)(2,1)S(1)}, u32[]{:S(2)}) copy-start(bf16[2048,128]{1,0:T(8,128)(2,1)S(1)} %collective-permute-done.5.refs_4_) | copy-start | bytes 1572868
  19.2 22.6 %collective-permute-start.6 = (bf16[2048,128]{1,0:T(8,128)(2,1)S(1)}, bf16[2048,128]{1,0:T(8,128)(2,1)}, u32[]{:S(2)}, u32[]{:S(2)}) collective-permute-start(bf16[2048,128]{1,0:T(8,128)(2,1)S(1)} %collective-permute-done.5.refs_4_), channel_id=1, source_target_pairs={{0,4},{8,0},{16,8},{24,16},{28,24},{20,28},{12,20},{4,12},{1,5},{9... | collective-permute-start | bytes 1572872 | tf_op jit(solution)/shard_map/ppermute | solution.py:357
  20.5 21.3 %collective-permute-start = (bf16[1024,128]{1,0:T(8,128)(2,1)S(1)}, bf16[1024,128]{1,0:T(8,128)(2,1)S(1)}, u32[]{:S(2)}, u32[]{:S(2)}) collective-permute-start(bf16[1024,128]{1,0:T(8,128)(2,1)S(1)} %get-tuple-element.38), channel_id=1, source_target_pairs={{0,8},{8,16},{16,24},{24,28},{28,20},{20,12},{12,4},{4,0},{1,9},{9... | collective-permute-start | bytes 786440 | tf_op jit(solution)/shard_map/ppermute | solution.py:357
  22.4 21.5 %collective-permute-start.2 = (bf16[1024,128]{1,0:T(8,128)(2,1)S(1)}, bf16[1024,128]{1,0:T(8,128)(2,1)}, u32[]{:S(2)}, u32[]{:S(2)}) collective-permute-start(bf16[1024,128]{1,0:T(8,128)(2,1)S(1)} %get-tuple-element.37), channel_id=1, source_target_pairs={{0,8},{8,16},{16,24},{24,28},{28,20},{20,12},{12,4},{4,0},{1,9},{9... | collective-permute-start | bytes 786440 | tf_op jit(solution)/shard_map/ppermute | solution.py:357
  30.6 59.8 %collective-permute-start.10 = (bf16[2048,128]{1,0:T(8,128)(2,1)}, bf16[2048,128]{1,0:T(8,128)(2,1)S(1)}, u32[]{:S(2)}, u32[]{:S(2)}) collective-permute-start(bf16[2048,128]{1,0:T(8,128)(2,1)} %collective-permute-done.9.refs_3_), channel_id=1, source_target_pairs={{0,4},{8,0},{16,8},{24,16},{28,24},{20,28},{12,20},{4,12},{1,5},{9... | collective-permute-start | bytes 1572872 | tf_op jit(solution)/shard_map/ppermute | solution.py:357
  31.2 60.5 %collective-permute-start.13 = (bf16[2048,128]{1,0:T(8,128)(2,1)}, bf16[2048,128]{1,0:T(8,128)(2,1)S(1)}, u32[]{:S(2)}, u32[]{:S(2)}) collective-permute-start(bf16[2048,128]{1,0:T(8,128)(2,1)} %collective-permute-done.12.refs_2_), channel_id=1, source_target_pairs={{0,8},{8,16},{16,24},{24,28},{28,20},{20,12},{12,4},{4,0},{1,9},{9... | collective-permute-start | bytes 1572872 | tf_op jit(solution)/shard_map/ppermute | solution.py:357
  41.8 52.0 %collective-permute-start.7 = (bf16[2048,128]{1,0:T(8,128)(2,1)}, bf16[2048,128]{1,0:T(8,128)(2,1)S(1)}, u32[]{:S(2)}, u32[]{:S(2)}) collective-permute-start(bf16[2048,128]{1,0:T(8,128)(2,1)} %collective-permute-done.6.refs_1_), channel_id=1, source_target_pairs={{0,4},{8,0},{16,8},{24,16},{28,24},{20,28},{12,20},{4,12},{1,5},{9... | collective-permute-start | bytes 1572872 | tf_op jit(solution)/shard_map/ppermute | solution.py:357
  41.8 36.7 %collective-permute-start.1 = (bf16[1024,128]{1,0:T(8,128)(2,1)S(1)}, bf16[1024,128]{1,0:T(8,128)(2,1)S(1)}, u32[]{:S(2)}, u32[]{:S(2)}) collective-permute-start(bf16[1024,128]{1,0:T(8,128)(2,1)S(1)} %collective-permute-done.refs_1_), channel_id=1, source_target_pairs={{0,8},{8,16},{16,24},{24,28},{28,20},{20,12},{12,4},{4,0},{1,9},{9... | collective-permute-start | bytes 786440 | tf_op jit(solution)/shard_map/ppermute | solution.py:357
  43.9 34.7 %collective-permute-start.3 = (bf16[1024,128]{1,0:T(8,128)(2,1)}, bf16[1024,128]{1,0:T(8,128)(2,1)S(1)}, u32[]{:S(2)}, u32[]{:S(2)}) collective-permute-start(bf16[1024,128]{1,0:T(8,128)(2,1)} %collective-permute-done.2.refs_2_), channel_id=1, source_target_pairs={{0,8},{8,16},{16,24},{24,28},{28,20},{20,12},{12,4},{4,0},{1,9},{9... | collective-permute-start | bytes 786440 | tf_op jit(solution)/shard_map/ppermute | solution.py:357
  56.9 17.4 %copy-start.14 = (s32[8,8,8]{2,1,0:T(8,128)S(1)}, s32[8,8,8]{2,1,0:T(8,128)}, u32[]{:S(2)}) copy-start(s32[8,8,8]{2,1,0:T(8,128)} %param.14) | copy-start | bytes 6148
  76.6 18.5 %copy-start.4 = (bf16[2,2048,1024]{2,1,0:T(8,128)(2,1)S(1)}, bf16[2,2048,1024]{2,1,0:T(8,128)(2,1)}, u32[]{:S(2)}) copy-start(bf16[2,2048,1024]{2,1,0:T(8,128)(2,1)} %copy-done.3) | copy-start | bytes 25165828
  78.6 16.5 %slice-start = ((s8[8388608]{0:T(1024)(128)(4,1)}), s8[4194304]{0:T(1024)(128)(4,1)S(1)}, s32[]{:S(2)}) async-start(s8[8388608]{0:T(1024)(128)(4,1)} %bitcast.2), calls=%async_computation | async-start | bytes 8388608
  79.3 27.3 %collective-permute-start.4 = (bf16[1024,128]{1,0:T(8,128)(2,1)S(1)}, bf16[1024,128]{1,0:T(8,128)(2,1)S(1)}, u32[]{:S(2)}, u32[]{:S(2)}) collective-permute-start(bf16[1024,128]{1,0:T(8,128)(2,1)S(1)} %pick.4), channel_id=1, source_target_pairs={{0,8},{8,16},{16,24},{24,28},{28,20},{20,12},{12,4},{4,0},{1,9},{9... | collective-permute-start | bytes 786440 | tf_op jit(solution)/shard_map/ppermute | solution.py:357
  86.3 8.8 %slice-start.1 = ((s8[8388608]{0:T(1024)(128)(4,1)}), s8[4194304]{0:T(1024)(128)(4,1)S(1)}, s32[]{:S(2)}) async-start(s8[8388608]{0:T(1024)(128)(4,1)} %bitcast.2), calls=%async_computation.1 | async-start | bytes 8388608
  91.0 12.4 %collective-permute-start.16 = (bf16[1024,128]{1,0:T(8,128)(2,1)S(1)}, bf16[1024,128]{1,0:T(8,128)(2,1)S(1)}, u32[]{:S(2)}, u32[]{:S(2)}) collective-permute-start(bf16[1024,128]{1,0:T(8,128)(2,1)S(1)} %pick.6), channel_id=1, source_target_pairs={{0,4},{8,0},{16,8},{24,16},{28,24},{20,28},{12,20},{4,12},{1,5},{9... | collective-permute-start | bytes 786440 | tf_op jit(solution)/shard_map/ppermute | solution.py:357
  92.3 11.2 %collective-permute-start.17 = (bf16[1024,128]{1,0:T(8,128)(2,1)S(1)}, bf16[1024,128]{1,0:T(8,128)(2,1)S(1)}, u32[]{:S(2)}, u32[]{:S(2)}) collective-permute-start(bf16[1024,128]{1,0:T(8,128)(2,1)S(1)} %pick.7), channel_id=1, source_target_pairs={{0,8},{8,16},{16,24},{24,28},{28,20},{20,12},{12,4},{4,0},{1,9},{9... | collective-permute-start | bytes 786440 | tf_op jit(solution)/shard_map/ppermute | solution.py:357
  94.4 12.2 %collective-permute-start.8 = (bf16[1024,128]{1,0:T(8,128)(2,1)S(1)}, bf16[1024,128]{1,0:T(8,128)(2,1)S(1)}, u32[]{:S(2)}, u32[]{:S(2)}) collective-permute-start(bf16[1024,128]{1,0:T(8,128)(2,1)S(1)} %pick.5), channel_id=1, source_target_pairs={{0,4},{8,0},{16,8},{24,16},{28,24},{20,28},{12,20},{4,12},{1,5},{9... | collective-permute-start | bytes 786440 | tf_op jit(solution)/shard_map/ppermute | solution.py:357
  100.1 3.4 %copy-start.2 = (bf16[1,2048,1024]{2,1,0:T(8,128)(2,1)S(1)}, bf16[1,2048,1024]{2,1,0:T(8,128)(2,1)}, u32[]{:S(2)}) copy-start(bf16[1,2048,1024]{2,1,0:T(8,128)(2,1)} %copy-done.1) | copy-start | bytes 12582916
  104.2 8.3 %collective-permute-start.21 = (bf16[512,128]{1,0:T(8,128)(2,1)S(1)}, bf16[512,128]{1,0:T(8,128)(2,1)S(1)}, u32[]{:S(2)}, u32[]{:S(2)}) collective-permute-start(bf16[512,128]{1,0:T(8,128)(2,1)S(1)} %finish.9), channel_id=1, source_target_pairs={{0,3},{1,2},{2,1},{3,0},{4,7},{5,6},{6,5},{7,4},{8,11},{9,10},{10,... | collective-permute-start | bytes 393224 | tf_op jit(solution)/shard_map/ppermute | solution.py:447
  105.0 8.1 %collective-permute-start.20 = (bf16[512,128]{1,0:T(8,128)(2,1)S(1)}, bf16[512,128]{1,0:T(8,128)(2,1)S(1)}, u32[]{:S(2)}, u32[]{:S(2)}) collective-permute-start(bf16[512,128]{1,0:T(8,128)(2,1)S(1)} %finish.8), channel_id=1, source_target_pairs={{0,2},{1,3},{2,0},{3,1},{4,6},{5,7},{6,4},{7,5},{8,10},{9,11},{10,... | collective-permute-start | bytes 393224 | tf_op jit(solution)/shard_map/ppermute | solution.py:447
  109.0 4.2 %collective-permute-start.18 = (bf16[512,128]{1,0:T(8,128)(2,1)S(1)}, bf16[512,128]{1,0:T(8,128)(2,1)S(1)}, u32[]{:S(2)}, u32[]{:S(2)}) collective-permute-start(bf16[512,128]{1,0:T(8,128)(2,1)S(1)} %get-tuple-element.33), channel_id=1, source_target_pairs={{0,1},{1,0},{2,3},{3,2},{4,5},{5,4},{6,7},{7,6},{8,9},{9,8},{10,11... | collective-permute-start | bytes 393224 | tf_op jit(solution)/shard_map/ppermute | solution.py:447
  109.4 3.8 %collective-permute-start.19 = (bf16[512,128]{1,0:T(8,128)(2,1)S(1)}, bf16[512,128]{1,0:T(8,128)(2,1)S(1)}, u32[]{:S(2)}, u32[]{:S(2)}) collective-permute-start(bf16[512,128]{1,0:T(8,128)(2,1)S(1)} %get-tuple-element.34), channel_id=1, source_target_pairs={{0,1},{1,0},{2,3},{3,2},{4,5},{5,4},{6,7},{7,6},{8,9},{9,8},{10,11... | collective-permute-start | bytes 393224 | tf_op jit(solution)/shard_map/ppermute | solution.py:447
  110.3 5.4 %collective-permute-start.15 = (bf16[512,128]{1,0:T(8,128)(2,1)S(1)}, bf16[512,128]{1,0:T(8,128)(2,1)S(1)}, u32[]{:S(2)}, u32[]{:S(2)}) collective-permute-start(bf16[512,128]{1,0:T(8,128)(2,1)S(1)} %finish.6), channel_id=1, source_target_pairs={{0,3},{1,2},{2,1},{3,0},{4,7},{5,6},{6,5},{7,4},{8,11},{9,10},{10,... | collective-permute-start | bytes 393224 | tf_op jit(solution)/shard_map/ppermute | solution.py:447
  112.5 6.4 %collective-permute-start.14 = (bf16[512,128]{1,0:T(8,128)(2,1)S(1)}, bf16[512,128]{1,0:T(8,128)(2,1)S(1)}, u32[]{:S(2)}, u32[]{:S(2)}) collective-permute-start(bf16[512,128]{1,0:T(8,128)(2,1)S(1)} %finish.5), channel_id=1, source_target_pairs={{0,2},{1,3},{2,0},{3,1},{4,6},{5,7},{6,4},{7,5},{8,10},{9,11},{10,... | collective-permute-start | bytes 393224 | tf_op jit(solution)/shard_map/ppermute | solution.py:447
  (10 other events, 24.4 us)

commit v7 on v6

--- a/solution.py
+++ b/solution.py
@@ -16,6 +16,7 @@
 DEPTH = NEED * TILE
 MIB = 1024 * 1024
 RESIDENT_PANELS = 8
+ROW_BLOCK = 512
 RESIDENT_LIMIT = 9 * MIB
 STREAM_LIMIT = 14 * MIB
 DENSIFY_LIMIT = 38 * MIB
@@ -134,6 +135,22 @@
     if not first:
         start_totals, refs = refs[:n_totals], refs[n_totals:]
     totals, (streamed, feats, sem) = refs[:n_totals], refs[n_totals:]
+    if in_row_blocks(plan, n_totals, first):
+        for e, (operand, index, resident, offset, pieces) in enumerate(plan):
+            ((part, chunks, whole),) = pieces
+
+            def put_entry(k, value):
+                feats[e, pl.ds(k * TILE, TILE), :] = value
+
+            gather_feats(need, groups, 0, offset, [sources[i] for i in chunks], whole, put_entry)
+        for row in range(0, ROWS, ROW_BLOCK):
+            rows = pl.ds(row, ROW_BLOCK)
+            total = start_totals[0][rows, :]
+            for e, (operand, index, resident, offset, pieces) in enumerate(plan):
+                lhs = denses[operand][index, rows, :]
+                total = total + jnp.dot(lhs, feats[e], preferred_element_type=jnp.float32)
+            totals[0][rows, :] = total
+        return
     starts = [sum(widths[:t]) for t in range(n_totals)]
     fresh = [first] * n_totals
 
@@ -223,9 +240,14 @@
     return None
 
 
+def in_row_blocks(plan, n_totals, first):
+    return n_totals == 1 and not first and all(entry[2] for entry in plan)
+
+
 def aggregate(plan, groups, need, sources, denses, totals, widths):
     first = totals is None
     n_totals = len(widths)
+    by_entry = (len(plan),) if in_row_blocks(plan, n_totals, first) else ()
     smem = pl.BlockSpec(memory_space=pltpu.SMEM)
     vmem = pl.BlockSpec(memory_space=pltpu.VMEM)
     spaces = [None] * len(denses)
@@ -234,7 +256,7 @@
     streams = any(not entry[2] for entry in plan)
     scratch = [
         pltpu.VMEM((ROWS, DEPTH) if streams else (8, TILE), jnp.bfloat16),
-        pltpu.VMEM((DEPTH, sum(widths)), jnp.bfloat16),
+        pltpu.VMEM(by_entry + (DEPTH, sum(widths)), jnp.bfloat16),
     ]
     out_shape = [jax.ShapeDtypeStruct((ROWS, w), jnp.float32) for w in widths]
     flops = sum(2 * ROWS * DEPTH * sum(widths[p[0]] for p in entry[4]) for entry in plan)
@@ -449,7 +471,8 @@
     order = [(c, m) for c in range(cuts) for m in reversed(range(blocks))]
     arrived = {key: exchange(*key) for key in order}
     soon = [(c, m) for m in range(2) for c in range(cuts)] + [(c, m) for c in range(last) for m in range(2, blocks)]
-    late = [(last, m) for m in range(2, blocks)]
+    soon += [(last, m) for m in reversed(range(3, blocks))]
+    late = [(last, 2)]
 
     def multiply(keys, start_total, final):
         starts = tuple((m, c * part) for c, m in keys)

time: 121 us -> 120 us (level)
  transfers between devices with their start and end apart: 22 -> 22, of which waited for: 7 -> 7; matrix products, arithmetic and copies ran while one was open for 1% -> 1% of each run, Pallas kernels for 31% -> 32%
where the time goes in v7:
time: 120 us
  Pallas kernels  39.2 us (33%)
  waiting for transfers between devices  30.3 us (25%)
  starting transfers between devices  24.6 us (20%)
  local copies, waits for them, and re-layouts  24.2 us (20%)
    ppermute x16, waiting for transfers between devices, send(): return lax.ppermute(array, 'rows', ring_pairs(groups, way))  26.4 us
    unnamed x40, local copies, waits for them, and re-layouts  21.6 us
    ppermute x16, starting transfers between devices, send(): return lax.ppermute(array, 'rows', ring_pairs(groups, way))  20 us
    pallas_call x2, Pallas kernels, densify(): pl.pallas_call(functools.partial(densify_kernel, stages, resident, groups...  14.5 us
    pallas_call x4, Pallas kernels, aggregate(): pl.pallas_call(functools.partial(aggregate_kernel, plan, groups, len(sour...  14.4 us
    pallas_call x5, Pallas kernels, finish(): pl.pallas_call(functools.partial(finish_kernel, jobs, len(sources), len(d...  5.25 us
    ppermute x6, starting transfers between devices, exchange(): lax.ppermute(finished[c, m], 'feat', [(f, f ^ m) for f in range(blocks)])  4.57 us
    ppermute x6, waiting for transfers between devices, exchange(): lax.ppermute(finished[c, m], 'feat', [(f, f ^ m) for f in range(blocks)])  3.84 us
  transfers between devices with their start and end apart: 22, of which 7 were waited for; matrix products, arithmetic and copies ran while one was open for 1% of the time, Pallas kernels for 32%

profile of v7, /device:TPU:0, one launch (start us, length us, event | category | flops | bytes accessed | tf_op | source)
XLA Modules:
  0.0 119.9 jit_solution(3048195341142496703)
XLA Ops:
  0.0 1.3 %fusion = (bf16[2048,128]{1,0:T(8,128)(2,1)S(1)}, bf16[2048,128]{1,0:T(8,128)(2,1)S(1)}) fusion(bf16[2048,256]{1,0:T(8,128)(2,1)} %param.8), kind=kLoop, calls=%fused_computation.5 | loop fusion | bytes 2097152 | tf_op jit(solution)/shard_map/slice | solution.py:383
  1.3 3.1 %collective-permute-start.11 = (bf16[2048,128]{1,0:T(8,128)(2,1)S(1)}, bf16[2048,128]{1,0:T(8,128)(2,1)S(1)}, u32[]{:S(2)}, u32[]{:S(2)}) collective-permute-start(bf16[2048,128]{1,0:T(8,128)(2,1)S(1)} %get-tuple-element.35.refs_0_), channel_id=1, source_target_pairs={{0,8},{8,16},{16,24},{24,28},{28,20},{20,12},{12,4},{4,0},{1,9},{9... | collective-permute-start | bytes 1572872 | tf_op jit(solution)/shard_map/ppermute | solution.py:379
  4.4 2.0 %collective-permute-start.9 = (bf16[2048,128]{1,0:T(8,128)(2,1)S(1)}, bf16[2048,128]{1,0:T(8,128)(2,1)}, u32[]{:S(2)}, u32[]{:S(2)}) collective-permute-start(bf16[2048,128]{1,0:T(8,128)(2,1)S(1)} %get-tuple-element.35.refs_0_), channel_id=1, source_target_pairs={{0,4},{8,0},{16,8},{24,16},{28,24},{20,28},{12,20},{4,12},{1,5},{9... | collective-permute-start | bytes 1572872 | tf_op jit(solution)/shard_map/ppermute | solution.py:379
  6.4 9.9 %collective-permute-done.11.refs_0_ = bf16[2048,128]{1,0:T(8,128)(2,1)S(1)} collective-permute-done((bf16[2048,128]{1,0:T(8,128)(2,1)S(1)}, bf16[2048,128]{1,0:T(8,128)(2,1)S(1)}, u32[]{:S(2)}, u32[]{:S(2)}) %collective-permute-start.11) | collective-permute-done | bytes 524320 | tf_op jit(solution)/shard_map/ppermute | solution.py:379
  16.3 1.8 %collective-permute-start.12 = (bf16[2048,128]{1,0:T(8,128)(2,1)S(1)}, bf16[2048,128]{1,0:T(8,128)(2,1)}, u32[]{:S(2)}, u32[]{:S(2)}) collective-permute-start(bf16[2048,128]{1,0:T(8,128)(2,1)S(1)} %collective-permute-done.11.refs_0_), channel_id=1, source_target_pairs={{0,8},{8,16},{16,24},{24,28},{28,20},{20,12},{12,4},{4,0},{1,9},{9... | collective-permute-start | bytes 1572872 | tf_op jit(solution)/shard_map/ppermute | solution.py:379
  20.5 1.9 %collective-permute-start = (bf16[1024,128]{1,0:T(8,128)(2,1)S(1)}, bf16[1024,128]{1,0:T(8,128)(2,1)S(1)}, u32[]{:S(2)}, u32[]{:S(2)}) collective-permute-start(bf16[1024,128]{1,0:T(8,128)(2,1)S(1)} %get-tuple-element.38), channel_id=1, source_target_pairs={{0,8},{8,16},{16,24},{24,28},{28,20},{20,12},{12,4},{4,0},{1,9},{9... | collective-permute-start | bytes 786440 | tf_op jit(solution)/shard_map/ppermute | solution.py:379
  22.4 1.6 %collective-permute-start.2 = (bf16[1024,128]{1,0:T(8,128)(2,1)S(1)}, bf16[1024,128]{1,0:T(8,128)(2,1)}, u32[]{:S(2)}, u32[]{:S(2)}) collective-permute-start(bf16[1024,128]{1,0:T(8,128)(2,1)S(1)} %get-tuple-element.37), channel_id=1, source_target_pairs={{0,8},{8,16},{16,24},{24,28},{28,20},{20,12},{12,4},{4,0},{1,9},{9... | collective-permute-start | bytes 786440 | tf_op jit(solution)/shard_map/ppermute | solution.py:379
  24.6 6.0 %collective-permute-done.9.refs_3_ = bf16[2048,128]{1,0:T(8,128)(2,1)} collective-permute-done((bf16[2048,128]{1,0:T(8,128)(2,1)S(1)}, bf16[2048,128]{1,0:T(8,128)(2,1)}, u32[]{:S(2)}, u32[]{:S(2)}) %collective-permute-start.9) | collective-permute-done | bytes 524320 | tf_op jit(solution)/shard_map/ppermute | solution.py:379
  31.2 1.8 %collective-permute-start.13 = (bf16[2048,128]{1,0:T(8,128)(2,1)}, bf16[2048,128]{1,0:T(8,128)(2,1)S(1)}, u32[]{:S(2)}, u32[]{:S(2)}) collective-permute-start(bf16[2048,128]{1,0:T(8,128)(2,1)} %collective-permute-done.12.refs_2_), channel_id=1, source_target_pairs={{0,8},{8,16},{16,24},{24,28},{28,20},{20,12},{12,4},{4,0},{1,9},{9... | collective-permute-start | bytes 1572872 | tf_op jit(solution)/shard_map/ppermute | solution.py:379
  33.0 8.8 %collective-permute-done.6.refs_1_ = bf16[2048,128]{1,0:T(8,128)(2,1)} collective-permute-done((bf16[2048,128]{1,0:T(8,128)(2,1)S(1)}, bf16[2048,128]{1,0:T(8,128)(2,1)}, u32[]{:S(2)}, u32[]{:S(2)}) %collective-permute-start.6) | collective-permute-done | bytes 524320 | tf_op jit(solution)/shard_map/ppermute | solution.py:379
  41.8 2.1 %collective-permute-start.1 = (bf16[1024,128]{1,0:T(8,128)(2,1)S(1)}, bf16[1024,128]{1,0:T(8,128)(2,1)S(1)}, u32[]{:S(2)}, u32[]{:S(2)}) collective-permute-start(bf16[1024,128]{1,0:T(8,128)(2,1)S(1)} %collective-permute-done.refs_1_), channel_id=1, source_target_pairs={{0,8},{8,16},{16,24},{24,28},{28,20},{20,12},{12,4},{4,0},{1,9},{9... | collective-permute-start | bytes 786440 | tf_op jit(solution)/shard_map/ppermute | solution.py:379
  43.9 1.6 %collective-permute-start.3 = (bf16[1024,128]{1,0:T(8,128)(2,1)}, bf16[1024,128]{1,0:T(8,128)(2,1)S(1)}, u32[]{:S(2)}, u32[]{:S(2)}) collective-permute-start(bf16[1024,128]{1,0:T(8,128)(2,1)} %collective-permute-done.2.refs_2_), channel_id=1, source_target_pairs={{0,8},{8,16},{16,24},{24,28},{28,20},{20,12},{12,4},{4,0},{1,9},{9... | collective-permute-start | bytes 786440 | tf_op jit(solution)/shard_map/ppermute | solution.py:379
  45.9 5.7 %densify.3 = (bf16[1,2048,1024]{2,1,0:T(8,128)(2,1)S(1)}, bf16[2,2048,1024]{2,1,0:T(8,128)(2,1)S(1)}) custom-call(s32[1024]{0:T(1024)S(1)} %select_reduce_fusion.table, bf16[640,128,128]{2,1,0:T(8,128)(2,1)} %tiles.3), custom_call_target="tpu_custom_call" | custom-call | bytes 12582912 | tf_op jit(solution)/shard_map/densify/pallas_call | solution.py:87
  51.6 3.3 %copy-done.5 = bf16[2,2048,1024]{2,1,0:T(8,128)(2,1)} copy-done((bf16[2,2048,1024]{2,1,0:T(8,128)(2,1)}, bf16[2,2048,1024]{2,1,0:T(8,128)(2,1)S(1)}, u32[]{:S(2)}) %copy-start.5) | copy-done | bytes 8388632
  54.9 2.0 %copy-done.8 = bf16[1,2048,1024]{2,1,0:T(8,128)(2,1)} copy-done((bf16[1,2048,1024]{2,1,0:T(8,128)(2,1)}, bf16[1,2048,1024]{2,1,0:T(8,128)(2,1)S(1)}, u32[]{:S(2)}) %copy-start.8) | copy-done | bytes 4194328
  56.9 8.8 %densify.2 = (bf16[2,2048,1024]{2,1,0:T(8,128)(2,1)S(1)}, bf16[2,2048,1024]{2,1,0:T(8,128)(2,1)S(1)}, bf16[1,2048,1024]{2,1,0:T(8,128)(2,1)S(1)}) custom-call(s32[1024]{0:T(1024)S(1)} %select_reduce_fusion.table, bf16[640,128,128]{2,1,0:T(8,128)(2,1)} %tiles.3), custom_call_target="tpu_custom_call" | custom-call | bytes 20971520 | tf_op jit(solution)/shard_map/densify/pallas_call | solution.py:87
  65.7 3.3 %copy-done = bf16[2,2048,1024]{2,1,0:T(8,128)(2,1)} copy-done((bf16[2,2048,1024]{2,1,0:T(8,128)(2,1)}, bf16[2,2048,1024]{2,1,0:T(8,128)(2,1)S(1)}, u32[]{:S(2)}) %copy-start) | copy-done | bytes 8388632
  69.0 2.1 %copy-done.1 = bf16[1,2048,1024]{2,1,0:T(8,128)(2,1)} copy-done((bf16[1,2048,1024]{2,1,0:T(8,128)(2,1)}, bf16[1,2048,1024]{2,1,0:T(8,128)(2,1)S(1)}, u32[]{:S(2)}) %copy-start.1) | copy-done | bytes 4194328
  71.0 3.2 %copy-done.3 = bf16[2,2048,1024]{2,1,0:T(8,128)(2,1)} copy-done((bf16[2,2048,1024]{2,1,0:T(8,128)(2,1)}, bf16[2,2048,1024]{2,1,0:T(8,128)(2,1)S(1)}, u32[]{:S(2)}) %copy-start.3) | copy-done | bytes 8388632
  74.4 2.2 %copy-done.9 = bf16[1,2048,1024]{2,1,0:T(8,128)(2,1)S(1)} copy-done((bf16[1,2048,1024]{2,1,0:T(8,128)(2,1)S(1)}, bf16[1,2048,1024]{2,1,0:T(8,128)(2,1)}, u32[]{:S(2)}) %copy-start.9) | copy-done | bytes 4194328
  76.6 2.0 %aggregate.4 = (f32[2048,128]{1,0:T(8,128)S(1)}, f32[2048,128]{1,0:T(8,128)S(1)}) custom-call(s32[512]{0:T(512)S(1)} %reshape.9.need, bf16[2048,128]{1,0:T(8,128)(2,1)S(1)} %get-tuple-element.35.refs_0_, bf16[2048,128]{1,0:T(8,128)(2,1)S(1)} %get-tuple-element.36.refs_1_, bf16[1,2048,1024]{2,1,0:T(8,128)(2,1)S(1)} %copy-done.9), custom_call_target="tpu_custom_call" | custom-call | flops 1073741824 | bytes 4194304 | tf_op jit(solution)/shard_map/aggregate/pallas_call | solution.py:263
  79.3 1.5 %collective-permute-start.4 = (bf16[1024,128]{1,0:T(8,128)(2,1)S(1)}, bf16[1024,128]{1,0:T(8,128)(2,1)S(1)}, u32[]{:S(2)}, u32[]{:S(2)}) collective-permute-start(bf16[1024,128]{1,0:T(8,128)(2,1)S(1)} %pick.4), channel_id=1, source_target_pairs={{0,8},{8,16},{16,24},{24,28},{28,20},{20,12},{12,4},{4,0},{1,9},{9... | collective-permute-start | bytes 786440 | tf_op jit(solution)/shard_map/ppermute | solution.py:379
  80.8 3.4 %copy-done.6 = bf16[2,2048,1024]{2,1,0:T(8,128)(2,1)S(1)} copy-done((bf16[2,2048,1024]{2,1,0:T(8,128)(2,1)S(1)}, bf16[2,2048,1024]{2,1,0:T(8,128)(2,1)}, u32[]{:S(2)}) %copy-start.6) | copy-done | bytes 8388632
  86.3 4.1 %aggregate.5 = (f32[2048,128]{1,0:T(8,128)S(1)}, f32[2048,128]{1,0:T(8,128)S(1)}) custom-call(s32[512]{0:T(512)S(1)} %reshape.9.need, bf16[2048,128]{1,0:T(8,128)(2,1)S(1)} %copy-done.11, bf16[1024,128]{1,0:T(8,128)(2,1)S(1)} %collective-permute-done.refs_1_, bf16[1024,128]{1,0:T(8,128)(2,1)} %collective-permute-done.2.refs_2_, ...), custom_call_target="tpu_custom_call" | custom-call | flops 2147483648 | bytes 8388608 | tf_op jit(solution)/shard_map/aggregate/pallas_call | solution.py:263
  93.3 1.8 %collective-permute-start.16 = (bf16[1024,128]{1,0:T(8,128)(2,1)S(1)}, bf16[1024,128]{1,0:T(8,128)(2,1)S(1)}, u32[]{:S(2)}, u32[]{:S(2)}) collective-permute-start(bf16[1024,128]{1,0:T(8,128)(2,1)S(1)} %pick.7), channel_id=1, source_target_pairs={{0,8},{8,16},{16,24},{24,28},{28,20},{20,12},{12,4},{4,0},{1,9},{9... | collective-permute-start | bytes 786440 | tf_op jit(solution)/shard_map/ppermute | solution.py:379
  95.1 5.0 %aggregate.6 = (f32[2048,128]{1,0:T(8,128)S(1)}, f32[2048,128]{1,0:T(8,128)S(1)}) custom-call(s32[512]{0:T(512)S(1)} %reshape.9.need, bf16[2048,128]{1,0:T(8,128)(2,1)S(1)} %collective-permute-done.10.refs_0_, bf16[2048,128]{1,0:T(8,128)(2,1)} %collective-permute-done.6.refs_1_, bf16[2048,128]{1,0:T(8,128)(2,1)} %collective-permute-done.12.refs_2_, ...), custom_call_target="tpu_custom_call" | custom-call | flops 2147483648 | bytes 12582912 | tf_op jit(solution)/shard_map/aggregate/pallas_call | solution.py:263
  100.1 3.3 %aggregate.7.refs_4_.refs_7_ = f32[2048,128]{1,0:T(8,128)S(1)} custom-call(s32[512]{0:T(512)S(1)} %reshape.9.need, bf16[1024,128]{1,0:T(8,128)(2,1)S(1)} %collective-permute-done.1.refs_0_, bf16[1024,128]{1,0:T(8,128)(2,1)S(1)} %collective-permute-done.3.refs_1_, bf16[2048,128]{1,0:T(8,128)(2,1)S(1)} %collective-permute-done.7.refs_0_.refs_2_, ...), custom_call_target="tpu_custom_call" | custom-call | flops 1073741824 | bytes 8388608 | tf_op jit(solution)/shard_map/aggregate/pallas_call | solution.py:263
  105.0 1.8 %collective-permute-start.20 = (bf16[512,128]{1,0:T(8,128)(2,1)S(1)}, bf16[512,128]{1,0:T(8,128)(2,1)S(1)}, u32[]{:S(2)}, u32[]{:S(2)}) collective-permute-start(bf16[512,128]{1,0:T(8,128)(2,1)S(1)} %finish.8), channel_id=1, source_target_pairs={{0,3},{1,2},{2,1},{3,0},{4,7},{5,6},{6,5},{7,4},{8,11},{9,10},{10,... | collective-permute-start | bytes 393224 | tf_op jit(solution)/shard_map/ppermute | solution.py:469
  107.5 1.6 %collective-permute-start.19 = (bf16[512,128]{1,0:T(8,128)(2,1)S(1)}, bf16[512,128]{1,0:T(8,128)(2,1)S(1)}, u32[]{:S(2)}, u32[]{:S(2)}) collective-permute-start(bf16[512,128]{1,0:T(8,128)(2,1)S(1)} %finish.7), channel_id=1, source_target_pairs={{0,2},{1,3},{2,0},{3,1},{4,6},{5,7},{6,4},{7,5},{8,10},{9,11},{10,... | collective-permute-start | bytes 393224 | tf_op jit(solution)/shard_map/ppermute | solution.py:469
  109.0 2.3 %finish.6 = (bf16[512,128]{1,0:T(8,128)(2,1)S(1)}, bf16[512,128]{1,0:T(8,128)(2,1)S(1)}, bf16[512,128]{1,0:T(8,128)(2,1)S(1)}, bf16[512,128]{1,0:T(8,128)(2,1)S(1)}) custom-call(bf16[1024,128]{1,0:T(8,128)(2,1)S(1)} %collective-permute-done.15.refs_0_, bf16[1024,128]{1,0:T(8,128)(2,1)S(1)} %collective-permute-done.16.refs_1_, ...), custom_call_target="tpu_custom_call" | custom-call | flops 1073741824 | bytes 8388608 | tf_op jit(solution)/shard_map/finish/pallas_call | solution.py:221
  113.3 2.3 %collective-permute-done.19.refs_4_ = bf16[512,128]{1,0:T(8,128)(2,1)S(1)} collective-permute-done((bf16[512,128]{1,0:T(8,128)(2,1)S(1)}, bf16[512,128]{1,0:T(8,128)(2,1)S(1)}, u32[]{:S(2)}, u32[]{:S(2)}) %collective-permute-start.19) | collective-permute-done | bytes 131104 | tf_op jit(solution)/shard_map/ppermute | solution.py:469
  116.9 1.5 %collective-permute-done.14.refs_0_ = bf16[512,128]{1,0:T(8,128)(2,1)S(1)} collective-permute-done((bf16[512,128]{1,0:T(8,128)(2,1)S(1)}, bf16[512,128]{1,0:T(8,128)(2,1)S(1)}, u32[]{:S(2)}, u32[]{:S(2)}) %collective-permute-start.14) | collective-permute-done | bytes 131104 | tf_op jit(solution)/shard_map/ppermute | solution.py:469
  (75 shorter events, 16.0 us)
Async XLA Ops:
  0.0 41.8 %copy-start.16 = (s32[640]{0:T(1024)S(1)}, s32[640]{0:T(1024)}, u32[]{:S(2)}) copy-start(s32[640]{0:T(1024)} %param.10) | copy-start | bytes 7684
  0.0 41.8 %copy-start.17 = (s32[640]{0:T(1024)S(1)}, s32[640]{0:T(1024)}, u32[]{:S(2)}) copy-start(s32[640]{0:T(1024)} %param.11) | copy-start | bytes 7684
  0.0 41.8 %copy-start.15 = (s32[640]{0:T(1024)S(1)}, s32[640]{0:T(1024)}, u32[]{:S(2)}) copy-start(s32[640]{0:T(1024)} %param.12) | copy-start | bytes 7684
  1.3 15.0 %collective-permute-start.11 = (bf16[2048,128]{1,0:T(8,128)(2,1)S(1)}, bf16[2048,128]{1,0:T(8,128)(2,1)S(1)}, u32[]{:S(2)}, u32[]{:S(2)}) collective-permute-start(bf16[2048,128]{1,0:T(8,128)(2,1)S(1)} %get-tuple-element.35.refs_0_), channel_id=1, source_target_pairs={{0,8},{8,16},{16,24},{24,28},{28,20},{20,12},{12,4},{4,0},{1,9},{9... | collective-permute-start | bytes 1572872 | tf_op jit(solution)/shard_map/ppermute | solution.py:379
  4.4 14.8 %collective-permute-start.5 = (bf16[2048,128]{1,0:T(8,128)(2,1)S(1)}, bf16[2048,128]{1,0:T(8,128)(2,1)S(1)}, u32[]{:S(2)}, u32[]{:S(2)}) collective-permute-start(bf16[2048,128]{1,0:T(8,128)(2,1)S(1)} %get-tuple-element.36.refs_1_), channel_id=1, source_target_pairs={{0,4},{8,0},{16,8},{24,16},{28,24},{20,28},{12,20},{4,12},{1,5},{9... | collective-permute-start | bytes 1572872 | tf_op jit(solution)/shard_map/ppermute | solution.py:379
  4.4 26.1 %collective-permute-start.9 = (bf16[2048,128]{1,0:T(8,128)(2,1)S(1)}, bf16[2048,128]{1,0:T(8,128)(2,1)}, u32[]{:S(2)}, u32[]{:S(2)}) collective-permute-start(bf16[2048,128]{1,0:T(8,128)(2,1)S(1)} %get-tuple-element.35.refs_0_), channel_id=1, source_target_pairs={{0,4},{8,0},{16,8},{24,16},{28,24},{20,28},{12,20},{4,12},{1,5},{9... | collective-permute-start | bytes 1572872 | tf_op jit(solution)/shard_map/ppermute | solution.py:379
  16.3 14.3 %copy-start.10 = (bf16[2048,128]{1,0:T(8,128)(2,1)}, bf16[2048,128]{1,0:T(8,128)(2,1)S(1)}, u32[]{:S(2)}) copy-start(bf16[2048,128]{1,0:T(8,128)(2,1)S(1)} %collective-permute-done.11.refs_0_) | copy-start | bytes 1572868
  16.3 14.9 %collective-permute-start.12 = (bf16[2048,128]{1,0:T(8,128)(2,1)S(1)}, bf16[2048,128]{1,0:T(8,128)(2,1)}, u32[]{:S(2)}, u32[]{:S(2)}) collective-permute-start(bf16[2048,128]{1,0:T(8,128)(2,1)S(1)} %collective-permute-done.11.refs_0_), channel_id=1, source_target_pairs={{0,8},{8,16},{16,24},{24,28},{28,20},{20,12},{12,4},{4,0},{1,9},{9... | collective-permute-start | bytes 1572872 | tf_op jit(solution)/shard_map/ppermute | solution.py:379
  19.2 13.8 %copy-start.12 = (bf16[2048,128]{1,0:T(8,128)(2,1)}, bf16[2048,128]{1,0:T(8,128)(2,1)S(1)}, u32[]{:S(2)}) copy-start(bf16[2048,128]{1,0:T(8,128)(2,1)S(1)} %collective-permute-done.5.refs_4_) | copy-start | bytes 1572868
  19.2 22.6 %collective-permute-start.6 = (bf16[2048,128]{1,0:T(8,128)(2,1)S(1)}, bf16[2048,128]{1,0:T(8,128)(2,1)}, u32[]{:S(2)}, u32[]{:S(2)}) collective-permute-start(bf16[2048,128]{1,0:T(8,128)(2,1)S(1)} %collective-permute-done.5.refs_4_), channel_id=1, source_target_pairs={{0,4},{8,0},{16,8},{24,16},{28,24},{20,28},{12,20},{4,12},{1,5},{9... | collective-permute-start | bytes 1572872 | tf_op jit(solution)/shard_map/ppermute | solution.py:379
  20.5 21.3 %collective-permute-start = (bf16[1024,128]{1,0:T(8,128)(2,1)S(1)}, bf16[1024,128]{1,0:T(8,128)(2,1)S(1)}, u32[]{:S(2)}, u32[]{:S(2)}) collective-permute-start(bf16[1024,128]{1,0:T(8,128)(2,1)S(1)} %get-tuple-element.38), channel_id=1, source_target_pairs={{0,8},{8,16},{16,24},{24,28},{28,20},{20,12},{12,4},{4,0},{1,9},{9... | collective-permute-start | bytes 786440 | tf_op jit(solution)/shard_map/ppermute | solution.py:379
  22.4 21.5 %collective-permute-start.2 = (bf16[1024,128]{1,0:T(8,128)(2,1)S(1)}, bf16[1024,128]{1,0:T(8,128)(2,1)}, u32[]{:S(2)}, u32[]{:S(2)}) collective-permute-start(bf16[1024,128]{1,0:T(8,128)(2,1)S(1)} %get-tuple-element.37), channel_id=1, source_target_pairs={{0,8},{8,16},{16,24},{24,28},{28,20},{20,12},{12,4},{4,0},{1,9},{9... | collective-permute-start | bytes 786440 | tf_op jit(solution)/shard_map/ppermute | solution.py:379
  30.6 59.8 %collective-permute-start.10 = (bf16[2048,128]{1,0:T(8,128)(2,1)}, bf16[2048,128]{1,0:T(8,128)(2,1)S(1)}, u32[]{:S(2)}, u32[]{:S(2)}) collective-permute-start(bf16[2048,128]{1,0:T(8,128)(2,1)} %collective-permute-done.9.refs_3_), channel_id=1, source_target_pairs={{0,4},{8,0},{16,8},{24,16},{28,24},{20,28},{12,20},{4,12},{1,5},{9... | collective-permute-start | bytes 1572872 | tf_op jit(solution)/shard_map/ppermute | solution.py:379
  31.2 61.5 %collective-permute-start.13 = (bf16[2048,128]{1,0:T(8,128)(2,1)}, bf16[2048,128]{1,0:T(8,128)(2,1)S(1)}, u32[]{:S(2)}, u32[]{:S(2)}) collective-permute-start(bf16[2048,128]{1,0:T(8,128)(2,1)} %collective-permute-done.12.refs_2_), channel_id=1, source_target_pairs={{0,8},{8,16},{16,24},{24,28},{28,20},{20,12},{12,4},{4,0},{1,9},{9... | collective-permute-start | bytes 1572872 | tf_op jit(solution)/shard_map/ppermute | solution.py:379
  41.8 49.9 %collective-permute-start.7 = (bf16[2048,128]{1,0:T(8,128)(2,1)}, bf16[2048,128]{1,0:T(8,128)(2,1)S(1)}, u32[]{:S(2)}, u32[]{:S(2)}) collective-permute-start(bf16[2048,128]{1,0:T(8,128)(2,1)} %collective-permute-done.6.refs_1_), channel_id=1, source_target_pairs={{0,4},{8,0},{16,8},{24,16},{28,24},{20,28},{12,20},{4,12},{1,5},{9... | collective-permute-start | bytes 1572872 | tf_op jit(solution)/shard_map/ppermute | solution.py:379
  41.8 36.7 %collective-permute-start.1 = (bf16[1024,128]{1,0:T(8,128)(2,1)S(1)}, bf16[1024,128]{1,0:T(8,128)(2,1)S(1)}, u32[]{:S(2)}, u32[]{:S(2)}) collective-permute-start(bf16[1024,128]{1,0:T(8,128)(2,1)S(1)} %collective-permute-done.refs_1_), channel_id=1, source_target_pairs={{0,8},{8,16},{16,24},{24,28},{28,20},{20,12},{12,4},{4,0},{1,9},{9... | collective-permute-start | bytes 786440 | tf_op jit(solution)/shard_map/ppermute | solution.py:379
  43.9 34.7 %collective-permute-start.3 = (bf16[1024,128]{1,0:T(8,128)(2,1)}, bf16[1024,128]{1,0:T(8,128)(2,1)S(1)}, u32[]{:S(2)}, u32[]{:S(2)}) collective-permute-start(bf16[1024,128]{1,0:T(8,128)(2,1)} %collective-permute-done.2.refs_2_), channel_id=1, source_target_pairs={{0,8},{8,16},{16,24},{24,28},{28,20},{20,12},{12,4},{4,0},{1,9},{9... | collective-permute-start | bytes 786440 | tf_op jit(solution)/shard_map/ppermute | solution.py:379
  56.9 17.4 %copy-start.14 = (s32[8,8,8]{2,1,0:T(8,128)S(1)}, s32[8,8,8]{2,1,0:T(8,128)}, u32[]{:S(2)}) copy-start(s32[8,8,8]{2,1,0:T(8,128)} %param.14) | copy-start | bytes 6148
  76.6 18.5 %copy-start.4 = (bf16[2,2048,1024]{2,1,0:T(8,128)(2,1)S(1)}, bf16[2,2048,1024]{2,1,0:T(8,128)(2,1)}, u32[]{:S(2)}) copy-start(bf16[2,2048,1024]{2,1,0:T(8,128)(2,1)} %copy-done.3) | copy-start | bytes 25165828
  78.6 16.5 %slice-start = ((s8[8388608]{0:T(1024)(128)(4,1)}), s8[4194304]{0:T(1024)(128)(4,1)S(1)}, s32[]{:S(2)}) async-start(s8[8388608]{0:T(1024)(128)(4,1)} %bitcast.2), calls=%async_computation | async-start | bytes 8388608
  79.3 24.0 %collective-permute-start.4 = (bf16[1024,128]{1,0:T(8,128)(2,1)S(1)}, bf16[1024,128]{1,0:T(8,128)(2,1)S(1)}, u32[]{:S(2)}, u32[]{:S(2)}) collective-permute-start(bf16[1024,128]{1,0:T(8,128)(2,1)S(1)} %pick.4), channel_id=1, source_target_pairs={{0,8},{8,16},{16,24},{24,28},{28,20},{20,12},{12,4},{4,0},{1,9},{9... | collective-permute-start | bytes 786440 | tf_op jit(solution)/shard_map/ppermute | solution.py:379
  86.3 8.8 %slice-start.1 = ((s8[8388608]{0:T(1024)(128)(4,1)}), s8[4194304]{0:T(1024)(128)(4,1)S(1)}, s32[]{:S(2)}) async-start(s8[8388608]{0:T(1024)(128)(4,1)} %bitcast.2), calls=%async_computation.1 | async-start | bytes 8388608
  91.0 13.2 %collective-permute-start.15 = (bf16[1024,128]{1,0:T(8,128)(2,1)S(1)}, bf16[1024,128]{1,0:T(8,128)(2,1)S(1)}, u32[]{:S(2)}, u32[]{:S(2)}) collective-permute-start(bf16[1024,128]{1,0:T(8,128)(2,1)S(1)} %pick.6), channel_id=1, source_target_pairs={{0,4},{8,0},{16,8},{24,16},{28,24},{20,28},{12,20},{4,12},{1,5},{9... | collective-permute-start | bytes 786440 | tf_op jit(solution)/shard_map/ppermute | solution.py:379
  92.3 11.1 %collective-permute-start.8 = (bf16[1024,128]{1,0:T(8,128)(2,1)S(1)}, bf16[1024,128]{1,0:T(8,128)(2,1)S(1)}, u32[]{:S(2)}, u32[]{:S(2)}) collective-permute-start(bf16[1024,128]{1,0:T(8,128)(2,1)S(1)} %pick.5), channel_id=1, source_target_pairs={{0,4},{8,0},{16,8},{24,16},{28,24},{20,28},{12,20},{4,12},{1,5},{9... | collective-permute-start | bytes 786440 | tf_op jit(solution)/shard_map/ppermute | solution.py:379
  93.3 10.9 %collective-permute-start.16 = (bf16[1024,128]{1,0:T(8,128)(2,1)S(1)}, bf16[1024,128]{1,0:T(8,128)(2,1)S(1)}, u32[]{:S(2)}, u32[]{:S(2)}) collective-permute-start(bf16[1024,128]{1,0:T(8,128)(2,1)S(1)} %pick.7), channel_id=1, source_target_pairs={{0,8},{8,16},{16,24},{24,28},{28,20},{20,12},{12,4},{4,0},{1,9},{9... | collective-permute-start | bytes 786440 | tf_op jit(solution)/shard_map/ppermute | solution.py:379
  104.1 8.6 %collective-permute-start.21 = (bf16[512,128]{1,0:T(8,128)(2,1)S(1)}, bf16[512,128]{1,0:T(8,128)(2,1)S(1)}, u32[]{:S(2)}, u32[]{:S(2)}) collective-permute-start(bf16[512,128]{1,0:T(8,128)(2,1)S(1)} %finish.9), channel_id=1, source_target_pairs={{0,3},{1,2},{2,1},{3,0},{4,7},{5,6},{6,5},{7,4},{8,11},{9,10},{10,... | collective-permute-start | bytes 393224 | tf_op jit(solution)/shard_map/ppermute | solution.py:469
  105.0 8.4 %collective-permute-start.20 = (bf16[512,128]{1,0:T(8,128)(2,1)S(1)}, bf16[512,128]{1,0:T(8,128)(2,1)S(1)}, u32[]{:S(2)}, u32[]{:S(2)}) collective-permute-start(bf16[512,128]{1,0:T(8,128)(2,1)S(1)} %finish.8), channel_id=1, source_target_pairs={{0,3},{1,2},{2,1},{3,0},{4,7},{5,6},{6,5},{7,4},{8,11},{9,10},{10,... | collective-permute-start | bytes 393224 | tf_op jit(solution)/shard_map/ppermute | solution.py:469
  107.5 8.2 %collective-permute-start.19 = (bf16[512,128]{1,0:T(8,128)(2,1)S(1)}, bf16[512,128]{1,0:T(8,128)(2,1)S(1)}, u32[]{:S(2)}, u32[]{:S(2)}) collective-permute-start(bf16[512,128]{1,0:T(8,128)(2,1)S(1)} %finish.7), channel_id=1, source_target_pairs={{0,2},{1,3},{2,0},{3,1},{4,6},{5,7},{6,4},{7,5},{8,10},{9,11},{10,... | collective-permute-start | bytes 393224 | tf_op jit(solution)/shard_map/ppermute | solution.py:469
  111.4 4.3 %collective-permute-start.17 = (bf16[512,128]{1,0:T(8,128)(2,1)S(1)}, bf16[512,128]{1,0:T(8,128)(2,1)S(1)}, u32[]{:S(2)}, u32[]{:S(2)}) collective-permute-start(bf16[512,128]{1,0:T(8,128)(2,1)S(1)} %get-tuple-element.33), channel_id=1, source_target_pairs={{0,1},{1,0},{2,3},{3,2},{4,5},{5,4},{6,7},{7,6},{8,9},{9,8},{10,11... | collective-permute-start | bytes 393224 | tf_op jit(solution)/shard_map/ppermute | solution.py:469
  111.5 4.2 %copy-start.7 = (bf16[1024,1024]{1,0:T(8,128)(2,1)S(1)}, bf16[1024,1024]{1,0:T(8,128)(2,1)}, u32[]{:S(2)}) copy-start(bf16[1024,1024]{1,0:T(8,128)(2,1)} %w.3) | copy-start | bytes 6291460
  111.5 4.2 %collective-permute-start.18 = (bf16[512,128]{1,0:T(8,128)(2,1)S(1)}, bf16[512,128]{1,0:T(8,128)(2,1)S(1)}, u32[]{:S(2)}, u32[]{:S(2)}) collective-permute-start(bf16[512,128]{1,0:T(8,128)(2,1)S(1)} %get-tuple-element.34), channel_id=1, source_target_pairs={{0,1},{1,0},{2,3},{3,2},{4,5},{5,4},{6,7},{7,6},{8,9},{9,8},{10,11... | collective-permute-start | bytes 393224 | tf_op jit(solution)/shard_map/ppermute | solution.py:469
  112.7 5.7 %collective-permute-start.14 = (bf16[512,128]{1,0:T(8,128)(2,1)S(1)}, bf16[512,128]{1,0:T(8,128)(2,1)S(1)}, u32[]{:S(2)}, u32[]{:S(2)}) collective-permute-start(bf16[512,128]{1,0:T(8,128)(2,1)S(1)} %finish.5), channel_id=1, source_target_pairs={{0,2},{1,3},{2,0},{3,1},{4,6},{5,7},{6,4},{7,5},{8,10},{9,11},{10,... | collective-permute-start | bytes 393224 | tf_op jit(solution)/shard_map/ppermute | solution.py:469
  (10 other events, 24.9 us)
